TPU v7x, 32 devices: a whole 2x2x4 slice. The times are simulated.
32 devices in a mesh: dp: 1, fsdp: 32 (over z, y, x, core).
Axes of the slice: x: 2, y: 2, z: 4, core: 2. Of those that a mesh axis runs over, the one named last changes fastest.
Arguments:
- hidden_states: bfloat16 [128, 4096], P(('dp', 'fsdp')), may hold values from -400 to 400
- token_ids: int32 [128], P(('dp', 'fsdp')), may hold values from 0 to 4095
- norm_gain: float32 [4096], replicated, may hold values from 0.5 to 1.5
- ref_gate_w: bfloat16 [4096, 14784], P('dp', 'fsdp'), may hold values from -0.1875 to 0.1875
- ref_up_w: bfloat16 [4096, 14784], P('dp', 'fsdp'), may hold values from -0.1875 to 0.1875
- ref_down_w: bfloat16 [14784, 4096], P('fsdp', 'dp'), may hold values from -0.09375 to 0.09375
- pol_gate_w: bfloat16 [4096, 14784], P('dp', 'fsdp'), may hold values from -0.1875 to 0.1875
- pol_up_w: bfloat16 [4096, 14784], P('dp', 'fsdp'), may hold values from -0.1875 to 0.1875
- pol_down_w: bfloat16 [14784, 4096], P('fsdp', 'dp'), may hold values from -0.09375 to 0.09375
- sample_lengths: int32 [1, 32], P('dp'), may hold values from 1 to 24, 128 in all within a row
- prompt_index: int32 [1, 32], P('dp'), may hold values from 0 to 3, as said below
- rewards: float32 [1, 32], P('dp'), may hold values from -6 to 6
Outputs:
- grad_gate: float32 [4096, 14784], P('dp', 'fsdp')
- grad_up: float32 [4096, 14784], P('dp', 'fsdp')
- grad_down: float32 [14784, 4096], P('fsdp', 'dp')
- advantage: float32 [1, 32], P('dp')
Inputs may be any that keep to these rules, and one draw needn't show every extreme that they name: `prompt_index`: in each row, every prompt from 0 to 3 is answered by exactly 8 samples. `sample_lengths`: each row sums to 128.
All inputs are finite; a program needn't handle non-finite values.
Results may differ from a plain program's by a relative error of at most 0.013.
Values may be sent and summed in bfloat16 or wider, within the bound.
No kernel may reach another device: no remote copies, remote signals or barrier semaphores. Data moves between devices by JAX's collectives and lax.ppermute only.
A program may use at most 128 MiB of HBM per device.

v0:
```python
import jax
import jax.numpy as jnp
from jax import lax
from jax.sharding import PartitionSpec as P

K = 8


EPSILON = 1e-06
KL_WEIGHT = 0.05


def combined_all(part, axis, combine):
    gathered = jax.tree.map(lambda a: lax.all_gather(a, axis), part)

    def take(source):
        return jax.tree.map(lambda a: lax.dynamic_index_in_dim(a, source, 0, False), gathered)

    return lax.fori_loop(
        1, lax.axis_size(axis), lambda source, state: combine(state, take(source)), take(0)
    )


def normalize(states, norm_gain):
    values = states.astype(jnp.float32)
    factor = lax.rsqrt(jnp.mean(values * values, axis=-1, keepdims=True) + EPSILON)
    return (values * factor * norm_gain).astype(jnp.bfloat16)


def combine_totals(first, second):
    row_peak = jnp.maximum(first[0], second[0])
    summed = first[1] * jnp.exp(first[0] - row_peak) + second[1] * jnp.exp(second[0] - row_peak)
    return (row_peak, summed, first[2] + second[2])


def column_section(normed_cols, state_cols, ids_all, weight_sets, group_index):
    col_width = state_cols.shape[1]
    unit_count = weight_sets[0][0].shape[1]
    in_weights = jnp.concatenate(
        [matrix for triple in weight_sets for matrix in triple[:2]], axis=1
    )
    row_block = normed_cols
    pre_sums = lax.psum_scatter(
        jnp.dot(row_block, in_weights, preferred_element_type=jnp.float32),
        "dp",
        scatter_dimension=0,
        tiled=True,
    )
    gate_pre = pre_sums[:, 0:unit_count]
    up_pre = pre_sums[:, unit_count : 2 * unit_count]
    activations = jax.nn.silu(gate_pre) * up_pre
    hidden_local = activations.astype(jnp.bfloat16)
    hidden_all = lax.all_gather(hidden_local, "dp", axis=0, tiled=True)
    row_block = hidden_all
    pieces = jnp.dot(row_block, weight_sets[0][2], preferred_element_type=jnp.float32)
    out_cols = lax.psum_scatter(pieces, "fsdp", scatter_dimension=0, tiled=True)
    states = state_cols.astype(jnp.float32)
    col_ids = jnp.arange(col_width, dtype=jnp.int32) + group_index * col_width
    logits = states + out_cols
    row_peak = jnp.max(logits, axis=1)
    logits_list = [logits]
    peaks = [row_peak]
    sums = [jnp.sum(jnp.exp(logits - row_peak[:, None]), axis=1)]
    picks = [jnp.sum(jnp.where(col_ids[None, :] == ids_all[:, None], logits, 0.0), axis=1)]
    row_peak, summed, picked = combined_all(
        (jnp.stack(peaks, axis=1), jnp.stack(sums, axis=1), jnp.stack(picks, axis=1)),
        "dp",
        combine_totals,
    )
    log_total = row_peak + jnp.log(summed)
    return (pre_sums, hidden_all, logits_list, log_total, picked - log_total)


def leave_one_out(log_gap, inside, prompt_index, rewards):
    divergence = lax.psum(jnp.sum(log_gap[:, None] * inside, axis=0), "fsdp")
    scores = rewards[0] - KL_WEIGHT * divergence
    same_prompt = (prompt_index[0][:, None] == prompt_index[0][None, :]).astype(jnp.float32)
    others = jnp.sum(same_prompt * scores[None, :], axis=1) - scores
    advantage = scores - others / (K - 1)
    weight = jnp.sum(inside * advantage[None, :], axis=1)
    return (advantage, weight)


def local(
    hidden_states,
    token_ids,
    norm_gain,
    ref_gate_w,
    ref_up_w,
    ref_down_w,
    pol_gate_w,
    pol_up_w,
    pol_down_w,
    sample_lengths,
    prompt_index,
    rewards,
):
    token_count = hidden_states.shape[0]
    model_width = hidden_states.shape[1]
    group_index = lax.axis_index("dp")
    member_index = lax.axis_index("fsdp")
    unit_count = pol_gate_w.shape[1]
    normed = normalize(hidden_states, norm_gain)
    normed_mixed, state_cols = (
        lax.all_to_all(normed, "dp", split_axis=1, concat_axis=0, tiled=True),
        lax.all_to_all(hidden_states, "dp", split_axis=1, concat_axis=0, tiled=True),
    )
    normed_cols = lax.all_gather(normed_mixed, "fsdp", axis=0, tiled=True)
    ids_all = lax.all_gather(token_ids, "dp", axis=0, tiled=True)
    own_start = group_index * token_count
    position = member_index * token_count + jnp.arange(token_count, dtype=jnp.int32)
    sample_ends = jnp.cumsum(sample_lengths[0])
    sample_starts = sample_ends - sample_lengths[0]
    inside = (
        (position[:, None] >= sample_starts[None, :]) & (position[:, None] < sample_ends[None, :])
    ).astype(jnp.float32)
    _, _, _, _, ref_lp = column_section(
        normed_cols, state_cols, ids_all, [(ref_gate_w, ref_up_w, ref_down_w)], group_index
    )
    ref_own = lax.dynamic_slice_in_dim(ref_lp[:, 0], own_start, token_count, 0)
    group_normed = lax.all_gather(normed, "fsdp", axis=0, tiled=True)
    row_block = group_normed
    gate_pre = jnp.dot(
        row_block,
        lax.all_gather(pol_gate_w, "dp", axis=0, tiled=True),
        preferred_element_type=jnp.float32,
    )
    up_pre = jnp.dot(
        row_block,
        lax.all_gather(pol_up_w, "dp", axis=0, tiled=True),
        preferred_element_type=jnp.float32,
    )
    down_full = lax.all_gather(pol_down_w, "dp", axis=1, tiled=True)
    hidden = (jax.nn.silu(gate_pre) * up_pre).astype(jnp.bfloat16)
    row_block = hidden
    pol_out = lax.psum_scatter(
        jnp.dot(row_block, down_full, preferred_element_type=jnp.float32),
        "fsdp",
        scatter_dimension=0,
        tiled=True,
    )
    logits = hidden_states.astype(jnp.float32) + pol_out
    row_peak = jnp.max(logits, axis=1)
    log_total = row_peak + jnp.log(jnp.sum(jnp.exp(logits - row_peak[:, None]), axis=1))
    columns = jnp.arange(model_width, dtype=jnp.int32)
    onehot = (columns[None, :] == token_ids[:, None]).astype(jnp.float32)
    pol_own = (
        jnp.sum(jnp.where(columns[None, :] == token_ids[:, None], logits, 0.0), axis=1) - log_total
    )
    advantage, weight = leave_one_out(pol_own - ref_own, inside, prompt_index, rewards)
    grad_logits = (-weight[:, None] * (onehot - jnp.exp(logits - log_total[:, None]))).astype(
        jnp.bfloat16
    )
    group_grads = lax.all_gather(grad_logits, "fsdp", axis=0, tiled=True)
    down_term = lax.dot_general(
        hidden, group_grads, (((0,), (0,)), ((), ())), preferred_element_type=jnp.float32
    )
    grad_down = lax.psum_scatter(
        down_term.astype(jnp.bfloat16), "dp", scatter_dimension=1, tiled=True
    ).astype(jnp.float32)
    grad_hidden = lax.dot_general(
        group_grads, down_full, (((1,), (1,)), ((), ())), preferred_element_type=jnp.float32
    )
    sigmoid_gate = jax.nn.sigmoid(gate_pre)
    grad_gate_pre = grad_hidden * up_pre * sigmoid_gate * (1.0 + gate_pre * (1.0 - sigmoid_gate))
    grad_up_pre = grad_hidden * gate_pre * sigmoid_gate
    gate_grads = jnp.concatenate(
        [grad_gate_pre.astype(jnp.bfloat16), grad_up_pre.astype(jnp.bfloat16)], axis=1
    )
    row_block = group_normed
    grad_inner = lax.psum_scatter(
        lax.dot_general(
            row_block, gate_grads, (((0,), (0,)), ((), ())), preferred_element_type=jnp.float32
        ).astype(jnp.bfloat16),
        "dp",
        scatter_dimension=0,
        tiled=True,
    ).astype(jnp.float32)
    return (grad_inner[:, :unit_count], grad_inner[:, unit_count:], grad_down, advantage[None, :])


def solution(mesh):
    return jax.shard_map(
        local,
        mesh=mesh,
        in_specs=(
            P(("dp", "fsdp"), None),
            P(("dp", "fsdp")),
            P(),
            P("dp", "fsdp"),
            P("dp", "fsdp"),
            P("fsdp", "dp"),
            P("dp", "fsdp"),
            P("dp", "fsdp"),
            P("fsdp", "dp"),
            P("dp", None),
            P("dp", None),
            P("dp", None),
        ),
        out_specs=(P("dp", "fsdp"), P("dp", "fsdp"), P("fsdp", "dp"), P("dp", None)),
        check_vma=False,
    )
```

profile of v0, /device:TPU:0, one launch (start us, length us, event | category | flops | bytes accessed | tf_op | source)
XLA Modules:
  0.0 356.7 jit_solution(6231580681784564363)
XLA Ops:
  7.2 0.0 all-gather.5.cloned.1.call-start
  7.2 0.9 fusion.12
  8.1 1.5 fusion.15
  9.6 0.0 all-reduce.5.cloned.1.call-start
  9.7 58.1 %all-gather.5.cloned.1.call-done = bf16[32,4,4096]{2,1,0:T(4,128)(2,1)} async-done(((bf16[1,4,4096]{2,1,0:T(4,128)(2,1)}), bf16[32,4,4096]{2,1,0:T(4,128)(2,1)}) %all-gather.5.cloned.1.call-update) | async-done | bytes 1048592 | tf_op jit(solution)/shard_map/all_gather | solution.py:121
  67.8 1.3 reshape.84
  69.1 3.4 fusion.24
  72.5 1.2 multiply_convert_fusion.2
  73.7 0.9 copy-done
  74.6 2.1 fusion.25
  76.7 1.1 copy-done.8
  77.8 2.1 fusion
  80.0 2.1 fusion.9
  82.1 0.0 all-gather.7.cloned.1.call-start
  82.2 0.1 copy.19
  82.3 0.1 reduce-window.4
  82.3 0.1 reduce
  82.5 141.3 %all-reduce.5.cloned.1.call-done = (f32[128,4096]{1,0:T(8,128)}, f32[128,4096]{1,0:T(8,128)}) async-done(((f32[128,4096]{1,0:T(8,128)}, f32[128,4096]{1,0:T(8,128)}), (f32[128,4096]{1,0:T(8,128)}, f32[128,4096]{1,0:T(8,128)})) %all-reduce.5.cloned.1.call-update) | async-done | bytes 4194320
  223.8 1.1 fusion.17
  224.8 1.2 exponential_reduce_fusion
  226.1 1.1 exponential_reduce_fusion.1
  227.2 0.1 select_reduce_fusion.4
  227.3 39.5 %psum.7 = f32[32]{0:T(128)S(1)} all-reduce(f32[32]{0:T(128)S(1)} %get-tuple-element.12), channel_id=1, replica_groups=mesh['dp'=1,'fsdp'=32] {'fsdp'}, use_global_device_ids=true, to_apply=%region_11.12 | all-reduce | flops 32 | bytes 256 | tf_op jit(solution)/shard_map/psum | solution.py:75
  266.9 0.2 select_reduce_fusion.2
  267.1 0.1 select_reduce_fusion.3
  267.2 1.6 fusion.16
  268.8 53.2 %all-gather.7.cloned.1.call-done = bf16[32,4,4096]{2,1,0:T(4,128)(2,1)} async-done(((bf16[1,4,4096]{2,1,0:T(4,128)(2,1)}), bf16[32,4,4096]{2,1,0:T(4,128)(2,1)}) %all-gather.7.cloned.1.call-update) | async-done | bytes 1048592 | tf_op jit(solution)/shard_map/all_gather | solution.py:154
  322.1 1.3 reshape.86
  323.4 4.3 %fusion.4 = f32[462,4096]{1,0:T(8,128)} fusion(bf16[128,462]{0,1:T(8,128)(2,1)S(1)} %get-tuple-element.20, bf16[128,4096]{1,0:T(8,128)(2,1)S(1)} %reshape.86), kind=kOutput, calls=%fused_computation.6 | convolution fusion | flops 488226816 | bytes 8736256 | tf_op jit(solution)/shard_map/dot_general | solution.py:155
  327.7 1.1 multiply_convert_fusion.1
  328.8 7.5 %convert_convert_fusion = f32[4096,924]{0,1:T(8,128)} fusion(bf16[128,4096]{1,0:T(8,128)(2,1)S(1)} %reshape.84, bf16[128,462]{0,1:T(8,128)(2,1)S(1)} %get-tuple-element.19, bf16[128,462]{0,1:T(8,128)(2,1)S(1)} %get-tuple-element.18), kind=kOutput, calls=%fused_computation.4 | convolution fusion | flops 976926720 | bytes 16423936 | tf_op jit(solution)/shard_map/dot_general | solution.py:172
  336.3 13.9 %fusion.23 = (f32[4096,462]{0,1:T(8,128)}, f32[4096,462]{0,1:T(8,128)}) fusion(f32[4096,924]{0,1:T(8,128)} %convert_convert_fusion), kind=kLoop, calls=%fused_computation.50 | loop fusion | bytes 30277632 | tf_op jit(solution)/shard_map/slice | solution.py:179
  (32 shorter events, 0.2 us)
Async XLA Ops:
  7.2 60.6 %all-gather.5.cloned.1.call-start = ((), (), s32[]{:S(2)}) async-start(), calls=%async_computation | async-start | bytes 1081344 | tf_op jit(solution)/shard_map/all_gather | solution.py:121
  9.6 214.1 %all-reduce.5.cloned.1.call-start = ((), (), s32[]{:S(2)}) async-start(), calls=%async_computation.2 | async-start | bytes 8388608
  69.1 3.4 copy-start.2
  72.5 2.1 copy-start
  72.5 4.1 %copy-start.9 = (bf16[4096,462]{0,1:T(8,128)(2,1)S(1)}, bf16[4096,462]{0,1:T(8,128)(2,1)}, u32[]{:S(2)}) copy-start(bf16[4096,462]{0,1:T(8,128)(2,1)} %param.15) | copy-start | bytes 11354116
  73.7 4.1 %copy-start.8 = (bf16[4096,462]{0,1:T(8,128)(2,1)S(1)}, bf16[4096,462]{0,1:T(8,128)(2,1)}, u32[]{:S(2)}) copy-start(bf16[4096,462]{0,1:T(8,128)(2,1)} %param.16) | copy-start | bytes 11354116
  77.8 2.1 copy-start.3
  79.9 2.2 copy-start.7
  80.0 143.8 %copy-start.4 = (bf16[4,4096]{1,0:T(4,128)(2,1)S(1)}, bf16[4,4096]{1,0:T(4,128)(2,1)}, u32[]{:S(2)}) copy-start(bf16[4,4096]{1,0:T(4,128)(2,1)} %param.12) | copy-start | bytes 98308
  80.0 144.8 %copy-start.5 = (s32[4]{0:T(128)S(1)}, s32[4]{0:T(128)}, u32[]{:S(2)}) copy-start(s32[4]{0:T(128)} %param.13) | copy-start | bytes 52
  82.1 184.8 %copy-start.10 = (f32[1,32]{1,0:T(1,128)S(1)}, f32[1,32]{1,0:T(1,128)}, u32[]{:S(2)}) copy-start(f32[1,32]{1,0:T(1,128)} %param.23) | copy-start | bytes 388
  82.1 184.8 %copy-start.6 = (s32[1,32]{1,0:T(1,128)S(1)}, s32[1,32]{1,0:T(1,128)}, u32[]{:S(2)}) copy-start(s32[1,32]{1,0:T(1,128)} %param.22) | copy-start | bytes 388
  82.1 239.9 %all-gather.7.cloned.1.call-start = ((), (), s32[]{:S(2)}) async-start(), calls=%async_computation.1 | async-start | bytes 1081344 | tf_op jit(solution)/shard_map/all_gather | solution.py:154
  267.0 60.6 %copy-start.11 = (f32[32]{0:T(128)}, f32[32]{0:T(128)S(1)}, u32[]{:S(2)}) copy-start(f32[32]{0:T(128)S(1)} %multiply_subtract_fusion) | copy-start | bytes 388
  323.4 4.3 %copy-start.1 = (bf16[462,4096]{1,0:T(8,128)(2,1)S(1)}, bf16[462,4096]{1,0:T(8,128)(2,1)}, u32[]{:S(2)}) copy-start(bf16[462,4096]{1,0:T(8,128)(2,1)} %param.20) | copy-start | bytes 11354116
Sparse Core Ops, SparseCore 0:
  11.4 56.3 all-gather.4
  82.2 141.4 all-reduce.4
  269.0 53.0 all-gather.6
where the time goes:
time: 357 us
  waiting for transfers between devices  253 us (71%)
  blocking collectives  39.5 us (11%)
  matrix products  23.7 us (7%)
  local copies, waits for them, and re-layouts  18.7 us (5%)
  between operations  13.9 us (4%)
  other arithmetic  8.04 us (2%)
    unnamed x4, waiting for transfers between devices  141 us
    all_gather x1, waiting for transfers between devices, local(): group_normed = lax.all_gather(normed, 'fsdp', axis=0, tiled=True)  58.1 us
    all_gather x1, waiting for transfers between devices, local(): group_grads = lax.all_gather(grad_logits, 'fsdp', axis=0, tiled=True)  53.2 us
    psum x1, blocking collectives, leave_one_out(): divergence = lax.psum(jnp.sum(log_gap[:, None] * inside, axis=0), 'fsdp')  39.5 us
    slice x1, local copies, waits for them, and re-layouts, local(): grad_inner[:, unit_count:]  13.9 us
    dot_general x1, matrix products, local(): lax.dot_general(row_block, gate_grads, (((0,), (0,)), ((), ())), preferre...  7.46 us
  transfers between devices with their start and end apart: 3, of which 3 were waited for; matrix products, arithmetic and copies ran while one was open for 0% of the time, Pallas kernels for 0%

commit v1 on v0

--- a/solution.py
+++ b/solution.py
@@ -1,5 +1,6 @@
 import jax
 import jax.numpy as jnp
+import numpy as np
 from jax import lax
 from jax.sharding import PartitionSpec as P
 
@@ -8,6 +9,148 @@
 
 EPSILON = 1e-06
 KL_WEIGHT = 0.05
+PIECES = 3
+LANES = 128
+
+
+def exchange_levels(members):
+    bits = [1 << b for b in range(members.bit_length() - 1)]
+    levels, rest = [bits[:1]], bits[1:]
+    while rest:
+        low, rest = rest[:2], rest[2:]
+        levels.append(low + [low[0] | low[1]] if len(low) == 2 else low)
+    return [level for level in levels if level]
+
+
+def swap(values, mask):
+    members = lax.axis_size("fsdp")
+    return lax.ppermute(values, "fsdp", [(i, i ^ mask) for i in range(members)])
+
+
+def gather_rows(rows, levels):
+    for level in reversed(levels):
+        rows = jnp.concatenate([rows] + [swap(rows, mask) for mask in level], axis=0)
+    return rows
+
+
+def scatter_rows(sums, levels):
+    for level in levels:
+        count = sums.shape[0] // (len(level) + 1)
+        own = sums[:count]
+        for place, mask in enumerate(level):
+            block = sums[(place + 1) * count : (place + 2) * count]
+            own = own + swap(block.astype(jnp.bfloat16), mask).astype(jnp.float32)
+        sums = own
+    return sums
+
+
+def row_masks(levels):
+    masks = np.zeros((1,), np.int32)
+    for level in reversed(levels):
+        masks = np.concatenate([masks] + [masks ^ mask for mask in level])
+    return masks
+
+
+def split_float(value):
+    pieces = []
+    for _ in range(PIECES):
+        piece = lax.reduce_precision(value, 8, 7)
+        pieces.append(piece)
+        value = value - piece
+    return pieces
+
+
+def local_single(
+    hidden_states,
+    token_ids,
+    norm_gain,
+    ref_gate_w,
+    ref_up_w,
+    ref_down_w,
+    pol_gate_w,
+    pol_up_w,
+    pol_down_w,
+    sample_lengths,
+    prompt_index,
+    rewards,
+):
+    token_count, width = hidden_states.shape
+    levels = exchange_levels(lax.axis_size("fsdp"))
+    masks = row_masks(levels)
+    tokens = token_count * masks.size
+    member = lax.axis_index("fsdp").astype(jnp.int32)
+
+    normed = normalize(gather_rows(hidden_states, levels), norm_gain)
+
+    def forward(gate_w, up_w, down_w):
+        gate_pre = jnp.dot(normed, gate_w, preferred_element_type=jnp.float32)
+        up_pre = jnp.dot(normed, up_w, preferred_element_type=jnp.float32)
+        hidden = (jax.nn.silu(gate_pre) * up_pre).astype(jnp.bfloat16)
+        return gate_pre, up_pre, hidden, jnp.dot(hidden, down_w, preferred_element_type=jnp.float32)
+
+    gate_pre, up_pre, hidden, pol_part = forward(pol_gate_w, pol_up_w, pol_down_w)
+    _, _, _, ref_part = forward(ref_gate_w, ref_up_w, ref_down_w)
+    sums = scatter_rows(jnp.concatenate([pol_part, ref_part], axis=1), levels)
+
+    states = hidden_states.astype(jnp.float32)
+    columns = jnp.arange(width, dtype=jnp.int32)
+    chosen = columns[None, :] == token_ids[:, None]
+
+    def token_logprob(logits):
+        row_peak = jnp.max(logits, axis=1)
+        log_total = row_peak + jnp.log(jnp.sum(jnp.exp(logits - row_peak[:, None]), axis=1))
+        return jnp.sum(jnp.where(chosen, logits, 0.0), axis=1) - log_total, log_total
+
+    logits = states + sums[:, :width]
+    pol_lp, log_total = token_logprob(logits)
+    ref_lp, _ = token_logprob(states + sums[:, width:])
+    slopes = jnp.exp(logits - log_total[:, None]) - chosen.astype(jnp.float32)
+    extra = jnp.stack(split_float(pol_lp - ref_lp), axis=1)
+    extra = jnp.pad(extra, ((0, 0), (0, LANES - PIECES)))
+    sent = jnp.concatenate([slopes, extra], axis=1).astype(jnp.bfloat16)
+    received = gather_rows(sent, levels)
+    slopes_all = received[:, :width]
+    gap = jnp.sum(received[:, width : width + PIECES].astype(jnp.float32), axis=1)
+
+    sample_ends = jnp.cumsum(sample_lengths[0])
+    sample_starts = sample_ends - sample_lengths[0]
+
+    def inside_of(position):
+        return (position[:, None] >= sample_starts[None, :]) & (
+            position[:, None] < sample_ends[None, :]
+        )
+
+    row_place = (
+        (member ^ jnp.asarray(np.repeat(masks, token_count))) * token_count
+        + jnp.asarray(np.tile(np.arange(token_count, dtype=np.int32), masks.size))
+    )
+    place = jnp.arange(tokens, dtype=jnp.int32)
+    ordered = jnp.sum(jnp.where(place[:, None] == row_place[None, :], gap[None, :], 0.0), axis=1)
+    divergence = jnp.sum(jnp.where(inside_of(place), ordered[:, None], 0.0), axis=0)
+    scores = rewards[0] - KL_WEIGHT * divergence
+    same_prompt = prompt_index[0][:, None] == prompt_index[0][None, :]
+    others = jnp.sum(jnp.where(same_prompt, scores[None, :], 0.0), axis=1) - scores
+    advantage = scores - others / (K - 1)
+    weight = jnp.sum(jnp.where(inside_of(row_place), advantage[None, :], 0.0), axis=1)
+
+    weighted = (hidden.astype(jnp.float32) * weight[:, None]).astype(jnp.bfloat16)
+    rows_first = (((0,), (0,)), ((), ()))
+    grad_down = lax.dot_general(
+        weighted, slopes_all, rows_first, preferred_element_type=jnp.float32
+    )
+    grad_hidden = weight[:, None] * lax.dot_general(
+        slopes_all, pol_down_w, (((1,), (1,)), ((), ())), preferred_element_type=jnp.float32
+    )
+    sigmoid_gate = jax.nn.sigmoid(gate_pre)
+    grad_gate_pre = grad_hidden * up_pre * sigmoid_gate * (1.0 + gate_pre * (1.0 - sigmoid_gate))
+    grad_up_pre = grad_hidden * gate_pre * sigmoid_gate
+    grad_gate = lax.dot_general(
+        normed, grad_gate_pre.astype(jnp.bfloat16), rows_first, preferred_element_type=jnp.float32
+    )
+    grad_up = lax.dot_general(
+        normed, grad_up_pre.astype(jnp.bfloat16), rows_first, preferred_element_type=jnp.float32
+    )
+    return grad_gate, grad_up, grad_down, advantage[None, :]
 
 
 def combined_all(part, axis, combine):
@@ -180,8 +323,10 @@
 
 
 def solution(mesh):
+    members = mesh.shape["fsdp"]
+    single = mesh.shape["dp"] == 1 and members > 1 and members & (members - 1) == 0
     return jax.shard_map(
-        local,
+        local_single if single else local,
         mesh=mesh,
         in_specs=(
             P(("dp", "fsdp"), None),

time: 357 us -> 114 us (0.32)
  waiting for transfers between devices: 253 us -> 37.6 us
  blocking collectives: 39.5 us -> 0 us
  starting transfers between devices: 0.12 us -> 25.6 us
  between operations: 13.9 us -> 0.92 us
  local copies, waits for them, and re-layouts: 18.7 us -> 9.21 us
  matrix products: 23.7 us -> 31.9 us
    unnamed x4 -> x0, waiting for transfers between devices: 141 us -> none
    all_gather x2 -> x0, waiting for transfers between devices: 111 us -> none  [the longest x1 58.1 us: local(): group_normed = lax.all_gather(normed, 'fsdp', axis=0, tiled=True)]
    psum x1 -> x0, blocking collectives: 39.5 us -> none  [leave_one_out(): divergence = lax.psum(jnp.sum(log_gap[:, None] * inside, axis=0), 'fsdp')]
    ppermute x0 -> x21, waiting for transfers between devices: none -> 37.6 us  [swap(): return lax.ppermute(values, 'fsdp', [(i, i ^ mask) for i in range(members)])]
    ppermute x0 -> x21, starting transfers between devices: none -> 25.6 us  [swap(): return lax.ppermute(values, 'fsdp', [(i, i ^ mask) for i in range(members)])]
    slice x1 -> x2, local copies, waits for them, and re-layouts: 13.9 us -> 0.13 us  [scatter_rows(): block = sums[(place + 1) * count:(place + 2) * count]]
    dot_general x8 -> x9, matrix products: 23.7 us -> 31.9 us  [the longest x2 8.38 us: forward(): jnp.dot(hidden, down_w, preferred_element_type=jnp.float32)]
    concatenate x0 -> x4, local copies, waits for them, and re-layouts: none -> 7.88 us  [gather_rows(): jnp.concatenate([rows] + [swap(rows, mask) for mask in level], axis=0)]
  transfers between devices with their start and end apart: 3 -> 21, of which waited for: 3 -> 17; matrix products, arithmetic and copies ran while one was open for 0% -> 2% of each run, Pallas kernels for 0% -> 0%
where the time goes in v1:
time: 114 us; the launch traced here: 113 us
  waiting for transfers between devices  37.6 us (33%)
  matrix products  31.9 us (28%)
  starting transfers between devices  25.6 us (22%)
  local copies, waits for them, and re-layouts  9.21 us (8%)
  other arithmetic  8.1 us (7%)
    ppermute x21, waiting for transfers between devices, swap(): return lax.ppermute(values, 'fsdp', [(i, i ^ mask) for i in range(members)])  37.6 us
    ppermute x21, starting transfers between devices, swap(): return lax.ppermute(values, 'fsdp', [(i, i ^ mask) for i in range(members)])  25.6 us
    dot_general x2, matrix products, forward(): jnp.dot(hidden, down_w, preferred_element_type=jnp.float32)  8.38 us
    concatenate x4, local copies, waits for them, and re-layouts, gather_rows(): jnp.concatenate([rows] + [swap(rows, mask) for mask in level], axis=0)  7.88 us
    dot_general x2, matrix products, forward(): gate_pre = jnp.dot(normed, gate_w, preferred_element_type=jnp.float32)  5.37 us
    dot_general x1, matrix products, local_single(): lax.dot_general(normed, grad_gate_pre.astype(jnp.bfloat16), rows_first, p...  4.38 us
    dot_general x1, matrix products, local_single(): lax.dot_general(normed, grad_up_pre.astype(jnp.bfloat16), rows_first, pre...  4.36 us
    dot_general x1, matrix products, local_single(): lax.dot_general(weighted, slopes_all, rows_first, preferred_element_type=...  4.27 us
  transfers between devices with their start and end apart: 21, of which 17 were waited for; matrix products, arithmetic and copies ran while one was open for 2% of the time, Pallas kernels for 0%

profile of v1, /device:TPU:0, one launch (start us, length us, event | category | flops | bytes accessed | tf_op | source)
XLA Modules:
  0.0 113.4 jit_solution(7275168301519902232)
XLA Ops:
  0.6 3.1 %collective-permute-start = (bf16[4,4096]{1,0:T(4,128)(2,1)}, bf16[4,4096]{1,0:T(4,128)(2,1)S(1)}, u32[]{:S(2)}, u32[]{:S(2)}) collective-permute-start(bf16[4,4096]{1,0:T(4,128)(2,1)} %param.14), channel_id=1, source_target_pairs={{0,8},{1,9},{2,10},{3,11},{4,12},{5,13},{6,14},{7,15},{8,0},{9,1},... | collective-permute-start | bytes 98312 | tf_op jit(solution)/shard_map/ppermute | solution.py:27
  3.7 2.6 %collective-permute-start.1 = (bf16[4,4096]{1,0:T(4,128)(2,1)}, bf16[4,4096]{1,0:T(4,128)(2,1)S(1)}, u32[]{:S(2)}, u32[]{:S(2)}) collective-permute-start(bf16[4,4096]{1,0:T(4,128)(2,1)} %param.14), channel_id=1, source_target_pairs={{0,16},{1,17},{2,18},{3,19},{4,20},{5,21},{6,22},{7,23},{8,24},{9,... | collective-permute-start | bytes 98312 | tf_op jit(solution)/shard_map/ppermute | solution.py:27
  6.3 3.0 %collective-permute-done.1 = bf16[4,4096]{1,0:T(4,128)(2,1)S(1)} collective-permute-done((bf16[4,4096]{1,0:T(4,128)(2,1)}, bf16[4,4096]{1,0:T(4,128)(2,1)S(1)}, u32[]{:S(2)}, u32[]{:S(2)}) %collective-permute-start.1) | collective-permute-done | bytes 32800 | tf_op jit(solution)/shard_map/ppermute | solution.py:27
  9.4 2.9 %collective-permute-done.2 = bf16[4,4096]{1,0:T(4,128)(2,1)S(1)} collective-permute-done((bf16[4,4096]{1,0:T(4,128)(2,1)}, bf16[4,4096]{1,0:T(4,128)(2,1)S(1)}, u32[]{:S(2)}, u32[]{:S(2)}) %collective-permute-start.2) | collective-permute-done | bytes 32800 | tf_op jit(solution)/shard_map/ppermute | solution.py:27
  13.1 1.6 %collective-permute-start.3 = (bf16[16,4096]{1,0:T(8,128)(2,1)S(1)}, bf16[16,4096]{1,0:T(8,128)(2,1)S(1)}, u32[]{:S(2)}, u32[]{:S(2)}) collective-permute-start(bf16[16,4096]{1,0:T(8,128)(2,1)S(1)} %pad_maximum_fusion.2), channel_id=1, source_target_pairs={{0,2},{1,3},{2,0},{3,1},{4,6},{5,7},{6,4},{7,5},{8,10},{9,11},{10,... | collective-permute-start | bytes 393224 | tf_op jit(solution)/shard_map/ppermute | solution.py:27
  14.7 1.5 %collective-permute-start.4 = (bf16[16,4096]{1,0:T(8,128)(2,1)S(1)}, bf16[16,4096]{1,0:T(8,128)(2,1)S(1)}, u32[]{:S(2)}, u32[]{:S(2)}) collective-permute-start(bf16[16,4096]{1,0:T(8,128)(2,1)S(1)} %pad_maximum_fusion.2), channel_id=1, source_target_pairs={{0,4},{1,5},{2,6},{3,7},{4,0},{5,1},{6,2},{7,3},{8,12},{9,13},{10,... | collective-permute-start | bytes 393224 | tf_op jit(solution)/shard_map/ppermute | solution.py:27
  16.7 2.5 %collective-permute-done.3 = bf16[16,4096]{1,0:T(8,128)(2,1)S(1)} collective-permute-done((bf16[16,4096]{1,0:T(8,128)(2,1)S(1)}, bf16[16,4096]{1,0:T(8,128)(2,1)S(1)}, u32[]{:S(2)}, u32[]{:S(2)}) %collective-permute-start.3) | collective-permute-done | bytes 131104 | tf_op jit(solution)/shard_map/ppermute | solution.py:27
  20.4 1.6 %collective-permute-done.5 = bf16[16,4096]{1,0:T(8,128)(2,1)S(1)} collective-permute-done((bf16[16,4096]{1,0:T(8,128)(2,1)S(1)}, bf16[16,4096]{1,0:T(8,128)(2,1)S(1)}, u32[]{:S(2)}, u32[]{:S(2)}) %collective-permute-start.5) | collective-permute-done | bytes 131104 | tf_op jit(solution)/shard_map/ppermute | solution.py:27
  23.0 1.9 %collective-permute-done.6 = bf16[64,4096]{1,0:T(8,128)(2,1)S(1)} collective-permute-done((bf16[64,4096]{1,0:T(8,128)(2,1)S(1)}, bf16[64,4096]{1,0:T(8,128)(2,1)S(1)}, u32[]{:S(2)}, u32[]{:S(2)}) %collective-permute-start.6) | collective-permute-done | bytes 524320 | tf_op jit(solution)/shard_map/ppermute | solution.py:27
  26.3 3.5 %fusion.47 = f32[128,462]{0,1:T(8,128)S(1)} fusion(bf16[4096,462]{0,1:T(8,128)(2,1)} %param.20, bf16[128,4096]{1,0:T(8,128)(2,1)S(1)} %concatenate.31, f32[4096]{0:T(1024)S(1)} %copy-done.3, f32[128]{0:T(128)S(1)} %add_rsqrt_fusion), kind=kOutput, calls=%fused_computation.85 | convolution fusion | flops 486539264 | bytes 5086720 | tf_op jit(solution)/shard_map/dot_general | solution.py:86
  29.8 1.9 %fusion.43 = f32[128,462]{0,1:T(8,128)} fusion(bf16[4096,462]{0,1:T(8,128)(2,1)S(1)} %copy-done.11, bf16[128,4096]{1,0:T(8,128)(2,1)S(1)} %concatenate.31, f32[4096]{0:T(1024)S(1)} %copy-done.3, f32[128]{0:T(128)S(1)} %add_rsqrt_fusion), kind=kOutput, calls=%fused_computation.83 | convolution fusion | flops 486539264 | bytes 5086720 | tf_op jit(solution)/shard_map/dot_general | solution.py:86
  31.8 1.9 %multiply_convert_fusion.4 = (bf16[128,462]{0,1:T(8,128)(2,1)S(1)}, f32[128,462]{0,1:T(8,128)}) fusion(f32[128,462]{0,1:T(8,128)S(1)} %fusion.47, bf16[4096,462]{0,1:T(8,128)(2,1)S(1)} %copy-done.12, bf16[128,4096]{1,0:T(8,128)(2,1)S(1)} %concatenate.31, f32[4096]{0:T(1024)S(1)} %copy-done.3, f32[128]{0:T(128)S(1)} %add_rsqrt_fusion), kind=kOutput, calls=%fused_computation.22 | convolution fusion | flops 486894080 | bytes 5441536 | tf_op jit(solution)/shard_map/dot_general | solution.py:87
  33.9 2.1 %fusion.55 = f32[128,4096]{1,0:T(8,128)} fusion(bf16[128,462]{0,1:T(8,128)(2,1)S(1)} %get-tuple-element.25, bf16[462,4096]{1,0:T(8,128)(2,1)S(1)} %copy-done.1), kind=kOutput, calls=%fused_computation.90 | convolution fusion | flops 484442112 | bytes 6000128 | tf_op jit(solution)/shard_map/dot_general | solution.py:89
  36.0 6.3 %fusion.13 = f32[128,4096]{1,0:T(8,128)S(1)} fusion(bf16[462,4096]{1,0:T(8,128)(2,1)} %param.19, f32[128,462]{0,1:T(8,128)} %fusion.43, bf16[4096,462]{0,1:T(8,128)(2,1)} %param.18, bf16[128,4096]{1,0:T(8,128)(2,1)S(1)} %concatenate.31, f32[4096]{0:T(1024)S(1)} %copy-done.3, f32[128]{0:T(128)S(1)} %add_rsqrt_fusion), kind=kOutput, calls=%fused_computation.29 | convolution fusion | flops 971336192 | bytes 10968576 | tf_op jit(solution)/shard_map/dot_general | solution.py:89
  44.0 2.5 %collective-permute-done.7 = bf16[64,8192]{1,0:T(8,128)(2,1)S(1)} collective-permute-done((bf16[64,8192]{1,0:T(8,128)(2,1)S(1)}, bf16[64,8192]{1,0:T(8,128)(2,1)S(1)}, u32[]{:S(2)}, u32[]{:S(2)}) %collective-permute-start.7) | collective-permute-done | bytes 1048608 | tf_op jit(solution)/shard_map/ppermute | solution.py:27
  47.4 1.5 %collective-permute-start.9 = (bf16[16,8192]{1,0:T(8,128)(2,1)S(1)}, bf16[16,8192]{1,0:T(8,128)(2,1)S(1)}, u32[]{:S(2)}, u32[]{:S(2)}) collective-permute-start(bf16[16,8192]{1,0:T(8,128)(2,1)S(1)} %get-tuple-element.18), channel_id=1, source_target_pairs={{0,4},{1,5},{2,6},{3,7},{4,0},{5,1},{6,2},{7,3},{8,12},{9,13},{10,... | collective-permute-start | bytes 786440 | tf_op jit(solution)/shard_map/ppermute | solution.py:27
  48.9 1.5 %collective-permute-start.8 = (bf16[16,8192]{1,0:T(8,128)(2,1)S(1)}, bf16[16,8192]{1,0:T(8,128)(2,1)S(1)}, u32[]{:S(2)}, u32[]{:S(2)}) collective-permute-start(bf16[16,8192]{1,0:T(8,128)(2,1)S(1)} %get-tuple-element.16), channel_id=1, source_target_pairs={{0,2},{1,3},{2,0},{3,1},{4,6},{5,7},{6,4},{7,5},{8,10},{9,11},{10,... | collective-permute-start | bytes 786440 | tf_op jit(solution)/shard_map/ppermute | solution.py:27
  50.4 6.6 %collective-permute-done.10 = bf16[16,8192]{1,0:T(8,128)(2,1)S(1)} collective-permute-done((bf16[16,8192]{1,0:T(8,128)(2,1)S(1)}, bf16[16,8192]{1,0:T(8,128)(2,1)S(1)}, u32[]{:S(2)}, u32[]{:S(2)}) %collective-permute-start.10) | collective-permute-done | bytes 262176 | tf_op jit(solution)/shard_map/ppermute | solution.py:27
  57.1 4.1 %collective-permute-done.9 = bf16[16,8192]{1,0:T(8,128)(2,1)S(1)} collective-permute-done((bf16[16,8192]{1,0:T(8,128)(2,1)S(1)}, bf16[16,8192]{1,0:T(8,128)(2,1)S(1)}, u32[]{:S(2)}, u32[]{:S(2)}) %collective-permute-start.9) | collective-permute-done | bytes 262176 | tf_op jit(solution)/shard_map/ppermute | solution.py:27
  62.1 3.8 %collective-permute-start.11 = (bf16[4,8192]{1,0:T(4,128)(2,1)S(1)}, bf16[4,8192]{1,0:T(4,128)(2,1)S(1)}, u32[]{:S(2)}, u32[]{:S(2)}) collective-permute-start(bf16[4,8192]{1,0:T(4,128)(2,1)S(1)} %get-tuple-element.19), channel_id=1, source_target_pairs={{0,8},{1,9},{2,10},{3,11},{4,12},{5,13},{6,14},{7,15},{8,0},{9,1},... | collective-permute-start | bytes 196616 | tf_op jit(solution)/shard_map/ppermute | solution.py:27
  65.9 2.2 %collective-permute-done.13 = bf16[4,8192]{1,0:T(4,128)(2,1)S(1)} collective-permute-done((bf16[4,8192]{1,0:T(4,128)(2,1)S(1)}, bf16[4,8192]{1,0:T(4,128)(2,1)S(1)}, u32[]{:S(2)}, u32[]{:S(2)}) %collective-permute-start.13) | collective-permute-done | bytes 65568 | tf_op jit(solution)/shard_map/ppermute | solution.py:27
  72.4 1.7 %collective-permute-start.16 = (bf16[4,4224]{1,0:T(4,128)(2,1)S(1)}, bf16[4,4224]{1,0:T(4,128)(2,1)S(1)}, u32[]{:S(2)}, u32[]{:S(2)}) collective-permute-start(bf16[4,4224]{1,0:T(4,128)(2,1)S(1)} %pad_maximum_fusion.3), channel_id=1, source_target_pairs={{0,24},{1,25},{2,26},{3,27},{4,28},{5,29},{6,30},{7,31},{8,16},{9,... | collective-permute-start | bytes 101384 | tf_op jit(solution)/shard_map/ppermute | solution.py:27
  74.1 2.2 %collective-permute-done.15 = bf16[4,4224]{1,0:T(4,128)(2,1)S(1)} collective-permute-done((bf16[4,4224]{1,0:T(4,128)(2,1)S(1)}, bf16[4,4224]{1,0:T(4,128)(2,1)S(1)}, u32[]{:S(2)}, u32[]{:S(2)}) %collective-permute-start.15) | collective-permute-done | bytes 33824 | tf_op jit(solution)/shard_map/ppermute | solution.py:27
  76.3 1.9 %collective-permute-done.16 = bf16[4,4224]{1,0:T(4,128)(2,1)S(1)} collective-permute-done((bf16[4,4224]{1,0:T(4,128)(2,1)S(1)}, bf16[4,4224]{1,0:T(4,128)(2,1)S(1)}, u32[]{:S(2)}, u32[]{:S(2)}) %collective-permute-start.16) | collective-permute-done | bytes 33824 | tf_op jit(solution)/shard_map/ppermute | solution.py:27
  80.1 1.7 %collective-permute-start.19 = (bf16[16,4224]{1,0:T(8,128)(2,1)S(1)}, bf16[16,4224]{1,0:T(8,128)(2,1)S(1)}, u32[]{:S(2)}, u32[]{:S(2)}) collective-permute-start(bf16[16,4224]{1,0:T(8,128)(2,1)S(1)} %pad_maximum_fusion.1), channel_id=1, source_target_pairs={{0,6},{1,7},{2,4},{3,5},{4,2},{5,3},{6,0},{7,1},{8,14},{9,15},{10,... | collective-permute-start | bytes 405512 | tf_op jit(solution)/shard_map/ppermute | solution.py:27
  81.8 1.5 %collective-permute-done.17 = bf16[16,4224]{1,0:T(8,128)(2,1)S(1)} collective-permute-done((bf16[16,4224]{1,0:T(8,128)(2,1)S(1)}, bf16[16,4224]{1,0:T(8,128)(2,1)S(1)}, u32[]{:S(2)}, u32[]{:S(2)}) %collective-permute-start.17) | collective-permute-done | bytes 135200 | tf_op jit(solution)/shard_map/ppermute | solution.py:27
  84.5 1.5 %collective-permute-done.19 = bf16[16,4224]{1,0:T(8,128)(2,1)S(1)} collective-permute-done((bf16[16,4224]{1,0:T(8,128)(2,1)S(1)}, bf16[16,4224]{1,0:T(8,128)(2,1)S(1)}, u32[]{:S(2)}, u32[]{:S(2)}) %collective-permute-start.19) | collective-permute-done | bytes 135200 | tf_op jit(solution)/shard_map/ppermute | solution.py:27
  88.7 5.6 %concatenate.36 = bf16[128,4224]{1,0:T(8,128)(2,1)S(1)} concatenate(bf16[4,4224]{1,0:T(4,128)(2,1)} %copy-done.5, bf16[4,4224]{1,0:T(4,128)(2,1)S(1)} %collective-permute-done.14, bf16[4,4224]{1,0:T(4,128)(2,1)S(1)} %collective-permute-done.15, bf16[4,4224]{1,0:T(4,128)(2,1)} %copy-done.4, bf16[16,4224]{1,0:T(8,128)(2,1)S(1)} %collective-permute-done.17, ...), dimensions={0} | concatenate | bytes 2162688 | tf_op jit(solution)/shard_map/concatenate | solution.py:32
  97.1 3.2 %convolution_multiply_fusion = f32[128,462]{0,1:T(8,128)S(1)} fusion(bf16[462,4096]{1,0:T(8,128)(2,1)} %param.22, bf16[128,4224]{1,0:T(8,128)(2,1)S(1)} %concatenate.36, f32[128]{0:T(128)S(1)} %select_reduce_fusion.3), kind=kOutput, calls=%fused_computation.11 | convolution fusion | flops 484501248 | bytes 5070336 | tf_op jit(solution)/shard_map/dot_general | solution.py:141
  100.4 4.3 %fusion.6 = f32[462,4096]{1,0:T(8,128)} fusion(bf16[128,4224]{1,0:T(8,128)(2,1)S(1)} %concatenate.36, bf16[128,462]{0,1:T(8,128)(2,1)S(1)} %get-tuple-element.25, f32[128]{0:T(128)S(1)} %select_reduce_fusion.3), kind=kOutput, calls=%fused_computation.12 | convolution fusion | flops 484619520 | bytes 8737280 | tf_op jit(solution)/shard_map/dot_general | solution.py:138
  104.7 4.4 %fusion.17 = f32[4096,462]{0,1:T(8,128)} fusion(f32[128,462]{0,1:T(8,128)S(1)} %convolution_multiply_fusion, f32[128,462]{0,1:T(8,128)S(1)} %fusion.47, bf16[128,4096]{1,0:T(8,128)(2,1)S(1)} %concatenate.31, f32[4096]{0:T(1024)S(1)} %copy-done.3, f32[128]{0:T(128)S(1)} %copy-done.8), kind=kOutput, calls=%fused_computation.32 | convolution fusion | flops 486894080 | bytes 9107968 | tf_op jit(solution)/shard_map/dot_general | solution.py:150
  109.0 4.4 %fusion.16 = f32[4096,462]{0,1:T(8,128)} fusion(f32[128,462]{0,1:T(8,128)S(1)} %fusion.47, f32[128,462]{0,1:T(8,128)S(1)} %convolution_multiply_fusion, f32[128,462]{0,1:T(8,128)S(1)} %copy-done.6, bf16[128,4096]{1,0:T(8,128)(2,1)S(1)} %concatenate.31, f32[4096]{0:T(1024)S(1)} %copy-done.3, f32[128]{0:T(128)S(1)} %copy-done.8), kind=kOutput, calls=%fused_computation.31 | convolution fusion | flops 487130624 | bytes 9344512 | tf_op jit(solution)/shard_map/dot_general | solution.py:147
  (79 shorter events, 21.6 us)
Async XLA Ops:
  0.6 5.7 %collective-permute-start = (bf16[4,4096]{1,0:T(4,128)(2,1)}, bf16[4,4096]{1,0:T(4,128)(2,1)S(1)}, u32[]{:S(2)}, u32[]{:S(2)}) collective-permute-start(bf16[4,4096]{1,0:T(4,128)(2,1)} %param.14), channel_id=1, source_target_pairs={{0,8},{1,9},{2,10},{3,11},{4,12},{5,13},{6,14},{7,15},{8,0},{9,1},... | collective-permute-start | bytes 98312 | tf_op jit(solution)/shard_map/ppermute | solution.py:27
  3.7 5.6 %collective-permute-start.1 = (bf16[4,4096]{1,0:T(4,128)(2,1)}, bf16[4,4096]{1,0:T(4,128)(2,1)S(1)}, u32[]{:S(2)}, u32[]{:S(2)}) collective-permute-start(bf16[4,4096]{1,0:T(4,128)(2,1)} %param.14), channel_id=1, source_target_pairs={{0,16},{1,17},{2,18},{3,19},{4,20},{5,21},{6,22},{7,23},{8,24},{9,... | collective-permute-start | bytes 98312 | tf_op jit(solution)/shard_map/ppermute | solution.py:27
  6.3 5.9 %collective-permute-start.2 = (bf16[4,4096]{1,0:T(4,128)(2,1)}, bf16[4,4096]{1,0:T(4,128)(2,1)S(1)}, u32[]{:S(2)}, u32[]{:S(2)}) collective-permute-start(bf16[4,4096]{1,0:T(4,128)(2,1)} %param.14), channel_id=1, source_target_pairs={{0,24},{1,25},{2,26},{3,27},{4,28},{5,29},{6,30},{7,31},{8,16},{9,... | collective-permute-start | bytes 98312 | tf_op jit(solution)/shard_map/ppermute | solution.py:27
  13.1 13.1 %copy-start.3 = (f32[4096]{0:T(1024)S(1)}, f32[4096]{0:T(1024)}, u32[]{:S(2)}) copy-start(f32[4096]{0:T(1024)} %param.16) | copy-start | bytes 49156
  13.1 6.1 %collective-permute-start.3 = (bf16[16,4096]{1,0:T(8,128)(2,1)S(1)}, bf16[16,4096]{1,0:T(8,128)(2,1)S(1)}, u32[]{:S(2)}, u32[]{:S(2)}) collective-permute-start(bf16[16,4096]{1,0:T(8,128)(2,1)S(1)} %pad_maximum_fusion.2), channel_id=1, source_target_pairs={{0,2},{1,3},{2,0},{3,1},{4,6},{5,7},{6,4},{7,5},{8,10},{9,11},{10,... | collective-permute-start | bytes 393224 | tf_op jit(solution)/shard_map/ppermute | solution.py:27
  14.7 5.8 %collective-permute-start.4 = (bf16[16,4096]{1,0:T(8,128)(2,1)S(1)}, bf16[16,4096]{1,0:T(8,128)(2,1)S(1)}, u32[]{:S(2)}, u32[]{:S(2)}) collective-permute-start(bf16[16,4096]{1,0:T(8,128)(2,1)S(1)} %pad_maximum_fusion.2), channel_id=1, source_target_pairs={{0,4},{1,5},{2,6},{3,7},{4,0},{5,1},{6,2},{7,3},{8,12},{9,13},{10,... | collective-permute-start | bytes 393224 | tf_op jit(solution)/shard_map/ppermute | solution.py:27
  16.2 5.9 %collective-permute-start.5 = (bf16[16,4096]{1,0:T(8,128)(2,1)S(1)}, bf16[16,4096]{1,0:T(8,128)(2,1)S(1)}, u32[]{:S(2)}, u32[]{:S(2)}) collective-permute-start(bf16[16,4096]{1,0:T(8,128)(2,1)S(1)} %pad_maximum_fusion.2), channel_id=1, source_target_pairs={{0,6},{1,7},{2,4},{3,5},{4,2},{5,3},{6,0},{7,1},{8,14},{9,15},{10,... | collective-permute-start | bytes 393224 | tf_op jit(solution)/shard_map/ppermute | solution.py:27
  22.9 2.0 %collective-permute-start.6 = (bf16[64,4096]{1,0:T(8,128)(2,1)S(1)}, bf16[64,4096]{1,0:T(8,128)(2,1)S(1)}, u32[]{:S(2)}, u32[]{:S(2)}) collective-permute-start(bf16[64,4096]{1,0:T(8,128)(2,1)S(1)} %concatenate.30), channel_id=1, source_target_pairs={{0,1},{1,0},{2,3},{3,2},{4,5},{5,4},{6,7},{7,6},{8,9},{9,8},{10,11... | collective-permute-start | bytes 1572872 | tf_op jit(solution)/shard_map/ppermute | solution.py:27
  26.3 9.7 %copy-start.7 = (f32[128]{0:T(128)}, f32[128]{0:T(128)S(1)}, u32[]{:S(2)}) copy-start(f32[128]{0:T(128)S(1)} %add_rsqrt_fusion) | copy-start | bytes 1540
  26.3 3.5 %copy-start.11 = (bf16[4096,462]{0,1:T(8,128)(2,1)S(1)}, bf16[4096,462]{0,1:T(8,128)(2,1)}, u32[]{:S(2)}) copy-start(bf16[4096,462]{0,1:T(8,128)(2,1)} %param.17) | copy-start | bytes 11354116
  42.3 4.2 %copy-start = (f32[128,4096]{1,0:T(8,128)S(1)}, f32[128,4096]{1,0:T(8,128)}, u32[]{:S(2)}) copy-start(f32[128,4096]{1,0:T(8,128)} %fusion.55) | copy-start | bytes 6291460
  43.8 2.7 %collective-permute-start.7 = (bf16[64,8192]{1,0:T(8,128)(2,1)S(1)}, bf16[64,8192]{1,0:T(8,128)(2,1)S(1)}, u32[]{:S(2)}, u32[]{:S(2)}) collective-permute-start(bf16[64,8192]{1,0:T(8,128)(2,1)S(1)} %fusion.5), channel_id=1, source_target_pairs={{0,1},{1,0},{2,3},{3,2},{4,5},{5,4},{6,7},{7,6},{8,9},{9,8},{10,11... | collective-permute-start | bytes 3145736 | tf_op jit(solution)/shard_map/ppermute | solution.py:27
  46.8 22.0 %copy-start.2 = (bf16[4,4096]{1,0:T(4,128)(2,1)S(1)}, bf16[4,4096]{1,0:T(4,128)(2,1)}, u32[]{:S(2)}) copy-start(bf16[4,4096]{1,0:T(4,128)(2,1)} %param.14) | copy-start | bytes 98308
  46.8 22.2 %copy-start.9 = (s32[4]{0:T(128)S(1)}, s32[4]{0:T(128)}, u32[]{:S(2)}) copy-start(s32[4]{0:T(128)} %param.15) | copy-start | bytes 52
  46.9 10.2 %collective-permute-start.10 = (bf16[16,8192]{1,0:T(8,128)(2,1)S(1)}, bf16[16,8192]{1,0:T(8,128)(2,1)S(1)}, u32[]{:S(2)}, u32[]{:S(2)}) collective-permute-start(bf16[16,8192]{1,0:T(8,128)(2,1)S(1)} %get-tuple-element.17), channel_id=1, source_target_pairs={{0,6},{1,7},{2,4},{3,5},{4,2},{5,3},{6,0},{7,1},{8,14},{9,15},{10,... | collective-permute-start | bytes 786440 | tf_op jit(solution)/shard_map/ppermute | solution.py:27
  47.4 13.7 %collective-permute-start.9 = (bf16[16,8192]{1,0:T(8,128)(2,1)S(1)}, bf16[16,8192]{1,0:T(8,128)(2,1)S(1)}, u32[]{:S(2)}, u32[]{:S(2)}) collective-permute-start(bf16[16,8192]{1,0:T(8,128)(2,1)S(1)} %get-tuple-element.18), channel_id=1, source_target_pairs={{0,4},{1,5},{2,6},{3,7},{4,0},{5,1},{6,2},{7,3},{8,12},{9,13},{10,... | collective-permute-start | bytes 786440 | tf_op jit(solution)/shard_map/ppermute | solution.py:27
  48.9 12.2 %collective-permute-start.8 = (bf16[16,8192]{1,0:T(8,128)(2,1)S(1)}, bf16[16,8192]{1,0:T(8,128)(2,1)S(1)}, u32[]{:S(2)}, u32[]{:S(2)}) collective-permute-start(bf16[16,8192]{1,0:T(8,128)(2,1)S(1)} %get-tuple-element.16), channel_id=1, source_target_pairs={{0,2},{1,3},{2,0},{3,1},{4,6},{5,7},{6,4},{7,5},{8,10},{9,11},{10,... | collective-permute-start | bytes 786440 | tf_op jit(solution)/shard_map/ppermute | solution.py:27
  61.4 6.6 %collective-permute-start.13 = (bf16[4,8192]{1,0:T(4,128)(2,1)S(1)}, bf16[4,8192]{1,0:T(4,128)(2,1)S(1)}, u32[]{:S(2)}, u32[]{:S(2)}) collective-permute-start(bf16[4,8192]{1,0:T(4,128)(2,1)S(1)} %get-tuple-element.20), channel_id=1, source_target_pairs={{0,24},{1,25},{2,26},{3,27},{4,28},{5,29},{6,30},{7,31},{8,16},{9,... | collective-permute-start | bytes 196616 | tf_op jit(solution)/shard_map/ppermute | solution.py:27
  62.0 6.7 %collective-permute-start.12 = (bf16[4,8192]{1,0:T(4,128)(2,1)S(1)}, bf16[4,8192]{1,0:T(4,128)(2,1)S(1)}, u32[]{:S(2)}, u32[]{:S(2)}) collective-permute-start(bf16[4,8192]{1,0:T(4,128)(2,1)S(1)} %get-tuple-element.21), channel_id=1, source_target_pairs={{0,16},{1,17},{2,18},{3,19},{4,20},{5,21},{6,22},{7,23},{8,24},{9,... | collective-permute-start | bytes 196616 | tf_op jit(solution)/shard_map/ppermute | solution.py:27
  62.1 6.7 %collective-permute-start.11 = (bf16[4,8192]{1,0:T(4,128)(2,1)S(1)}, bf16[4,8192]{1,0:T(4,128)(2,1)S(1)}, u32[]{:S(2)}, u32[]{:S(2)}) collective-permute-start(bf16[4,8192]{1,0:T(4,128)(2,1)S(1)} %get-tuple-element.19), channel_id=1, source_target_pairs={{0,8},{1,9},{2,10},{3,11},{4,12},{5,13},{6,14},{7,15},{8,0},{9,1},... | collective-permute-start | bytes 196616 | tf_op jit(solution)/shard_map/ppermute | solution.py:27
  69.6 19.1 %copy-start.5 = (bf16[4,4224]{1,0:T(4,128)(2,1)}, bf16[4,4224]{1,0:T(4,128)(2,1)S(1)}, u32[]{:S(2)}) copy-start(bf16[4,4224]{1,0:T(4,128)(2,1)S(1)} %pad_maximum_fusion.3) | copy-start | bytes 101380
  69.6 4.5 %collective-permute-start.14 = (bf16[4,4224]{1,0:T(4,128)(2,1)S(1)}, bf16[4,4224]{1,0:T(4,128)(2,1)S(1)}, u32[]{:S(2)}, u32[]{:S(2)}) collective-permute-start(bf16[4,4224]{1,0:T(4,128)(2,1)S(1)} %pad_maximum_fusion.3), channel_id=1, source_target_pairs={{0,8},{1,9},{2,10},{3,11},{4,12},{5,13},{6,14},{7,15},{8,0},{9,1},... | collective-permute-start | bytes 101384 | tf_op jit(solution)/shard_map/ppermute | solution.py:27
  71.1 5.2 %collective-permute-start.15 = (bf16[4,4224]{1,0:T(4,128)(2,1)S(1)}, bf16[4,4224]{1,0:T(4,128)(2,1)S(1)}, u32[]{:S(2)}, u32[]{:S(2)}) collective-permute-start(bf16[4,4224]{1,0:T(4,128)(2,1)S(1)} %pad_maximum_fusion.3), channel_id=1, source_target_pairs={{0,16},{1,17},{2,18},{3,19},{4,20},{5,21},{6,22},{7,23},{8,24},{9,... | collective-permute-start | bytes 101384 | tf_op jit(solution)/shard_map/ppermute | solution.py:27
  72.4 5.7 %collective-permute-start.16 = (bf16[4,4224]{1,0:T(4,128)(2,1)S(1)}, bf16[4,4224]{1,0:T(4,128)(2,1)S(1)}, u32[]{:S(2)}, u32[]{:S(2)}) collective-permute-start(bf16[4,4224]{1,0:T(4,128)(2,1)S(1)} %pad_maximum_fusion.3), channel_id=1, source_target_pairs={{0,24},{1,25},{2,26},{3,27},{4,28},{5,29},{6,30},{7,31},{8,16},{9,... | collective-permute-start | bytes 101384 | tf_op jit(solution)/shard_map/ppermute | solution.py:27
  78.2 10.6 %copy-start.4 = (bf16[4,4224]{1,0:T(4,128)(2,1)}, bf16[4,4224]{1,0:T(4,128)(2,1)S(1)}, u32[]{:S(2)}) copy-start(bf16[4,4224]{1,0:T(4,128)(2,1)S(1)} %collective-permute-done.16) | copy-start | bytes 101380
  78.2 5.1 %collective-permute-start.17 = (bf16[16,4224]{1,0:T(8,128)(2,1)S(1)}, bf16[16,4224]{1,0:T(8,128)(2,1)S(1)}, u32[]{:S(2)}, u32[]{:S(2)}) collective-permute-start(bf16[16,4224]{1,0:T(8,128)(2,1)S(1)} %pad_maximum_fusion.1), channel_id=1, source_target_pairs={{0,2},{1,3},{2,0},{3,1},{4,6},{5,7},{6,4},{7,5},{8,10},{9,11},{10,... | collective-permute-start | bytes 405512 | tf_op jit(solution)/shard_map/ppermute | solution.py:27
  79.5 5.0 %collective-permute-start.18 = (bf16[16,4224]{1,0:T(8,128)(2,1)S(1)}, bf16[16,4224]{1,0:T(8,128)(2,1)S(1)}, u32[]{:S(2)}, u32[]{:S(2)}) collective-permute-start(bf16[16,4224]{1,0:T(8,128)(2,1)S(1)} %pad_maximum_fusion.1), channel_id=1, source_target_pairs={{0,4},{1,5},{2,6},{3,7},{4,0},{5,1},{6,2},{7,3},{8,12},{9,13},{10,... | collective-permute-start | bytes 405512 | tf_op jit(solution)/shard_map/ppermute | solution.py:27
  80.1 5.9 %collective-permute-start.19 = (bf16[16,4224]{1,0:T(8,128)(2,1)S(1)}, bf16[16,4224]{1,0:T(8,128)(2,1)S(1)}, u32[]{:S(2)}, u32[]{:S(2)}) collective-permute-start(bf16[16,4224]{1,0:T(8,128)(2,1)S(1)} %pad_maximum_fusion.1), channel_id=1, source_target_pairs={{0,6},{1,7},{2,4},{3,5},{4,2},{5,3},{6,0},{7,1},{8,14},{9,15},{10,... | collective-permute-start | bytes 405512 | tf_op jit(solution)/shard_map/ppermute | solution.py:27
  86.4 2.3 %collective-permute-start.20 = (bf16[64,4224]{1,0:T(8,128)(2,1)S(1)}, bf16[64,4224]{1,0:T(8,128)(2,1)}, u32[]{:S(2)}, u32[]{:S(2)}) collective-permute-start(bf16[64,4224]{1,0:T(8,128)(2,1)S(1)} %concatenate.35), channel_id=1, source_target_pairs={{0,1},{1,0},{2,3},{3,2},{4,5},{5,4},{6,7},{7,6},{8,9},{9,8},{10,11... | collective-permute-start | bytes 1622024 | tf_op jit(solution)/shard_map/ppermute | solution.py:27
  97.0 3.3 %copy-start.10 = (f32[1,32]{1,0:T(1,128)}, f32[1,32]{1,0:T(1,128)S(1)}, u32[]{:S(2)}) copy-start(f32[1,32]{1,0:T(1,128)S(1)} %fusion.33) | copy-start | bytes 388
  100.4 4.3 %copy-start.8 = (f32[128]{0:T(128)S(1)}, f32[128]{0:T(128)}, u32[]{:S(2)}) copy-start(f32[128]{0:T(128)} %copy-done.7) | copy-start | bytes 1540
  104.7 4.4 %copy-start.6 = (f32[128,462]{0,1:T(8,128)S(1)}, f32[128,462]{0,1:T(8,128)}, u32[]{:S(2)}) copy-start(f32[128,462]{0,1:T(8,128)} %get-tuple-element.26) | copy-start | bytes 709636
  (2 other events, 4.2 us)

commit v2 on v1

--- a/solution.py
+++ b/solution.py
@@ -1,7 +1,11 @@
+import functools
+
 import jax
 import jax.numpy as jnp
 import numpy as np
 from jax import lax
+from jax.experimental import pallas as pl
+from jax.experimental.pallas import tpu as pltpu
 from jax.sharding import PartitionSpec as P
 
 K = 8
@@ -11,6 +15,9 @@
 KL_WEIGHT = 0.05
 PIECES = 3
 LANES = 128
+FETCH_VMEM = 4 << 20
+FORWARD_VMEM = 8 << 20
+BACKWARD_VMEM = 36 << 20
 
 
 def exchange_levels(members):
@@ -27,10 +34,23 @@
     return lax.ppermute(values, "fsdp", [(i, i ^ mask) for i in range(members)])
 
 
-def gather_rows(rows, levels):
-    for level in reversed(levels):
-        rows = jnp.concatenate([rows] + [swap(rows, mask) for mask in level], axis=0)
-    return rows
+def tie(first, second):
+    return lax.optimization_barrier((first, second))
+
+
+def gather_blocks(rows, levels, beside=(None, None)):
+    beside = list(beside)
+    for level in reversed(levels[2:]):
+        parts = [swap(rows, mask) for mask in level]
+        if beside[0] is not None:
+            parts, beside[0] = tie(parts, beside[0])
+        rows = jnp.concatenate([rows] + parts, axis=0)
+    blocks = [rows]
+    if len(levels) > 1:
+        blocks = blocks + [swap(rows, mask) for mask in levels[1]]
+    if beside[1] is not None:
+        blocks[1:], beside[1] = tie(blocks[1:], beside[1])
+    return blocks + [swap(block, mask) for mask in levels[0] for block in blocks], beside
 
 
 def scatter_rows(sums, levels):
@@ -58,6 +78,287 @@
         pieces.append(piece)
         value = value - piece
     return pieces
+
+
+NT = (((1,), (1,)), ((), ()))
+NN = (((1,), (0,)), ((), ()))
+
+
+def column_chunk(width):
+    return 1024 if width % 1024 == 0 else width
+
+
+def dot(left, right, dims):
+    return lax.dot_general(left, right, dims, preferred_element_type=jnp.float32)
+
+
+def fetch_kernel(*refs):
+    count = len(refs) // 2
+    sources, targets, sems = refs[:count], refs[count:-1], refs[-1]
+    copies = [
+        pltpu.make_async_copy(source, target, sems.at[place])
+        for place, (source, target) in enumerate(zip(sources, targets))
+    ]
+    for copy in copies:
+        copy.start()
+    for copy in copies:
+        copy.wait()
+
+
+def fetch(weights):
+    vmem = pl.BlockSpec(memory_space=pltpu.VMEM)
+    hbm = pl.BlockSpec(memory_space=pltpu.HBM)
+    return pl.pallas_call(
+        fetch_kernel,
+        out_shape=[jax.ShapeDtypeStruct(w.shape, w.dtype) for w in weights],
+        in_specs=[hbm] * len(weights),
+        out_specs=[vmem] * len(weights),
+        scratch_shapes=[pltpu.SemaphoreType.DMA((len(weights),))],
+        compiler_params=pltpu.CompilerParams(vmem_limit_bytes=FETCH_VMEM),
+        cost_estimate=pl.CostEstimate(
+            flops=0, bytes_accessed=sum(2 * w.size for w in weights), transcendentals=0
+        ),
+    )(*[pltpu.with_memory_space_constraint(w, pltpu.HBM) for w in weights])
+
+
+def forward_model(weights, normed, hidden_rows, sent, kept, chunk):
+    gate_w, up_w, down_w = weights
+    half = kept.shape[0]
+    gate = dot(gate_w[...], normed[...], NT)
+    up = dot(up_w[...], normed[...], NT)
+    hidden = gate * (1.0 / (1.0 + jnp.exp(-gate))) * up
+    hidden_rows[...] = hidden.T.astype(jnp.bfloat16)
+
+    def outer(step, _):
+        columns = pl.ds(pl.multiple_of(step * chunk, chunk), chunk)
+        part = dot(hidden_rows[...], down_w[:, columns], NN)
+        kept[:, columns] = part[:half]
+        sent[:, columns] = part[half:].astype(jnp.bfloat16)
+        return 0
+
+    lax.fori_loop(0, normed.shape[1] // chunk, outer, 0)
+    return gate, up, hidden
+
+
+def reference_kernel(block_count, chunk, *refs):
+    blocks = refs[:block_count]
+    gain, *weights = refs[block_count : block_count + 4]
+    normed, sent, kept, hidden_rows = refs[block_count + 4 :]
+    height = blocks[0].shape[0]
+    for place, block in enumerate(blocks):
+        values = block[...].astype(jnp.float32)
+        factor = lax.rsqrt(jnp.mean(values * values, axis=1, keepdims=True) + EPSILON)
+        normed[place * height : (place + 1) * height, :] = (values * factor * gain[...]).astype(
+            jnp.bfloat16
+        )
+    forward_model(weights, normed, hidden_rows, sent, kept, chunk)
+
+
+def policy_kernel(chunk, normed, *refs):
+    weights = refs[:3]
+    gate_out, up_out, hidden_out, sent, kept, hidden_rows = refs[3:]
+    gate, up, hidden = forward_model(weights, normed, hidden_rows, sent, kept, chunk)
+    gate_out[...] = gate
+    up_out[...] = up
+    hidden_out[...] = hidden.astype(jnp.bfloat16)
+
+
+def forward_call(kernel, operands, extra, weights, tokens):
+    units, width = weights[0].shape
+    vmem = pl.BlockSpec(memory_space=pltpu.VMEM)
+    shapes = extra + [
+        jax.ShapeDtypeStruct((tokens // 2, width), jnp.bfloat16),
+        jax.ShapeDtypeStruct((tokens // 2, width), jnp.float32),
+    ]
+    return pl.pallas_call(
+        kernel,
+        out_shape=shapes,
+        in_specs=[vmem] * (len(operands) + 3),
+        out_specs=[vmem] * len(shapes),
+        scratch_shapes=[pltpu.VMEM((tokens, units), jnp.bfloat16)],
+        compiler_params=pltpu.CompilerParams(vmem_limit_bytes=FORWARD_VMEM),
+        cost_estimate=pl.CostEstimate(
+            flops=6 * tokens * width * units,
+            bytes_accessed=6 * units * width,
+            transcendentals=tokens * units,
+        ),
+    )(*operands, *weights)
+
+
+def forward_reference(blocks, gain, weights):
+    width = blocks[0].shape[1]
+    tokens = sum(block.shape[0] for block in blocks)
+    return forward_call(
+        functools.partial(reference_kernel, len(blocks), column_chunk(width)),
+        blocks + [gain],
+        [jax.ShapeDtypeStruct((tokens, width), jnp.bfloat16)],
+        weights,
+        tokens,
+    )
+
+
+def forward_policy(normed, weights):
+    tokens, width = normed.shape
+    units = weights[0].shape[0]
+    return forward_call(
+        functools.partial(policy_kernel, column_chunk(width)),
+        [normed],
+        [jax.ShapeDtypeStruct((units, tokens), jnp.float32)] * 2
+        + [jax.ShapeDtypeStruct((units, tokens), jnp.bfloat16)],
+        weights,
+        tokens,
+    )
+
+
+def backward_kernel(block_count, chunk, *refs):
+    blocks = refs[:block_count]
+    normed, gate_ref, up_ref, hidden_ref, lengths, prompts, rewards, places, down = refs[
+        block_count : block_count + 9
+    ]
+    grad_gate, grad_up, grad_down, advantage_out = refs[block_count + 9 : block_count + 13]
+    slopes, held, total, gate_left, up_left, down_left, gate_buf, up_buf, down_buf, in_sems, sems = (
+        refs[block_count + 13 :]
+    )
+    width = normed.shape[1]
+    steps = width // chunk
+    tokens = normed.shape[0]
+    samples = lengths.shape[1]
+    height = blocks[0].shape[0]
+
+    def columns(step):
+        return pl.ds(pl.multiple_of(step * chunk, chunk), chunk)
+
+    def copy_in(step):
+        return pltpu.make_async_copy(
+            down.at[:, columns(step)], held.at[:, columns(step)], in_sems.at[step]
+        )
+
+    def copy_out(which, step):
+        source = (gate_buf, up_buf, down_buf)[which]
+        target = (grad_gate, grad_up, grad_down)[which]
+        return pltpu.make_async_copy(
+            source.at[:, columns(step)], target.at[:, columns(step)], sems.at[which, step]
+        )
+
+    for step in range(steps):
+        copy_in(step).start()
+
+    gaps = []
+    for place, block in enumerate(blocks):
+        slopes[place * height : (place + 1) * height, :] = block[:, :width]
+        gaps.append(jnp.sum(block[:, width:].astype(jnp.float32), axis=1, keepdims=True))
+    gap = jnp.concatenate(gaps, axis=0)
+
+    row = lax.broadcasted_iota(jnp.int32, (samples, samples), 0)
+    col = lax.broadcasted_iota(jnp.int32, (samples, samples), 1)
+    diagonal = row == col
+
+    def as_row(column):
+        return jnp.sum(jnp.where(diagonal, column, 0.0), axis=0, keepdims=True)
+
+    def as_column(line, mask):
+        return jnp.sum(jnp.where(mask, line, 0.0), axis=1, keepdims=True)
+
+    counts = lengths[...].astype(jnp.float32)
+    ends = as_column(counts, col <= row)
+    starts = ends - as_column(counts, diagonal)
+    kinds = prompts[...].astype(jnp.float32)
+    place_line = places[...].astype(jnp.float32)
+    token_row = lax.broadcasted_iota(jnp.int32, (tokens, tokens), 0)
+    token_col = lax.broadcasted_iota(jnp.int32, (tokens, tokens), 1)
+    place_column = as_column(place_line, token_row == token_col)
+
+    def inside(position):
+        return (position >= starts) & (position < ends)
+
+    lane = lax.broadcasted_iota(jnp.int32, (1, tokens), 1).astype(jnp.float32)
+    ordered = jnp.sum(jnp.where(place_column == lane, gap, 0.0), axis=0, keepdims=True)
+    divergence = as_column(ordered, inside(lane))
+    scores = as_column(rewards[...], diagonal) - KL_WEIGHT * divergence
+    others = as_column(as_row(scores), as_column(kinds, diagonal) == kinds) - scores
+    advantage = scores - others / (K - 1)
+    advantage_out[...] = as_row(advantage)
+    weight = jnp.sum(jnp.where(inside(place_line), advantage, 0.0), axis=0, keepdims=True)
+
+    down_left[...] = (hidden_ref[...].astype(jnp.float32) * weight).astype(jnp.bfloat16)
+    total[...] = jnp.zeros_like(total)
+
+    def first(step, _):
+        down_buf[:, columns(step)] = dot(down_left[...], slopes[:, columns(step)], NN)
+        copy_out(2, step).start()
+        copy_in(step).wait()
+        total[...] += dot(held[:, columns(step)], slopes[:, columns(step)], NT)
+        return 0
+
+    lax.fori_loop(0, steps, first, 0)
+    grad_hidden = total[...] * weight
+    gate = gate_ref[...]
+    sigmoid = 1.0 / (1.0 + jnp.exp(-gate))
+    gate_left[...] = (
+        grad_hidden * up_ref[...] * sigmoid * (1.0 + gate * (1.0 - sigmoid))
+    ).astype(jnp.bfloat16)
+    up_left[...] = (grad_hidden * gate * sigmoid).astype(jnp.bfloat16)
+
+    def second(step, _):
+        for which, left, buffer in ((0, gate_left, gate_buf), (1, up_left, up_buf)):
+            buffer[:, columns(step)] = dot(left[...], normed[:, columns(step)], NN)
+            copy_out(which, step).start()
+        return 0
+
+    lax.fori_loop(0, steps, second, 0)
+
+    def finish(step, _):
+        for which in range(3):
+            copy_out(which, step).wait()
+        return 0
+
+    lax.fori_loop(0, steps, finish, 0)
+
+
+def backward(blocks, normed, gate, up, hidden, samples, down):
+    tokens, width = normed.shape
+    units = gate.shape[0]
+    chunk = column_chunk(width)
+    vmem = pl.BlockSpec(memory_space=pltpu.VMEM)
+    hbm = pl.BlockSpec(memory_space=pl.ANY)
+    grad = jax.ShapeDtypeStruct((units, width), jnp.float32)
+    count = samples[0].shape[1]
+    left = pltpu.VMEM((units, tokens), jnp.bfloat16)
+    buffer = pltpu.VMEM((units, width), jnp.float32)
+    steps = width // chunk
+    return pl.pallas_call(
+        functools.partial(backward_kernel, len(blocks), chunk),
+        out_shape=(grad, grad, grad, jax.ShapeDtypeStruct((1, count), jnp.float32)),
+        in_specs=[vmem] * (len(blocks) + 8) + [hbm],
+        out_specs=(hbm, hbm, hbm, vmem),
+        scratch_shapes=[
+            pltpu.VMEM((tokens, width), jnp.bfloat16),
+            pltpu.VMEM((units, width), jnp.bfloat16),
+            pltpu.VMEM((units, tokens), jnp.float32),
+            left,
+            left,
+            left,
+            buffer,
+            buffer,
+            buffer,
+            pltpu.SemaphoreType.DMA((steps,)),
+            pltpu.SemaphoreType.DMA((3, steps)),
+        ],
+        compiler_params=pltpu.CompilerParams(vmem_limit_bytes=BACKWARD_VMEM),
+        cost_estimate=pl.CostEstimate(
+            flops=8 * tokens * width * units,
+            bytes_accessed=14 * units * width,
+            transcendentals=tokens * units,
+        ),
+    )(
+        *blocks,
+        normed,
+        gate,
+        up,
+        hidden,
+        *samples,
+        pltpu.with_memory_space_constraint(down, pltpu.HBM),
+    )
 
 
 def local_single(
@@ -80,17 +381,22 @@
     tokens = token_count * masks.size
     member = lax.axis_index("fsdp").astype(jnp.int32)
 
-    normed = normalize(gather_rows(hidden_states, levels), norm_gain)
-
-    def forward(gate_w, up_w, down_w):
-        gate_pre = jnp.dot(normed, gate_w, preferred_element_type=jnp.float32)
-        up_pre = jnp.dot(normed, up_w, preferred_element_type=jnp.float32)
-        hidden = (jax.nn.silu(gate_pre) * up_pre).astype(jnp.bfloat16)
-        return gate_pre, up_pre, hidden, jnp.dot(hidden, down_w, preferred_element_type=jnp.float32)
-
-    gate_pre, up_pre, hidden, pol_part = forward(pol_gate_w, pol_up_w, pol_down_w)
-    _, _, _, ref_part = forward(ref_gate_w, ref_up_w, ref_down_w)
-    sums = scatter_rows(jnp.concatenate([pol_part, ref_part], axis=1), levels)
+    blocks, (ref_weights, pol_weights) = gather_blocks(
+        hidden_states,
+        levels,
+        (
+            fetch([ref_gate_w.T, ref_up_w.T, ref_down_w]),
+            fetch([pol_gate_w.T, pol_up_w.T, pol_down_w]),
+        ),
+    )
+    normed, ref_sent, ref_kept = forward_reference(blocks, norm_gain[None, :], ref_weights)
+    gate, up, hidden, pol_sent, pol_kept = forward_policy(normed, pol_weights)
+
+    def reduce_rows(sent, kept):
+        return scatter_rows(kept + swap(sent, levels[0][0]).astype(jnp.float32), levels[1:])
+
+    ref_sums = reduce_rows(ref_sent, ref_kept)
+    pol_sums = reduce_rows(pol_sent, pol_kept)
 
     states = hidden_states.astype(jnp.float32)
     columns = jnp.arange(width, dtype=jnp.int32)
@@ -101,56 +407,29 @@
         log_total = row_peak + jnp.log(jnp.sum(jnp.exp(logits - row_peak[:, None]), axis=1))
         return jnp.sum(jnp.where(chosen, logits, 0.0), axis=1) - log_total, log_total
 
-    logits = states + sums[:, :width]
+    logits = states + pol_sums
     pol_lp, log_total = token_logprob(logits)
-    ref_lp, _ = token_logprob(states + sums[:, width:])
+    ref_lp, _ = token_logprob(states + ref_sums)
     slopes = jnp.exp(logits - log_total[:, None]) - chosen.astype(jnp.float32)
     extra = jnp.stack(split_float(pol_lp - ref_lp), axis=1)
     extra = jnp.pad(extra, ((0, 0), (0, LANES - PIECES)))
-    sent = jnp.concatenate([slopes, extra], axis=1).astype(jnp.bfloat16)
-    received = gather_rows(sent, levels)
-    slopes_all = received[:, :width]
-    gap = jnp.sum(received[:, width : width + PIECES].astype(jnp.float32), axis=1)
-
-    sample_ends = jnp.cumsum(sample_lengths[0])
-    sample_starts = sample_ends - sample_lengths[0]
-
-    def inside_of(position):
-        return (position[:, None] >= sample_starts[None, :]) & (
-            position[:, None] < sample_ends[None, :]
-        )
+    payload = jnp.concatenate([slopes, extra], axis=1).astype(jnp.bfloat16)
 
     row_place = (
         (member ^ jnp.asarray(np.repeat(masks, token_count))) * token_count
         + jnp.asarray(np.tile(np.arange(token_count, dtype=np.int32), masks.size))
     )
-    place = jnp.arange(tokens, dtype=jnp.int32)
-    ordered = jnp.sum(jnp.where(place[:, None] == row_place[None, :], gap[None, :], 0.0), axis=1)
-    divergence = jnp.sum(jnp.where(inside_of(place), ordered[:, None], 0.0), axis=0)
-    scores = rewards[0] - KL_WEIGHT * divergence
-    same_prompt = prompt_index[0][:, None] == prompt_index[0][None, :]
-    others = jnp.sum(jnp.where(same_prompt, scores[None, :], 0.0), axis=1) - scores
-    advantage = scores - others / (K - 1)
-    weight = jnp.sum(jnp.where(inside_of(row_place), advantage[None, :], 0.0), axis=1)
-
-    weighted = (hidden.astype(jnp.float32) * weight[:, None]).astype(jnp.bfloat16)
-    rows_first = (((0,), (0,)), ((), ()))
-    grad_down = lax.dot_general(
-        weighted, slopes_all, rows_first, preferred_element_type=jnp.float32
-    )
-    grad_hidden = weight[:, None] * lax.dot_general(
-        slopes_all, pol_down_w, (((1,), (1,)), ((), ())), preferred_element_type=jnp.float32
-    )
-    sigmoid_gate = jax.nn.sigmoid(gate_pre)
-    grad_gate_pre = grad_hidden * up_pre * sigmoid_gate * (1.0 + gate_pre * (1.0 - sigmoid_gate))
-    grad_up_pre = grad_hidden * gate_pre * sigmoid_gate
-    grad_gate = lax.dot_general(
-        normed, grad_gate_pre.astype(jnp.bfloat16), rows_first, preferred_element_type=jnp.float32
-    )
-    grad_up = lax.dot_general(
-        normed, grad_up_pre.astype(jnp.bfloat16), rows_first, preferred_element_type=jnp.float32
-    )
-    return grad_gate, grad_up, grad_down, advantage[None, :]
+    slope_blocks, _ = gather_blocks(payload, levels)
+    grad_gate, grad_up, grad_down, advantage = backward(
+        slope_blocks,
+        normed,
+        gate,
+        up,
+        hidden,
+        (sample_lengths, prompt_index, rewards, row_place[None, :]),
+        pol_down_w,
+    )
+    return grad_gate.T, grad_up.T, grad_down, advantage
 
 
 def combined_all(part, axis, combine):

time: 114 us -> 83.8 us (0.74)
  matrix products: 31.9 us -> 0 us
  Pallas kernels: 0 us -> 26.6 us
  waiting for transfers between devices: 37.6 us -> 19 us
  starting transfers between devices: 25.6 us -> 35.5 us
  local copies, waits for them, and re-layouts: 9.21 us -> 0.28 us
  other arithmetic: 8.1 us -> 1.27 us
    dot_general x9 -> x0, matrix products: 31.9 us -> none  [the longest x2 8.38 us: forward(): jnp.dot(hidden, down_w, preferred_element_type=jnp.float32)]
    pallas_call x0 -> x5, Pallas kernels: none -> 26.6 us  [the longest x1 10.7 us: backward(): pl.pallas_call(functools.partial(backward_kernel, len(blocks), chunk), ou...]
    ppermute x21 -> x34, waiting for transfers between devices: 37.6 us -> 19 us  [swap(): return lax.ppermute(values, 'fsdp', [(i, i ^ mask) for i in range(members)])]
    ppermute x21 -> x34, starting transfers between devices: 25.6 us -> 35.5 us  [swap(): return lax.ppermute(values, 'fsdp', [(i, i ^ mask) for i in range(members)])]
    concatenate x4 -> x0, local copies, waits for them, and re-layouts: 7.88 us -> none  [gather_rows(): jnp.concatenate([rows] + [swap(rows, mask) for mask in level], axis=0)]
    another operation x7 -> x6, other arithmetic: 2.18 us -> 0.49 us
    reduce_sum x7 -> x1, other arithmetic: 1.97 us -> 0.29 us  [token_logprob(): jnp.sum(jnp.exp(logits - row_peak[:, None]), axis=1)]
  transfers between devices with their start and end apart: 21 -> 34, of which waited for: 17 -> 16; matrix products, arithmetic and copies ran while one was open for 2% -> 1% of each run, Pallas kernels for 0% -> 15%
where the time goes in v2:
time: 83.8 us; the launch traced here: 83.7 us
  starting transfers between devices  35.5 us (42%)
  Pallas kernels  26.6 us (32%)
  waiting for transfers between devices  19 us (23%)
  other arithmetic  1.27 us (2%)
  between operations  0.93 us (1%)
    ppermute x34, starting transfers between devices, swap(): return lax.ppermute(values, 'fsdp', [(i, i ^ mask) for i in range(members)])  35.5 us
    ppermute x34, waiting for transfers between devices, swap(): return lax.ppermute(values, 'fsdp', [(i, i ^ mask) for i in range(members)])  19 us
    pallas_call x1, Pallas kernels, backward(): pl.pallas_call(functools.partial(backward_kernel, len(blocks), chunk), ou...  10.7 us
    pallas_call x2, Pallas kernels, fetch(): pl.pallas_call(fetch_kernel, out_shape=[jax.ShapeDtypeStruct(w.shape, w.d...  8.69 us
    pallas_call x2, Pallas kernels, forward_call(): pl.pallas_call(kernel, out_shape=shapes, in_specs=[vmem] * (len(operands)...  7.26 us
  transfers between devices with their start and end apart: 34, of which 16 were waited for; matrix products, arithmetic and copies ran while one was open for 1% of the time, Pallas kernels for 15%

profile of v2, /device:TPU:0, one launch (start us, length us, event | category | flops | bytes accessed | tf_op | source)
XLA Modules:
  0.0 83.7 jit_solution(15900803827784355723)
XLA Ops:
  0.6 3.1 %collective-permute-start = (bf16[4,4096]{1,0:T(4,128)(2,1)}, bf16[4,4096]{1,0:T(4,128)(2,1)S(1)}, u32[]{:S(2)}, u32[]{:S(2)}) collective-permute-start(bf16[4,4096]{1,0:T(4,128)(2,1)} %param.14), channel_id=1, source_target_pairs={{0,8},{1,9},{2,10},{3,11},{4,12},{5,13},{6,14},{7,15},{8,0},{9,1},... | collective-permute-start | bytes 98312 | tf_op jit(solution)/shard_map/ppermute | solution.py:34
  3.7 2.6 %collective-permute-start.1 = (bf16[4,4096]{1,0:T(4,128)(2,1)}, bf16[4,4096]{1,0:T(4,128)(2,1)S(1)}, u32[]{:S(2)}, u32[]{:S(2)}) collective-permute-start(bf16[4,4096]{1,0:T(4,128)(2,1)} %param.14), channel_id=1, source_target_pairs={{0,16},{1,17},{2,18},{3,19},{4,20},{5,21},{6,22},{7,23},{8,24},{9,... | collective-permute-start | bytes 98312 | tf_op jit(solution)/shard_map/ppermute | solution.py:34
  6.3 4.3 %shard_map.165 = (bf16[462,4096]{1,0:T(8,128)(2,1)S(1)}, bf16[462,4096]{1,0:T(8,128)(2,1)S(1)}, bf16[462,4096]{1,0:T(8,128)(2,1)S(1)}) custom-call(bf16[462,4096]{1,0:T(8,128)(2,1)} %bitcast.12, bf16[462,4096]{1,0:T(8,128)(2,1)} %bitcast.13, bf16[462,4096]{1,0:T(8,128)(2,1)} %refs_2_.2), custom_call_target="tpu_custom_call" | custom-call | bytes 11354112 | tf_op jit(solution)/shard_map/pallas_call | solution.py:111
  10.7 1.5 %collective-permute-done.2 = bf16[4,4096]{1,0:T(4,128)(2,1)S(1)} collective-permute-done((bf16[4,4096]{1,0:T(4,128)(2,1)}, bf16[4,4096]{1,0:T(4,128)(2,1)S(1)}, u32[]{:S(2)}, u32[]{:S(2)}) %collective-permute-start.2) | collective-permute-done | bytes 32800 | tf_op jit(solution)/shard_map/ppermute | solution.py:34
  12.3 1.6 %collective-permute-start.3 = (bf16[16,4096]{1,0:T(8,128)(2,1)S(1)}, bf16[16,4096]{1,0:T(8,128)(2,1)S(1)}, u32[]{:S(2)}, u32[]{:S(2)}) collective-permute-start(bf16[16,4096]{1,0:T(8,128)(2,1)S(1)} %pad_maximum_fusion.1.refs_0_), channel_id=1, source_target_pairs={{0,2},{1,3},{2,0},{3,1},{4,6},{5,7},{6,4},{7,5},{8,10},{9,11},{10,... | collective-permute-start | bytes 393224 | tf_op jit(solution)/shard_map/ppermute | solution.py:34
  13.9 1.5 %collective-permute-start.4 = (bf16[16,4096]{1,0:T(8,128)(2,1)S(1)}, bf16[16,4096]{1,0:T(8,128)(2,1)S(1)}, u32[]{:S(2)}, u32[]{:S(2)}) collective-permute-start(bf16[16,4096]{1,0:T(8,128)(2,1)S(1)} %pad_maximum_fusion.1.refs_0_), channel_id=1, source_target_pairs={{0,4},{1,5},{2,6},{3,7},{4,0},{5,1},{6,2},{7,3},{8,12},{9,13},{10,... | collective-permute-start | bytes 393224 | tf_op jit(solution)/shard_map/ppermute | solution.py:34
  15.9 4.3 %shard_map.166 = (bf16[462,4096]{1,0:T(8,128)(2,1)S(1)}, bf16[462,4096]{1,0:T(8,128)(2,1)S(1)}, bf16[462,4096]{1,0:T(8,128)(2,1)S(1)}) custom-call(bf16[462,4096]{1,0:T(8,128)(2,1)} %bitcast.14, bf16[462,4096]{1,0:T(8,128)(2,1)} %bitcast.15, bf16[462,4096]{1,0:T(8,128)(2,1)} %refs_16_.1), custom_call_target="tpu_custom_call" | custom-call | bytes 11354112 | tf_op jit(solution)/shard_map/pallas_call | solution.py:111
  20.4 0.9 %collective-permute-done.5.refs_3_ = bf16[16,4096]{1,0:T(8,128)(2,1)S(1)} collective-permute-done((bf16[16,4096]{1,0:T(8,128)(2,1)S(1)}, bf16[16,4096]{1,0:T(8,128)(2,1)S(1)}, u32[]{:S(2)}, u32[]{:S(2)}) %collective-permute-start.5) | collective-permute-done | bytes 131104 | tf_op jit(solution)/shard_map/ppermute | solution.py:34
  23.2 3.8 %shard_map.167 = (bf16[128,4096]{1,0:T(8,128)(2,1)S(1)}, bf16[64,4096]{1,0:T(8,128)(2,1)S(1)}, f32[64,4096]{1,0:T(8,128)S(1)}) custom-call(bf16[16,4096]{1,0:T(8,128)(2,1)S(1)} %pad_maximum_fusion.1.refs_0_, bf16[16,4096]{1,0:T(8,128)(2,1)S(1)} %collective-permute-done.3.refs_1_, bf16[16,4096]{1,0:T(8,128)(2,1)S(1)} %collective-permute-done.4.refs_2_, ...), custom_call_target="tpu_custom_call" | custom-call | flops 1453326336 | bytes 11354112 | tf_op jit(solution)/shard_map/pallas_call | solution.py:173
  27.2 3.5 %shard_map.168 = (f32[462,128]{1,0:T(8,128)S(1)}, f32[462,128]{1,0:T(8,128)S(1)}, bf16[462,128]{1,0:T(8,128)(2,1)S(1)}, bf16[64,4096]{1,0:T(8,128)(2,1)S(1)}, f32[64,4096]{1,0:T(8,128)S(1)}) custom-call(bf16[128,4096]{1,0:T(8,128)(2,1)S(1)} %get-tuple-element.49.normed.refs_8_, bf16[462,4096]{1,0:T(8,128)(2,1)S(1)} %get-tuple-element.50.refs_0_, ...), custom_call_target="tpu_custom_call" | custom-call | flops 1453326336 | bytes 11354112 | tf_op jit(solution)/shard_map/pallas_call | solution.py:173
  31.3 0.9 %collective-permute-start.18 = (bf16[16,4096]{1,0:T(8,128)(2,1)S(1)}, bf16[16,4096]{1,0:T(8,128)(2,1)S(1)}, u32[]{:S(2)}, u32[]{:S(2)}) collective-permute-start(bf16[16,4096]{1,0:T(8,128)(2,1)S(1)} %get-tuple-element.85), channel_id=1, source_target_pairs={{0,2},{1,3},{2,0},{3,1},{4,6},{5,7},{6,4},{7,5},{8,10},{9,11},{10,... | collective-permute-start | bytes 393224 | tf_op jit(solution)/shard_map/ppermute | solution.py:34
  32.2 1.5 %collective-permute-start.19 = (bf16[16,4096]{1,0:T(8,128)(2,1)S(1)}, bf16[16,4096]{1,0:T(8,128)(2,1)S(1)}, u32[]{:S(2)}, u32[]{:S(2)}) collective-permute-start(bf16[16,4096]{1,0:T(8,128)(2,1)S(1)} %get-tuple-element.87), channel_id=1, source_target_pairs={{0,4},{1,5},{2,6},{3,7},{4,0},{5,1},{6,2},{7,3},{8,12},{9,13},{10,... | collective-permute-start | bytes 393224 | tf_op jit(solution)/shard_map/ppermute | solution.py:34
  33.7 1.2 %collective-permute-start.20 = (bf16[16,4096]{1,0:T(8,128)(2,1)S(1)}, bf16[16,4096]{1,0:T(8,128)(2,1)S(1)}, u32[]{:S(2)}, u32[]{:S(2)}) collective-permute-start(bf16[16,4096]{1,0:T(8,128)(2,1)S(1)} %get-tuple-element.86), channel_id=1, source_target_pairs={{0,6},{1,7},{2,4},{3,5},{4,2},{5,3},{6,0},{7,1},{8,14},{9,15},{10,... | collective-permute-start | bytes 393224 | tf_op jit(solution)/shard_map/ppermute | solution.py:34
  35.0 0.9 %collective-permute-start.11 = (bf16[16,4096]{1,0:T(8,128)(2,1)S(1)}, bf16[16,4096]{1,0:T(8,128)(2,1)S(1)}, u32[]{:S(2)}, u32[]{:S(2)}) collective-permute-start(bf16[16,4096]{1,0:T(8,128)(2,1)S(1)} %get-tuple-element.82), channel_id=1, source_target_pairs={{0,2},{1,3},{2,0},{3,1},{4,6},{5,7},{6,4},{7,5},{8,10},{9,11},{10,... | collective-permute-start | bytes 393224 | tf_op jit(solution)/shard_map/ppermute | solution.py:34
  35.9 1.5 %collective-permute-start.12 = (bf16[16,4096]{1,0:T(8,128)(2,1)S(1)}, bf16[16,4096]{1,0:T(8,128)(2,1)S(1)}, u32[]{:S(2)}, u32[]{:S(2)}) collective-permute-start(bf16[16,4096]{1,0:T(8,128)(2,1)S(1)} %get-tuple-element.84), channel_id=1, source_target_pairs={{0,4},{1,5},{2,6},{3,7},{4,0},{5,1},{6,2},{7,3},{8,12},{9,13},{10,... | collective-permute-start | bytes 393224 | tf_op jit(solution)/shard_map/ppermute | solution.py:34
  37.7 1.7 %collective-permute-start.13 = (bf16[16,4096]{1,0:T(8,128)(2,1)S(1)}, bf16[16,4096]{1,0:T(8,128)(2,1)S(1)}, u32[]{:S(2)}, u32[]{:S(2)}) collective-permute-start(bf16[16,4096]{1,0:T(8,128)(2,1)S(1)} %get-tuple-element.83), channel_id=1, source_target_pairs={{0,6},{1,7},{2,4},{3,5},{4,2},{5,3},{6,0},{7,1},{8,14},{9,15},{10,... | collective-permute-start | bytes 393224 | tf_op jit(solution)/shard_map/ppermute | solution.py:34
  39.5 1.0 %collective-permute-done.19 = bf16[16,4096]{1,0:T(8,128)(2,1)S(1)} collective-permute-done((bf16[16,4096]{1,0:T(8,128)(2,1)S(1)}, bf16[16,4096]{1,0:T(8,128)(2,1)S(1)}, u32[]{:S(2)}, u32[]{:S(2)}) %collective-permute-start.19) | collective-permute-done | bytes 131104 | tf_op jit(solution)/shard_map/ppermute | solution.py:34
  41.2 3.3 %collective-permute-start.22 = (bf16[4,4096]{1,0:T(4,128)(2,1)S(1)}, bf16[4,4096]{1,0:T(4,128)(2,1)S(1)}, u32[]{:S(2)}, u32[]{:S(2)}) collective-permute-start(bf16[4,4096]{1,0:T(4,128)(2,1)S(1)} %get-tuple-element.93), channel_id=1, source_target_pairs={{0,16},{1,17},{2,18},{3,19},{4,20},{5,21},{6,22},{7,23},{8,24},{9,... | collective-permute-start | bytes 98312 | tf_op jit(solution)/shard_map/ppermute | solution.py:34
  44.4 1.6 %collective-permute-start.23 = (bf16[4,4096]{1,0:T(4,128)(2,1)S(1)}, bf16[4,4096]{1,0:T(4,128)(2,1)S(1)}, u32[]{:S(2)}, u32[]{:S(2)}) collective-permute-start(bf16[4,4096]{1,0:T(4,128)(2,1)S(1)} %get-tuple-element.92), channel_id=1, source_target_pairs={{0,24},{1,25},{2,26},{3,27},{4,28},{5,29},{6,30},{7,31},{8,16},{9,... | collective-permute-start | bytes 98312 | tf_op jit(solution)/shard_map/ppermute | solution.py:34
  46.3 3.0 %collective-permute-start.15 = (bf16[4,4096]{1,0:T(4,128)(2,1)S(1)}, bf16[4,4096]{1,0:T(4,128)(2,1)S(1)}, u32[]{:S(2)}, u32[]{:S(2)}) collective-permute-start(bf16[4,4096]{1,0:T(4,128)(2,1)S(1)} %get-tuple-element.90), channel_id=1, source_target_pairs={{0,16},{1,17},{2,18},{3,19},{4,20},{5,21},{6,22},{7,23},{8,24},{9,... | collective-permute-start | bytes 98312 | tf_op jit(solution)/shard_map/ppermute | solution.py:34
  49.3 1.3 %collective-permute-start.16 = (bf16[4,4096]{1,0:T(4,128)(2,1)S(1)}, bf16[4,4096]{1,0:T(4,128)(2,1)S(1)}, u32[]{:S(2)}, u32[]{:S(2)}) collective-permute-start(bf16[4,4096]{1,0:T(4,128)(2,1)S(1)} %get-tuple-element.89), channel_id=1, source_target_pairs={{0,24},{1,25},{2,26},{3,27},{4,28},{5,29},{6,30},{7,31},{8,16},{9,... | collective-permute-start | bytes 98312 | tf_op jit(solution)/shard_map/ppermute | solution.py:34
  51.3 3.7 %collective-permute-done.16 = bf16[4,4096]{1,0:T(4,128)(2,1)S(1)} collective-permute-done((bf16[4,4096]{1,0:T(4,128)(2,1)S(1)}, bf16[4,4096]{1,0:T(4,128)(2,1)S(1)}, u32[]{:S(2)}, u32[]{:S(2)}) %collective-permute-start.16) | collective-permute-done | bytes 32800 | tf_op jit(solution)/shard_map/ppermute | solution.py:34
  55.9 1.9 %collective-permute-start.25 = (bf16[4,4224]{1,0:T(4,128)(2,1)S(1)}, bf16[4,4224]{1,0:T(4,128)(2,1)S(1)}, u32[]{:S(2)}, u32[]{:S(2)}) collective-permute-start(bf16[4,4224]{1,0:T(4,128)(2,1)S(1)} %pad_maximum_fusion.2), channel_id=1, source_target_pairs={{0,16},{1,17},{2,18},{3,19},{4,20},{5,21},{6,22},{7,23},{8,24},{9,... | collective-permute-start | bytes 101384 | tf_op jit(solution)/shard_map/ppermute | solution.py:34
  57.8 2.5 %collective-permute-start.26 = (bf16[4,4224]{1,0:T(4,128)(2,1)S(1)}, bf16[4,4224]{1,0:T(4,128)(2,1)S(1)}, u32[]{:S(2)}, u32[]{:S(2)}) collective-permute-start(bf16[4,4224]{1,0:T(4,128)(2,1)S(1)} %pad_maximum_fusion.2), channel_id=1, source_target_pairs={{0,24},{1,25},{2,26},{3,27},{4,28},{5,29},{6,30},{7,31},{8,16},{9,... | collective-permute-start | bytes 101384 | tf_op jit(solution)/shard_map/ppermute | solution.py:34
  60.8 2.7 %collective-permute-done.26 = bf16[4,4224]{1,0:T(4,128)(2,1)S(1)} collective-permute-done((bf16[4,4224]{1,0:T(4,128)(2,1)S(1)}, bf16[4,4224]{1,0:T(4,128)(2,1)S(1)}, u32[]{:S(2)}, u32[]{:S(2)}) %collective-permute-start.26) | collective-permute-done | bytes 33824 | tf_op jit(solution)/shard_map/ppermute | solution.py:34
  63.6 1.3 %collective-permute-start.27 = (bf16[16,4224]{1,0:T(8,128)(2,1)S(1)}, bf16[16,4224]{1,0:T(8,128)(2,1)S(1)}, u32[]{:S(2)}, u32[]{:S(2)}) collective-permute-start(bf16[16,4224]{1,0:T(8,128)(2,1)S(1)} %pad_maximum_fusion.refs_0_), channel_id=1, source_target_pairs={{0,2},{1,3},{2,0},{3,1},{4,6},{5,7},{6,4},{7,5},{8,10},{9,11},{10,... | collective-permute-start | bytes 405512 | tf_op jit(solution)/shard_map/ppermute | solution.py:34
  65.7 1.5 %collective-permute-start.29 = (bf16[16,4224]{1,0:T(8,128)(2,1)S(1)}, bf16[16,4224]{1,0:T(8,128)(2,1)S(1)}, u32[]{:S(2)}, u32[]{:S(2)}) collective-permute-start(bf16[16,4224]{1,0:T(8,128)(2,1)S(1)} %pad_maximum_fusion.refs_0_), channel_id=1, source_target_pairs={{0,6},{1,7},{2,4},{3,5},{4,2},{5,3},{6,0},{7,1},{8,14},{9,15},{10,... | collective-permute-start | bytes 405512 | tf_op jit(solution)/shard_map/ppermute | solution.py:34
  67.2 1.5 %collective-permute-done.27.refs_1_ = bf16[16,4224]{1,0:T(8,128)(2,1)S(1)} collective-permute-done((bf16[16,4224]{1,0:T(8,128)(2,1)S(1)}, bf16[16,4224]{1,0:T(8,128)(2,1)S(1)}, u32[]{:S(2)}, u32[]{:S(2)}) %collective-permute-start.27) | collective-permute-done | bytes 135200 | tf_op jit(solution)/shard_map/ppermute | solution.py:34
  68.7 1.3 %collective-permute-done.28.refs_2_ = bf16[16,4224]{1,0:T(8,128)(2,1)S(1)} collective-permute-done((bf16[16,4224]{1,0:T(8,128)(2,1)S(1)}, bf16[16,4224]{1,0:T(8,128)(2,1)S(1)}, u32[]{:S(2)}, u32[]{:S(2)}) %collective-permute-start.28) | collective-permute-done | bytes 135200 | tf_op jit(solution)/shard_map/ppermute | solution.py:34
  70.0 1.7 %collective-permute-done.29.refs_3_ = bf16[16,4224]{1,0:T(8,128)(2,1)S(1)} collective-permute-done((bf16[16,4224]{1,0:T(8,128)(2,1)S(1)}, bf16[16,4224]{1,0:T(8,128)(2,1)S(1)}, u32[]{:S(2)}, u32[]{:S(2)}) %collective-permute-start.29) | collective-permute-done | bytes 135200 | tf_op jit(solution)/shard_map/ppermute | solution.py:34
  71.7 1.3 %collective-permute-done.33.refs_7_ = bf16[16,4224]{1,0:T(8,128)(2,1)S(1)} collective-permute-done((bf16[16,4224]{1,0:T(8,128)(2,1)S(1)}, bf16[16,4224]{1,0:T(8,128)(2,1)S(1)}, u32[]{:S(2)}, u32[]{:S(2)}) %collective-permute-start.33) | collective-permute-done | bytes 135200 | tf_op jit(solution)/shard_map/ppermute | solution.py:34
  73.0 10.7 %shard_map.169 = (f32[462,4096]{1,0:T(8,128)}, f32[462,4096]{1,0:T(8,128)}, f32[462,4096]{1,0:T(8,128)}, f32[1,32]{1,0:T(1,128)}) custom-call(bf16[16,4224]{1,0:T(8,128)(2,1)S(1)} %pad_maximum_fusion.refs_0_, bf16[16,4224]{1,0:T(8,128)(2,1)S(1)} %collective-permute-done.27.refs_1_, bf16[16,4224]{1,0:T(8,128)(2,1)S(1)} %collective-permute-done.28.refs_2_, ...), custom_call_target="tpu_custom_call" | custom-call | flops 1937768448 | bytes 26492928 | tf_op jit(solution)/shard_map/pallas_call | solution.py:329
  (76 shorter events, 7.7 us)
Async XLA Ops:
  0.6 10.1 %collective-permute-start = (bf16[4,4096]{1,0:T(4,128)(2,1)}, bf16[4,4096]{1,0:T(4,128)(2,1)S(1)}, u32[]{:S(2)}, u32[]{:S(2)}) collective-permute-start(bf16[4,4096]{1,0:T(4,128)(2,1)} %param.14), channel_id=1, source_target_pairs={{0,8},{1,9},{2,10},{3,11},{4,12},{5,13},{6,14},{7,15},{8,0},{9,1},... | collective-permute-start | bytes 98312 | tf_op jit(solution)/shard_map/ppermute | solution.py:34
  3.7 7.0 %collective-permute-start.1 = (bf16[4,4096]{1,0:T(4,128)(2,1)}, bf16[4,4096]{1,0:T(4,128)(2,1)S(1)}, u32[]{:S(2)}, u32[]{:S(2)}) collective-permute-start(bf16[4,4096]{1,0:T(4,128)(2,1)} %param.14), channel_id=1, source_target_pairs={{0,16},{1,17},{2,18},{3,19},{4,20},{5,21},{6,22},{7,23},{8,24},{9,... | collective-permute-start | bytes 98312 | tf_op jit(solution)/shard_map/ppermute | solution.py:34
  6.3 5.9 %collective-permute-start.2 = (bf16[4,4096]{1,0:T(4,128)(2,1)}, bf16[4,4096]{1,0:T(4,128)(2,1)S(1)}, u32[]{:S(2)}, u32[]{:S(2)}) collective-permute-start(bf16[4,4096]{1,0:T(4,128)(2,1)} %param.14), channel_id=1, source_target_pairs={{0,24},{1,25},{2,26},{3,27},{4,28},{5,29},{6,30},{7,31},{8,16},{9,... | collective-permute-start | bytes 98312 | tf_op jit(solution)/shard_map/ppermute | solution.py:34
  12.3 8.0 %collective-permute-start.3 = (bf16[16,4096]{1,0:T(8,128)(2,1)S(1)}, bf16[16,4096]{1,0:T(8,128)(2,1)S(1)}, u32[]{:S(2)}, u32[]{:S(2)}) collective-permute-start(bf16[16,4096]{1,0:T(8,128)(2,1)S(1)} %pad_maximum_fusion.1.refs_0_), channel_id=1, source_target_pairs={{0,2},{1,3},{2,0},{3,1},{4,6},{5,7},{6,4},{7,5},{8,10},{9,11},{10,... | collective-permute-start | bytes 393224 | tf_op jit(solution)/shard_map/ppermute | solution.py:34
  13.9 6.4 %collective-permute-start.4 = (bf16[16,4096]{1,0:T(8,128)(2,1)S(1)}, bf16[16,4096]{1,0:T(8,128)(2,1)S(1)}, u32[]{:S(2)}, u32[]{:S(2)}) collective-permute-start(bf16[16,4096]{1,0:T(8,128)(2,1)S(1)} %pad_maximum_fusion.1.refs_0_), channel_id=1, source_target_pairs={{0,4},{1,5},{2,6},{3,7},{4,0},{5,1},{6,2},{7,3},{8,12},{9,13},{10,... | collective-permute-start | bytes 393224 | tf_op jit(solution)/shard_map/ppermute | solution.py:34
  15.4 5.9 %collective-permute-start.5 = (bf16[16,4096]{1,0:T(8,128)(2,1)S(1)}, bf16[16,4096]{1,0:T(8,128)(2,1)S(1)}, u32[]{:S(2)}, u32[]{:S(2)}) collective-permute-start(bf16[16,4096]{1,0:T(8,128)(2,1)S(1)} %pad_maximum_fusion.1.refs_0_), channel_id=1, source_target_pairs={{0,6},{1,7},{2,4},{3,5},{4,2},{5,3},{6,0},{7,1},{8,14},{9,15},{10,... | collective-permute-start | bytes 393224 | tf_op jit(solution)/shard_map/ppermute | solution.py:34
  20.3 1.6 %collective-permute-start.6 = (bf16[16,4096]{1,0:T(8,128)(2,1)S(1)}, bf16[16,4096]{1,0:T(8,128)(2,1)S(1)}, u32[]{:S(2)}, u32[]{:S(2)}) collective-permute-start(bf16[16,4096]{1,0:T(8,128)(2,1)S(1)} %pad_maximum_fusion.1.refs_0_), channel_id=1, source_target_pairs={{0,1},{1,0},{2,3},{3,2},{4,5},{5,4},{6,7},{7,6},{8,9},{9,8},{10,11... | collective-permute-start | bytes 393224 | tf_op jit(solution)/shard_map/ppermute | solution.py:34
  21.3 1.5 %collective-permute-start.8 = (bf16[16,4096]{1,0:T(8,128)(2,1)S(1)}, bf16[16,4096]{1,0:T(8,128)(2,1)S(1)}, u32[]{:S(2)}, u32[]{:S(2)}) collective-permute-start(bf16[16,4096]{1,0:T(8,128)(2,1)S(1)} %collective-permute-done.4.refs_2_), channel_id=1, source_target_pairs={{0,1},{1,0},{2,3},{3,2},{4,5},{5,4},{6,7},{7,6},{8,9},{9,8},{10,11... | collective-permute-start | bytes 393224 | tf_op jit(solution)/shard_map/ppermute | solution.py:34
  26.9 4.1 %collective-permute-start.17 = (bf16[64,4096]{1,0:T(8,128)(2,1)S(1)}, bf16[64,4096]{1,0:T(8,128)(2,1)S(1)}, u32[]{:S(2)}, u32[]{:S(2)}) collective-permute-start(bf16[64,4096]{1,0:T(8,128)(2,1)S(1)} %get-tuple-element.56), channel_id=1, source_target_pairs={{0,1},{1,0},{2,3},{3,2},{4,5},{5,4},{6,7},{7,6},{8,9},{9,8},{10,11... | collective-permute-start | bytes 1572872 | tf_op jit(solution)/shard_map/ppermute | solution.py:34
  30.7 4.2 %collective-permute-start.10 = (bf16[64,4096]{1,0:T(8,128)(2,1)S(1)}, bf16[64,4096]{1,0:T(8,128)(2,1)S(1)}, u32[]{:S(2)}, u32[]{:S(2)}) collective-permute-start(bf16[64,4096]{1,0:T(8,128)(2,1)S(1)} %get-tuple-element.54), channel_id=1, source_target_pairs={{0,1},{1,0},{2,3},{3,2},{4,5},{5,4},{6,7},{7,6},{8,9},{9,8},{10,11... | collective-permute-start | bytes 1572872 | tf_op jit(solution)/shard_map/ppermute | solution.py:34
  31.3 6.4 %collective-permute-start.18 = (bf16[16,4096]{1,0:T(8,128)(2,1)S(1)}, bf16[16,4096]{1,0:T(8,128)(2,1)S(1)}, u32[]{:S(2)}, u32[]{:S(2)}) collective-permute-start(bf16[16,4096]{1,0:T(8,128)(2,1)S(1)} %get-tuple-element.85), channel_id=1, source_target_pairs={{0,2},{1,3},{2,0},{3,1},{4,6},{5,7},{6,4},{7,5},{8,10},{9,11},{10,... | collective-permute-start | bytes 393224 | tf_op jit(solution)/shard_map/ppermute | solution.py:34
  32.2 8.3 %collective-permute-start.19 = (bf16[16,4096]{1,0:T(8,128)(2,1)S(1)}, bf16[16,4096]{1,0:T(8,128)(2,1)S(1)}, u32[]{:S(2)}, u32[]{:S(2)}) collective-permute-start(bf16[16,4096]{1,0:T(8,128)(2,1)S(1)} %get-tuple-element.87), channel_id=1, source_target_pairs={{0,4},{1,5},{2,6},{3,7},{4,0},{5,1},{6,2},{7,3},{8,12},{9,13},{10,... | collective-permute-start | bytes 393224 | tf_op jit(solution)/shard_map/ppermute | solution.py:34
  33.7 7.3 %collective-permute-start.20 = (bf16[16,4096]{1,0:T(8,128)(2,1)S(1)}, bf16[16,4096]{1,0:T(8,128)(2,1)S(1)}, u32[]{:S(2)}, u32[]{:S(2)}) collective-permute-start(bf16[16,4096]{1,0:T(8,128)(2,1)S(1)} %get-tuple-element.86), channel_id=1, source_target_pairs={{0,6},{1,7},{2,4},{3,5},{4,2},{5,3},{6,0},{7,1},{8,14},{9,15},{10,... | collective-permute-start | bytes 393224 | tf_op jit(solution)/shard_map/ppermute | solution.py:34
  35.0 9.4 %collective-permute-start.11 = (bf16[16,4096]{1,0:T(8,128)(2,1)S(1)}, bf16[16,4096]{1,0:T(8,128)(2,1)S(1)}, u32[]{:S(2)}, u32[]{:S(2)}) collective-permute-start(bf16[16,4096]{1,0:T(8,128)(2,1)S(1)} %get-tuple-element.82), channel_id=1, source_target_pairs={{0,2},{1,3},{2,0},{3,1},{4,6},{5,7},{6,4},{7,5},{8,10},{9,11},{10,... | collective-permute-start | bytes 393224 | tf_op jit(solution)/shard_map/ppermute | solution.py:34
  35.9 10.1 %collective-permute-start.12 = (bf16[16,4096]{1,0:T(8,128)(2,1)S(1)}, bf16[16,4096]{1,0:T(8,128)(2,1)S(1)}, u32[]{:S(2)}, u32[]{:S(2)}) collective-permute-start(bf16[16,4096]{1,0:T(8,128)(2,1)S(1)} %get-tuple-element.84), channel_id=1, source_target_pairs={{0,4},{1,5},{2,6},{3,7},{4,0},{5,1},{6,2},{7,3},{8,12},{9,13},{10,... | collective-permute-start | bytes 393224 | tf_op jit(solution)/shard_map/ppermute | solution.py:34
  37.7 8.3 %collective-permute-start.13 = (bf16[16,4096]{1,0:T(8,128)(2,1)S(1)}, bf16[16,4096]{1,0:T(8,128)(2,1)S(1)}, u32[]{:S(2)}, u32[]{:S(2)}) collective-permute-start(bf16[16,4096]{1,0:T(8,128)(2,1)S(1)} %get-tuple-element.83), channel_id=1, source_target_pairs={{0,6},{1,7},{2,4},{3,5},{4,2},{5,3},{6,0},{7,1},{8,14},{9,15},{10,... | collective-permute-start | bytes 393224 | tf_op jit(solution)/shard_map/ppermute | solution.py:34
  41.1 8.2 %collective-permute-start.21 = (bf16[4,4096]{1,0:T(4,128)(2,1)S(1)}, bf16[4,4096]{1,0:T(4,128)(2,1)S(1)}, u32[]{:S(2)}, u32[]{:S(2)}) collective-permute-start(bf16[4,4096]{1,0:T(4,128)(2,1)S(1)} %get-tuple-element.91), channel_id=1, source_target_pairs={{0,8},{1,9},{2,10},{3,11},{4,12},{5,13},{6,14},{7,15},{8,0},{9,1},... | collective-permute-start | bytes 98312 | tf_op jit(solution)/shard_map/ppermute | solution.py:34
  41.2 9.4 %collective-permute-start.22 = (bf16[4,4096]{1,0:T(4,128)(2,1)S(1)}, bf16[4,4096]{1,0:T(4,128)(2,1)S(1)}, u32[]{:S(2)}, u32[]{:S(2)}) collective-permute-start(bf16[4,4096]{1,0:T(4,128)(2,1)S(1)} %get-tuple-element.93), channel_id=1, source_target_pairs={{0,16},{1,17},{2,18},{3,19},{4,20},{5,21},{6,22},{7,23},{8,24},{9,... | collective-permute-start | bytes 98312 | tf_op jit(solution)/shard_map/ppermute | solution.py:34
  44.4 6.2 %collective-permute-start.23 = (bf16[4,4096]{1,0:T(4,128)(2,1)S(1)}, bf16[4,4096]{1,0:T(4,128)(2,1)S(1)}, u32[]{:S(2)}, u32[]{:S(2)}) collective-permute-start(bf16[4,4096]{1,0:T(4,128)(2,1)S(1)} %get-tuple-element.92), channel_id=1, source_target_pairs={{0,24},{1,25},{2,26},{3,27},{4,28},{5,29},{6,30},{7,31},{8,16},{9,... | collective-permute-start | bytes 98312 | tf_op jit(solution)/shard_map/ppermute | solution.py:34
  46.2 4.5 %collective-permute-start.14 = (bf16[4,4096]{1,0:T(4,128)(2,1)S(1)}, bf16[4,4096]{1,0:T(4,128)(2,1)S(1)}, u32[]{:S(2)}, u32[]{:S(2)}) collective-permute-start(bf16[4,4096]{1,0:T(4,128)(2,1)S(1)} %get-tuple-element.88), channel_id=1, source_target_pairs={{0,8},{1,9},{2,10},{3,11},{4,12},{5,13},{6,14},{7,15},{8,0},{9,1},... | collective-permute-start | bytes 98312 | tf_op jit(solution)/shard_map/ppermute | solution.py:34
  46.3 5.0 %collective-permute-start.15 = (bf16[4,4096]{1,0:T(4,128)(2,1)S(1)}, bf16[4,4096]{1,0:T(4,128)(2,1)S(1)}, u32[]{:S(2)}, u32[]{:S(2)}) collective-permute-start(bf16[4,4096]{1,0:T(4,128)(2,1)S(1)} %get-tuple-element.90), channel_id=1, source_target_pairs={{0,16},{1,17},{2,18},{3,19},{4,20},{5,21},{6,22},{7,23},{8,24},{9,... | collective-permute-start | bytes 98312 | tf_op jit(solution)/shard_map/ppermute | solution.py:34
  49.3 5.7 %collective-permute-start.16 = (bf16[4,4096]{1,0:T(4,128)(2,1)S(1)}, bf16[4,4096]{1,0:T(4,128)(2,1)S(1)}, u32[]{:S(2)}, u32[]{:S(2)}) collective-permute-start(bf16[4,4096]{1,0:T(4,128)(2,1)S(1)} %get-tuple-element.89), channel_id=1, source_target_pairs={{0,24},{1,25},{2,26},{3,27},{4,28},{5,29},{6,30},{7,31},{8,16},{9,... | collective-permute-start | bytes 98312 | tf_op jit(solution)/shard_map/ppermute | solution.py:34
  55.8 4.5 %collective-permute-start.24 = (bf16[4,4224]{1,0:T(4,128)(2,1)S(1)}, bf16[4,4224]{1,0:T(4,128)(2,1)S(1)}, u32[]{:S(2)}, u32[]{:S(2)}) collective-permute-start(bf16[4,4224]{1,0:T(4,128)(2,1)S(1)} %pad_maximum_fusion.2), channel_id=1, source_target_pairs={{0,8},{1,9},{2,10},{3,11},{4,12},{5,13},{6,14},{7,15},{8,0},{9,1},... | collective-permute-start | bytes 101384 | tf_op jit(solution)/shard_map/ppermute | solution.py:34
  55.9 4.9 %collective-permute-start.25 = (bf16[4,4224]{1,0:T(4,128)(2,1)S(1)}, bf16[4,4224]{1,0:T(4,128)(2,1)S(1)}, u32[]{:S(2)}, u32[]{:S(2)}) collective-permute-start(bf16[4,4224]{1,0:T(4,128)(2,1)S(1)} %pad_maximum_fusion.2), channel_id=1, source_target_pairs={{0,16},{1,17},{2,18},{3,19},{4,20},{5,21},{6,22},{7,23},{8,24},{9,... | collective-permute-start | bytes 101384 | tf_op jit(solution)/shard_map/ppermute | solution.py:34
  57.8 5.7 %collective-permute-start.26 = (bf16[4,4224]{1,0:T(4,128)(2,1)S(1)}, bf16[4,4224]{1,0:T(4,128)(2,1)S(1)}, u32[]{:S(2)}, u32[]{:S(2)}) collective-permute-start(bf16[4,4224]{1,0:T(4,128)(2,1)S(1)} %pad_maximum_fusion.2), channel_id=1, source_target_pairs={{0,24},{1,25},{2,26},{3,27},{4,28},{5,29},{6,30},{7,31},{8,16},{9,... | collective-permute-start | bytes 101384 | tf_op jit(solution)/shard_map/ppermute | solution.py:34
  63.6 5.1 %collective-permute-start.27 = (bf16[16,4224]{1,0:T(8,128)(2,1)S(1)}, bf16[16,4224]{1,0:T(8,128)(2,1)S(1)}, u32[]{:S(2)}, u32[]{:S(2)}) collective-permute-start(bf16[16,4224]{1,0:T(8,128)(2,1)S(1)} %pad_maximum_fusion.refs_0_), channel_id=1, source_target_pairs={{0,2},{1,3},{2,0},{3,1},{4,6},{5,7},{6,4},{7,5},{8,10},{9,11},{10,... | collective-permute-start | bytes 405512 | tf_op jit(solution)/shard_map/ppermute | solution.py:34
  65.0 5.0 %collective-permute-start.28 = (bf16[16,4224]{1,0:T(8,128)(2,1)S(1)}, bf16[16,4224]{1,0:T(8,128)(2,1)S(1)}, u32[]{:S(2)}, u32[]{:S(2)}) collective-permute-start(bf16[16,4224]{1,0:T(8,128)(2,1)S(1)} %pad_maximum_fusion.refs_0_), channel_id=1, source_target_pairs={{0,4},{1,5},{2,6},{3,7},{4,0},{5,1},{6,2},{7,3},{8,12},{9,13},{10,... | collective-permute-start | bytes 405512 | tf_op jit(solution)/shard_map/ppermute | solution.py:34
  65.7 5.9 %collective-permute-start.29 = (bf16[16,4224]{1,0:T(8,128)(2,1)S(1)}, bf16[16,4224]{1,0:T(8,128)(2,1)S(1)}, u32[]{:S(2)}, u32[]{:S(2)}) collective-permute-start(bf16[16,4224]{1,0:T(8,128)(2,1)S(1)} %pad_maximum_fusion.refs_0_), channel_id=1, source_target_pairs={{0,6},{1,7},{2,4},{3,5},{4,2},{5,3},{6,0},{7,1},{8,14},{9,15},{10,... | collective-permute-start | bytes 405512 | tf_op jit(solution)/shard_map/ppermute | solution.py:34
  67.2 4.5 %collective-permute-start.30 = (bf16[16,4224]{1,0:T(8,128)(2,1)S(1)}, bf16[16,4224]{1,0:T(8,128)(2,1)S(1)}, u32[]{:S(2)}, u32[]{:S(2)}) collective-permute-start(bf16[16,4224]{1,0:T(8,128)(2,1)S(1)} %pad_maximum_fusion.refs_0_), channel_id=1, source_target_pairs={{0,1},{1,0},{2,3},{3,2},{4,5},{5,4},{6,7},{7,6},{8,9},{9,8},{10,11... | collective-permute-start | bytes 405512 | tf_op jit(solution)/shard_map/ppermute | solution.py:34
  68.7 3.0 %collective-permute-start.31 = (bf16[16,4224]{1,0:T(8,128)(2,1)S(1)}, bf16[16,4224]{1,0:T(8,128)(2,1)S(1)}, u32[]{:S(2)}, u32[]{:S(2)}) collective-permute-start(bf16[16,4224]{1,0:T(8,128)(2,1)S(1)} %collective-permute-done.27.refs_1_), channel_id=1, source_target_pairs={{0,1},{1,0},{2,3},{3,2},{4,5},{5,4},{6,7},{7,6},{8,9},{9,8},{10,11... | collective-permute-start | bytes 405512 | tf_op jit(solution)/shard_map/ppermute | solution.py:34
  70.0 1.7 %collective-permute-start.32 = (bf16[16,4224]{1,0:T(8,128)(2,1)S(1)}, bf16[16,4224]{1,0:T(8,128)(2,1)S(1)}, u32[]{:S(2)}, u32[]{:S(2)}) collective-permute-start(bf16[16,4224]{1,0:T(8,128)(2,1)S(1)} %collective-permute-done.28.refs_2_), channel_id=1, source_target_pairs={{0,1},{1,0},{2,3},{3,2},{4,5},{5,4},{6,7},{7,6},{8,9},{9,8},{10,11... | collective-permute-start | bytes 405512 | tf_op jit(solution)/shard_map/ppermute | solution.py:34
  71.6 1.4 %collective-permute-start.33 = (bf16[16,4224]{1,0:T(8,128)(2,1)S(1)}, bf16[16,4224]{1,0:T(8,128)(2,1)S(1)}, u32[]{:S(2)}, u32[]{:S(2)}) collective-permute-start(bf16[16,4224]{1,0:T(8,128)(2,1)S(1)} %collective-permute-done.29.refs_3_), channel_id=1, source_target_pairs={{0,1},{1,0},{2,3},{3,2},{4,5},{5,4},{6,7},{7,6},{8,9},{9,8},{10,11... | collective-permute-start | bytes 405512 | tf_op jit(solution)/shard_map/ppermute | solution.py:34
  (10 other events, 245.8 us)

commit v3 on v2

--- a/solution.py
+++ b/solution.py
@@ -17,7 +17,8 @@
 LANES = 128
 FETCH_VMEM = 4 << 20
 FORWARD_VMEM = 8 << 20
-BACKWARD_VMEM = 36 << 20
+BACKWARD_VMEM = 32 << 20
+BACKWARD_CHUNK = 1024
 
 
 def exchange_levels(members):
@@ -25,7 +26,7 @@
     levels, rest = [bits[:1]], bits[1:]
     while rest:
         low, rest = rest[:2], rest[2:]
-        levels.append(low + [low[0] | low[1]] if len(low) == 2 else low)
+        levels.append([low[0] | low[1], low[1], low[0]] if len(low) == 2 else low)
     return [level for level in levels if level]
 
 
@@ -84,12 +85,16 @@
 NN = (((1,), (0,)), ((), ()))
 
 
-def column_chunk(width):
-    return 1024 if width % 1024 == 0 else width
+def column_chunk(width, wanted=1024):
+    return wanted if width % wanted == 0 else width
 
 
 def dot(left, right, dims):
     return lax.dot_general(left, right, dims, preferred_element_type=jnp.float32)
+
+
+def keep_in_hbm(array):
+    return pltpu.with_memory_space_constraint(array, pltpu.HBM)
 
 
 def fetch_kernel(*refs):
@@ -118,7 +123,7 @@
         cost_estimate=pl.CostEstimate(
             flops=0, bytes_accessed=sum(2 * w.size for w in weights), transcendentals=0
         ),
-    )(*[pltpu.with_memory_space_constraint(w, pltpu.HBM) for w in weights])
+    )(*[keep_in_hbm(w) for w in weights])
 
 
 def forward_model(weights, normed, hidden_rows, sent, kept, chunk):
@@ -210,15 +215,15 @@
     )
 
 
-def backward_kernel(block_count, chunk, *refs):
+def backward_kernel(block_count, chunk, token_count, *refs):
     blocks = refs[:block_count]
-    normed, gate_ref, up_ref, hidden_ref, lengths, prompts, rewards, places, down = refs[
+    normed, gate_ref, up_ref, hidden_ref, lengths, prompts, rewards, masks, down = refs[
         block_count : block_count + 9
     ]
     grad_gate, grad_up, grad_down, advantage_out = refs[block_count + 9 : block_count + 13]
-    slopes, held, total, gate_left, up_left, down_left, gate_buf, up_buf, down_buf, in_sems, sems = (
-        refs[block_count + 13 :]
-    )
+    slopes, gate_left, up_left, down_left, gate_buf, up_buf, down_buf, sems = refs[
+        block_count + 13 :
+    ]
     width = normed.shape[1]
     steps = width // chunk
     tokens = normed.shape[0]
@@ -227,11 +232,6 @@
 
     def columns(step):
         return pl.ds(pl.multiple_of(step * chunk, chunk), chunk)
-
-    def copy_in(step):
-        return pltpu.make_async_copy(
-            down.at[:, columns(step)], held.at[:, columns(step)], in_sems.at[step]
-        )
 
     def copy_out(which, step):
         source = (gate_buf, up_buf, down_buf)[which]
@@ -240,9 +240,6 @@
             source.at[:, columns(step)], target.at[:, columns(step)], sems.at[which, step]
         )
 
-    for step in range(steps):
-        copy_in(step).start()
-
     gaps = []
     for place, block in enumerate(blocks):
         slopes[place * height : (place + 1) * height, :] = block[:, :width]
@@ -263,7 +260,9 @@
     ends = as_column(counts, col <= row)
     starts = ends - as_column(counts, diagonal)
     kinds = prompts[...].astype(jnp.float32)
-    place_line = places[...].astype(jnp.float32)
+    own = lax.axis_index("fsdp").astype(jnp.int32)
+    within = lax.broadcasted_iota(jnp.int32, (1, tokens), 1) % token_count
+    place_line = ((masks[...] ^ own) * token_count + within).astype(jnp.float32)
     token_row = lax.broadcasted_iota(jnp.int32, (tokens, tokens), 0)
     token_col = lax.broadcasted_iota(jnp.int32, (tokens, tokens), 1)
     place_column = as_column(place_line, token_row == token_col)
@@ -281,31 +280,28 @@
     weight = jnp.sum(jnp.where(inside(place_line), advantage, 0.0), axis=0, keepdims=True)
 
     down_left[...] = (hidden_ref[...].astype(jnp.float32) * weight).astype(jnp.bfloat16)
-    total[...] = jnp.zeros_like(total)
-
-    def first(step, _):
-        down_buf[:, columns(step)] = dot(down_left[...], slopes[:, columns(step)], NN)
-        copy_out(2, step).start()
-        copy_in(step).wait()
-        total[...] += dot(held[:, columns(step)], slopes[:, columns(step)], NT)
-        return 0
-
-    lax.fori_loop(0, steps, first, 0)
-    grad_hidden = total[...] * weight
+
+    def product(which, left, right, buffer):
+        def body(step, _):
+            buffer[:, columns(step)] = dot(left[...], right[:, columns(step)], NN)
+            copy_out(which, step).start()
+            return 0
+
+        return body
+
+    early = steps - steps // 4
+    down_step = product(2, down_left, slopes, down_buf)
+    lax.fori_loop(0, early, down_step, 0)
+    grad_hidden = dot(down[...], slopes[...], NT) * weight
+    lax.fori_loop(early, steps, down_step, 0)
     gate = gate_ref[...]
     sigmoid = 1.0 / (1.0 + jnp.exp(-gate))
     gate_left[...] = (
         grad_hidden * up_ref[...] * sigmoid * (1.0 + gate * (1.0 - sigmoid))
     ).astype(jnp.bfloat16)
     up_left[...] = (grad_hidden * gate * sigmoid).astype(jnp.bfloat16)
-
-    def second(step, _):
-        for which, left, buffer in ((0, gate_left, gate_buf), (1, up_left, up_buf)):
-            buffer[:, columns(step)] = dot(left[...], normed[:, columns(step)], NN)
-            copy_out(which, step).start()
-        return 0
-
-    lax.fori_loop(0, steps, second, 0)
+    lax.fori_loop(0, steps, product(0, gate_left, normed, gate_buf), 0)
+    lax.fori_loop(0, steps, product(1, up_left, normed, up_buf), 0)
 
     def finish(step, _):
         for which in range(3):
@@ -315,10 +311,10 @@
     lax.fori_loop(0, steps, finish, 0)
 
 
-def backward(blocks, normed, gate, up, hidden, samples, down):
+def backward(blocks, normed, gate, up, hidden, samples, down, token_count):
     tokens, width = normed.shape
     units = gate.shape[0]
-    chunk = column_chunk(width)
+    chunk = column_chunk(width, BACKWARD_CHUNK)
     vmem = pl.BlockSpec(memory_space=pltpu.VMEM)
     hbm = pl.BlockSpec(memory_space=pl.ANY)
     grad = jax.ShapeDtypeStruct((units, width), jnp.float32)
@@ -327,21 +323,18 @@
     buffer = pltpu.VMEM((units, width), jnp.float32)
     steps = width // chunk
     return pl.pallas_call(
-        functools.partial(backward_kernel, len(blocks), chunk),
+        functools.partial(backward_kernel, len(blocks), chunk, token_count),
         out_shape=(grad, grad, grad, jax.ShapeDtypeStruct((1, count), jnp.float32)),
-        in_specs=[vmem] * (len(blocks) + 8) + [hbm],
+        in_specs=[vmem] * (len(blocks) + 9),
         out_specs=(hbm, hbm, hbm, vmem),
         scratch_shapes=[
             pltpu.VMEM((tokens, width), jnp.bfloat16),
-            pltpu.VMEM((units, width), jnp.bfloat16),
-            pltpu.VMEM((units, tokens), jnp.float32),
             left,
             left,
             left,
             buffer,
             buffer,
             buffer,
-            pltpu.SemaphoreType.DMA((steps,)),
             pltpu.SemaphoreType.DMA((3, steps)),
         ],
         compiler_params=pltpu.CompilerParams(vmem_limit_bytes=BACKWARD_VMEM),
@@ -357,7 +350,7 @@
         up,
         hidden,
         *samples,
-        pltpu.with_memory_space_constraint(down, pltpu.HBM),
+        down,
     )
 
 
@@ -377,9 +370,7 @@
 ):
     token_count, width = hidden_states.shape
     levels = exchange_levels(lax.axis_size("fsdp"))
-    masks = row_masks(levels)
-    tokens = token_count * masks.size
-    member = lax.axis_index("fsdp").astype(jnp.int32)
+    row_members = jnp.asarray(np.repeat(row_masks(levels), token_count))
 
     blocks, (ref_weights, pol_weights) = gather_blocks(
         hidden_states,
@@ -415,19 +406,16 @@
     extra = jnp.pad(extra, ((0, 0), (0, LANES - PIECES)))
     payload = jnp.concatenate([slopes, extra], axis=1).astype(jnp.bfloat16)
 
-    row_place = (
-        (member ^ jnp.asarray(np.repeat(masks, token_count))) * token_count
-        + jnp.asarray(np.tile(np.arange(token_count, dtype=np.int32), masks.size))
-    )
-    slope_blocks, _ = gather_blocks(payload, levels)
+    slope_blocks, (_, down_again) = gather_blocks(payload, levels, (None, fetch([pol_down_w])))
     grad_gate, grad_up, grad_down, advantage = backward(
         slope_blocks,
         normed,
         gate,
         up,
         hidden,
-        (sample_lengths, prompt_index, rewards, row_place[None, :]),
-        pol_down_w,
+        (sample_lengths, prompt_index, rewards, row_members[None, :]),
+        down_again[0],
+        token_count,
     )
     return grad_gate.T, grad_up.T, grad_down, advantage
 

time: 83.8 us -> 80.3 us (0.958)
  waiting for transfers between devices: 19 us -> 13.7 us
  starting transfers between devices: 35.5 us -> 36.6 us
  Pallas kernels: 26.6 us -> 27.5 us
    ppermute x34, waiting for transfers between devices: 19 us -> 13.7 us  [swap(): return lax.ppermute(values, 'fsdp', [(i, i ^ mask) for i in range(members)])]
    pallas_call x2 -> x3, Pallas kernels: 8.69 us -> 10.8 us  [fetch(): pl.pallas_call(fetch_kernel, out_shape=[jax.ShapeDtypeStruct(w.shape, w.d...]
    pallas_call x1, Pallas kernels: 10.7 us -> 9.45 us  [backward(): pl.pallas_call(functools.partial(backward_kernel, len(blocks), chunk, tok...]
    ppermute x34, starting transfers between devices: 35.5 us -> 36.6 us  [swap(): return lax.ppermute(values, 'fsdp', [(i, i ^ mask) for i in range(members)])]
  transfers between devices with their start and end apart: 34 -> 34, of which waited for: 16 -> 21; matrix products, arithmetic and copies ran while one was open for 1% -> 1% of each run, Pallas kernels for 15% -> 18%
where the time goes in v3:
time: 80.3 us; the launch traced here: 80.2 us
  starting transfers between devices  36.6 us (46%)
  Pallas kernels  27.5 us (34%)
  waiting for transfers between devices  13.7 us (17%)
  other arithmetic  1.26 us (2%)
  between operations  0.89 us (1%)
    ppermute x34, starting transfers between devices, swap(): return lax.ppermute(values, 'fsdp', [(i, i ^ mask) for i in range(members)])  36.6 us
    ppermute x34, waiting for transfers between devices, swap(): return lax.ppermute(values, 'fsdp', [(i, i ^ mask) for i in range(members)])  13.7 us
    pallas_call x3, Pallas kernels, fetch(): pl.pallas_call(fetch_kernel, out_shape=[jax.ShapeDtypeStruct(w.shape, w.d...  10.8 us
    pallas_call x1, Pallas kernels, backward(): pl.pallas_call(functools.partial(backward_kernel, len(blocks), chunk, tok...  9.45 us
    pallas_call x2, Pallas kernels, forward_call(): pl.pallas_call(kernel, out_shape=shapes, in_specs=[vmem] * (len(operands)...  7.26 us
  transfers between devices with their start and end apart: 34, of which 21 were waited for; matrix products, arithmetic and copies ran while one was open for 1% of the time, Pallas kernels for 18%

profile of v3, /device:TPU:0, one launch (start us, length us, event | category | flops | bytes accessed | tf_op | source)
XLA Modules:
  0.0 80.2 jit_solution(946540105123623069)
XLA Ops:
  0.6 5.1 %collective-permute-start = (bf16[4,4096]{1,0:T(4,128)(2,1)}, bf16[4,4096]{1,0:T(4,128)(2,1)S(1)}, u32[]{:S(2)}, u32[]{:S(2)}) collective-permute-start(bf16[4,4096]{1,0:T(4,128)(2,1)} %param.13), channel_id=1, source_target_pairs={{0,24},{1,25},{2,26},{3,27},{4,28},{5,29},{6,30},{7,31},{8,16},{9,... | collective-permute-start | bytes 98312 | tf_op jit(solution)/shard_map/ppermute | solution.py:35
  5.8 0.6 collective-permute-start.2
  6.4 4.3 %shard_map.156 = (bf16[462,4096]{1,0:T(8,128)(2,1)S(1)}, bf16[462,4096]{1,0:T(8,128)(2,1)S(1)}, bf16[462,4096]{1,0:T(8,128)(2,1)S(1)}) custom-call(bf16[462,4096]{1,0:T(8,128)(2,1)} %bitcast.10, bf16[462,4096]{1,0:T(8,128)(2,1)} %bitcast.11, bf16[462,4096]{1,0:T(8,128)(2,1)} %refs_2_.2), custom_call_target="tpu_custom_call" | custom-call | bytes 11354112 | tf_op jit(solution)/shard_map/pallas_call | solution.py:116
  10.9 2.7 %collective-permute-start.3 = (bf16[16,4096]{1,0:T(8,128)(2,1)S(1)}, bf16[16,4096]{1,0:T(8,128)(2,1)S(1)}, u32[]{:S(2)}, u32[]{:S(2)}) collective-permute-start(bf16[16,4096]{1,0:T(8,128)(2,1)S(1)} %pad_maximum_fusion.1.refs_0_), channel_id=1, source_target_pairs={{0,6},{1,7},{2,4},{3,5},{4,2},{5,3},{6,0},{7,1},{8,14},{9,15},{10,... | collective-permute-start | bytes 393224 | tf_op jit(solution)/shard_map/ppermute | solution.py:35
  14.5 4.3 %shard_map.157 = (bf16[462,4096]{1,0:T(8,128)(2,1)S(1)}, bf16[462,4096]{1,0:T(8,128)(2,1)S(1)}, bf16[462,4096]{1,0:T(8,128)(2,1)S(1)}) custom-call(bf16[462,4096]{1,0:T(8,128)(2,1)} %bitcast.12, bf16[462,4096]{1,0:T(8,128)(2,1)} %bitcast.13, bf16[462,4096]{1,0:T(8,128)(2,1)} %refs_0_.1), custom_call_target="tpu_custom_call" | custom-call | bytes 11354112 | tf_op jit(solution)/shard_map/pallas_call | solution.py:116
  20.2 0.6 collective-permute-done.7.refs_5_
  21.3 3.8 %shard_map.158 = (bf16[128,4096]{1,0:T(8,128)(2,1)S(1)}, bf16[64,4096]{1,0:T(8,128)(2,1)S(1)}, f32[64,4096]{1,0:T(8,128)S(1)}) custom-call(bf16[16,4096]{1,0:T(8,128)(2,1)S(1)} %pad_maximum_fusion.1.refs_0_, bf16[16,4096]{1,0:T(8,128)(2,1)S(1)} %collective-permute-done.3.refs_1_, bf16[16,4096]{1,0:T(8,128)(2,1)S(1)} %collective-permute-done.4.refs_2_, ...), custom_call_target="tpu_custom_call" | custom-call | flops 1453326336 | bytes 11354112 | tf_op jit(solution)/shard_map/pallas_call | solution.py:178
  25.3 3.5 %shard_map.159 = (f32[462,128]{1,0:T(8,128)S(1)}, f32[462,128]{1,0:T(8,128)S(1)}, bf16[462,128]{1,0:T(8,128)(2,1)S(1)}, bf16[64,4096]{1,0:T(8,128)(2,1)S(1)}, f32[64,4096]{1,0:T(8,128)S(1)}) custom-call(bf16[128,4096]{1,0:T(8,128)(2,1)S(1)} %get-tuple-element.53.normed.refs_8_, bf16[462,4096]{1,0:T(8,128)(2,1)S(1)} %get-tuple-element.54.refs_0_, ...), custom_call_target="tpu_custom_call" | custom-call | flops 1453326336 | bytes 11354112 | tf_op jit(solution)/shard_map/pallas_call | solution.py:178
  29.4 2.3 %collective-permute-start.18 = (bf16[16,4096]{1,0:T(8,128)(2,1)S(1)}, bf16[16,4096]{1,0:T(8,128)(2,1)S(1)}, u32[]{:S(2)}, u32[]{:S(2)}) collective-permute-start(bf16[16,4096]{1,0:T(8,128)(2,1)S(1)} %get-tuple-element.93), channel_id=1, source_target_pairs={{0,6},{1,7},{2,4},{3,5},{4,2},{5,3},{6,0},{7,1},{8,14},{9,15},{10,... | collective-permute-start | bytes 393224 | tf_op jit(solution)/shard_map/ppermute | solution.py:35
  31.7 0.7 collective-permute-start.19
  33.1 2.3 %collective-permute-start.11 = (bf16[16,4096]{1,0:T(8,128)(2,1)S(1)}, bf16[16,4096]{1,0:T(8,128)(2,1)S(1)}, u32[]{:S(2)}, u32[]{:S(2)}) collective-permute-start(bf16[16,4096]{1,0:T(8,128)(2,1)S(1)} %get-tuple-element.90), channel_id=1, source_target_pairs={{0,6},{1,7},{2,4},{3,5},{4,2},{5,3},{6,0},{7,1},{8,14},{9,15},{10,... | collective-permute-start | bytes 393224 | tf_op jit(solution)/shard_map/ppermute | solution.py:35
  35.5 0.7 collective-permute-start.12
  36.3 1.9 %collective-permute-start.13 = (bf16[16,4096]{1,0:T(8,128)(2,1)S(1)}, bf16[16,4096]{1,0:T(8,128)(2,1)S(1)}, u32[]{:S(2)}, u32[]{:S(2)}) collective-permute-start(bf16[16,4096]{1,0:T(8,128)(2,1)S(1)} %get-tuple-element.91), channel_id=1, source_target_pairs={{0,2},{1,3},{2,0},{3,1},{4,6},{5,7},{6,4},{7,5},{8,10},{9,11},{10,... | collective-permute-start | bytes 393224 | tf_op jit(solution)/shard_map/ppermute | solution.py:35
  38.3 1.4 %collective-permute-done.19 = bf16[16,4096]{1,0:T(8,128)(2,1)S(1)} collective-permute-done((bf16[16,4096]{1,0:T(8,128)(2,1)S(1)}, bf16[16,4096]{1,0:T(8,128)(2,1)S(1)}, u32[]{:S(2)}, u32[]{:S(2)}) %collective-permute-start.19) | collective-permute-done | bytes 131104 | tf_op jit(solution)/shard_map/ppermute | solution.py:35
  39.8 3.7 %collective-permute-start.21 = (bf16[4,4096]{1,0:T(4,128)(2,1)S(1)}, bf16[4,4096]{1,0:T(4,128)(2,1)S(1)}, u32[]{:S(2)}, u32[]{:S(2)}) collective-permute-start(bf16[4,4096]{1,0:T(4,128)(2,1)S(1)} %get-tuple-element.99), channel_id=1, source_target_pairs={{0,24},{1,25},{2,26},{3,27},{4,28},{5,29},{6,30},{7,31},{8,16},{9,... | collective-permute-start | bytes 98312 | tf_op jit(solution)/shard_map/ppermute | solution.py:35
  43.5 0.8 collective-permute-start.23
  44.6 3.7 %collective-permute-start.14 = (bf16[4,4096]{1,0:T(4,128)(2,1)S(1)}, bf16[4,4096]{1,0:T(4,128)(2,1)S(1)}, u32[]{:S(2)}, u32[]{:S(2)}) collective-permute-start(bf16[4,4096]{1,0:T(4,128)(2,1)S(1)} %get-tuple-element.96), channel_id=1, source_target_pairs={{0,24},{1,25},{2,26},{3,27},{4,28},{5,29},{6,30},{7,31},{8,16},{9,... | collective-permute-start | bytes 98312 | tf_op jit(solution)/shard_map/ppermute | solution.py:35
  48.3 0.8 collective-permute-start.16
  49.1 1.6 %collective-permute-done.14 = bf16[4,4096]{1,0:T(4,128)(2,1)S(1)} collective-permute-done((bf16[4,4096]{1,0:T(4,128)(2,1)S(1)}, bf16[4,4096]{1,0:T(4,128)(2,1)S(1)}, u32[]{:S(2)}, u32[]{:S(2)}) %collective-permute-start.14) | collective-permute-done | bytes 32800 | tf_op jit(solution)/shard_map/ppermute | solution.py:35
  50.7 2.4 %collective-permute-done.15 = bf16[4,4096]{1,0:T(4,128)(2,1)S(1)} collective-permute-done((bf16[4,4096]{1,0:T(4,128)(2,1)S(1)}, bf16[4,4096]{1,0:T(4,128)(2,1)S(1)}, u32[]{:S(2)}, u32[]{:S(2)}) %collective-permute-start.15) | collective-permute-done | bytes 32800 | tf_op jit(solution)/shard_map/ppermute | solution.py:35
  54.0 1.5 %collective-permute-start.24 = (bf16[4,4224]{1,0:T(4,128)(2,1)S(1)}, bf16[4,4224]{1,0:T(4,128)(2,1)S(1)}, u32[]{:S(2)}, u32[]{:S(2)}) collective-permute-start(bf16[4,4224]{1,0:T(4,128)(2,1)S(1)} %pad_maximum_fusion.2), channel_id=1, source_target_pairs={{0,24},{1,25},{2,26},{3,27},{4,28},{5,29},{6,30},{7,31},{8,16},{9,... | collective-permute-start | bytes 101384 | tf_op jit(solution)/shard_map/ppermute | solution.py:35
  55.5 0.6 collective-permute-start.25
  56.1 2.3 %collective-permute-start.26 = (bf16[4,4224]{1,0:T(4,128)(2,1)S(1)}, bf16[4,4224]{1,0:T(4,128)(2,1)S(1)}, u32[]{:S(2)}, u32[]{:S(2)}) collective-permute-start(bf16[4,4224]{1,0:T(4,128)(2,1)S(1)} %pad_maximum_fusion.2), channel_id=1, source_target_pairs={{0,8},{1,9},{2,10},{3,11},{4,12},{5,13},{6,14},{7,15},{8,0},{9,1},... | collective-permute-start | bytes 101384 | tf_op jit(solution)/shard_map/ppermute | solution.py:35
  58.4 1.3 %collective-permute-done.24 = bf16[4,4224]{1,0:T(4,128)(2,1)S(1)} collective-permute-done((bf16[4,4224]{1,0:T(4,128)(2,1)S(1)}, bf16[4,4224]{1,0:T(4,128)(2,1)S(1)}, u32[]{:S(2)}, u32[]{:S(2)}) %collective-permute-start.24) | collective-permute-done | bytes 33824 | tf_op jit(solution)/shard_map/ppermute | solution.py:35
  59.7 0.6 collective-permute-done.25
  60.8 2.1 %collective-permute-start.27 = (bf16[16,4224]{1,0:T(8,128)(2,1)S(1)}, bf16[16,4224]{1,0:T(8,128)(2,1)S(1)}, u32[]{:S(2)}, u32[]{:S(2)}) collective-permute-start(bf16[16,4224]{1,0:T(8,128)(2,1)S(1)} %pad_maximum_fusion.refs_0_), channel_id=1, source_target_pairs={{0,6},{1,7},{2,4},{3,5},{4,2},{5,3},{6,0},{7,1},{8,14},{9,15},{10,... | collective-permute-start | bytes 405512 | tf_op jit(solution)/shard_map/ppermute | solution.py:35
  62.9 0.9 %collective-permute-start.28 = (bf16[16,4224]{1,0:T(8,128)(2,1)S(1)}, bf16[16,4224]{1,0:T(8,128)(2,1)S(1)}, u32[]{:S(2)}, u32[]{:S(2)}) collective-permute-start(bf16[16,4224]{1,0:T(8,128)(2,1)S(1)} %pad_maximum_fusion.refs_0_), channel_id=1, source_target_pairs={{0,4},{1,5},{2,6},{3,7},{4,0},{5,1},{6,2},{7,3},{8,12},{9,13},{10,... | collective-permute-start | bytes 405512 | tf_op jit(solution)/shard_map/ppermute | solution.py:35
  64.4 2.1 %shard_map.160.refs_16_ = bf16[462,4096]{1,0:T(8,128)(2,1)S(1)} custom-call(bf16[462,4096]{1,0:T(8,128)(2,1)} %refs_0_.1), custom_call_target="tpu_custom_call" | custom-call | bytes 3784704 | tf_op jit(solution)/shard_map/pallas_call | solution.py:116
  66.8 1.4 %collective-permute-done.28.refs_2_ = bf16[16,4224]{1,0:T(8,128)(2,1)S(1)} collective-permute-done((bf16[16,4224]{1,0:T(8,128)(2,1)S(1)}, bf16[16,4224]{1,0:T(8,128)(2,1)S(1)}, u32[]{:S(2)}, u32[]{:S(2)}) %collective-permute-start.28) | collective-permute-done | bytes 135200 | tf_op jit(solution)/shard_map/ppermute | solution.py:35
  68.2 0.6 collective-permute-done.29.refs_3_
  69.4 0.8 %collective-permute-done.31.refs_5_ = bf16[16,4224]{1,0:T(8,128)(2,1)S(1)} collective-permute-done((bf16[16,4224]{1,0:T(8,128)(2,1)S(1)}, bf16[16,4224]{1,0:T(8,128)(2,1)S(1)}, u32[]{:S(2)}, u32[]{:S(2)}) %collective-permute-start.31) | collective-permute-done | bytes 135200 | tf_op jit(solution)/shard_map/ppermute | solution.py:35
  70.7 9.4 %shard_map.161 = (f32[462,4096]{1,0:T(8,128)}, f32[462,4096]{1,0:T(8,128)}, f32[462,4096]{1,0:T(8,128)}, f32[1,32]{1,0:T(1,128)}) custom-call(bf16[16,4224]{1,0:T(8,128)(2,1)S(1)} %pad_maximum_fusion.refs_0_, bf16[16,4224]{1,0:T(8,128)(2,1)S(1)} %collective-permute-done.27.refs_1_, bf16[16,4224]{1,0:T(8,128)(2,1)S(1)} %collective-permute-done.28.refs_2_, ...), custom_call_target="tpu_custom_call" | custom-call | flops 1937768448 | bytes 26492928 | tf_op jit(solution)/shard_map/pallas_call | solution.py:325
  (74 shorter events, 8.2 us)
Async XLA Ops:
  0.6 10.1 %collective-permute-start = (bf16[4,4096]{1,0:T(4,128)(2,1)}, bf16[4,4096]{1,0:T(4,128)(2,1)S(1)}, u32[]{:S(2)}, u32[]{:S(2)}) collective-permute-start(bf16[4,4096]{1,0:T(4,128)(2,1)} %param.13), channel_id=1, source_target_pairs={{0,24},{1,25},{2,26},{3,27},{4,28},{5,29},{6,30},{7,31},{8,16},{9,... | collective-permute-start | bytes 98312 | tf_op jit(solution)/shard_map/ppermute | solution.py:35
  5.8 5.0 %collective-permute-start.1 = (bf16[4,4096]{1,0:T(4,128)(2,1)}, bf16[4,4096]{1,0:T(4,128)(2,1)S(1)}, u32[]{:S(2)}, u32[]{:S(2)}) collective-permute-start(bf16[4,4096]{1,0:T(4,128)(2,1)} %param.13), channel_id=1, source_target_pairs={{0,16},{1,17},{2,18},{3,19},{4,20},{5,21},{6,22},{7,23},{8,24},{9,... | collective-permute-start | bytes 98312 | tf_op jit(solution)/shard_map/ppermute | solution.py:35
  5.8 5.0 %collective-permute-start.2 = (bf16[4,4096]{1,0:T(4,128)(2,1)}, bf16[4,4096]{1,0:T(4,128)(2,1)S(1)}, u32[]{:S(2)}, u32[]{:S(2)}) collective-permute-start(bf16[4,4096]{1,0:T(4,128)(2,1)} %param.13), channel_id=1, source_target_pairs={{0,8},{1,9},{2,10},{3,11},{4,12},{5,13},{6,14},{7,15},{8,0},{9,1},... | collective-permute-start | bytes 98312 | tf_op jit(solution)/shard_map/ppermute | solution.py:35
  10.9 8.0 %collective-permute-start.3 = (bf16[16,4096]{1,0:T(8,128)(2,1)S(1)}, bf16[16,4096]{1,0:T(8,128)(2,1)S(1)}, u32[]{:S(2)}, u32[]{:S(2)}) collective-permute-start(bf16[16,4096]{1,0:T(8,128)(2,1)S(1)} %pad_maximum_fusion.1.refs_0_), channel_id=1, source_target_pairs={{0,6},{1,7},{2,4},{3,5},{4,2},{5,3},{6,0},{7,1},{8,14},{9,15},{10,... | collective-permute-start | bytes 393224 | tf_op jit(solution)/shard_map/ppermute | solution.py:35
  13.6 5.8 %collective-permute-start.4 = (bf16[16,4096]{1,0:T(8,128)(2,1)S(1)}, bf16[16,4096]{1,0:T(8,128)(2,1)S(1)}, u32[]{:S(2)}, u32[]{:S(2)}) collective-permute-start(bf16[16,4096]{1,0:T(8,128)(2,1)S(1)} %pad_maximum_fusion.1.refs_0_), channel_id=1, source_target_pairs={{0,4},{1,5},{2,6},{3,7},{4,0},{5,1},{6,2},{7,3},{8,12},{9,13},{10,... | collective-permute-start | bytes 393224 | tf_op jit(solution)/shard_map/ppermute | solution.py:35
  14.1 5.4 %collective-permute-start.5 = (bf16[16,4096]{1,0:T(8,128)(2,1)S(1)}, bf16[16,4096]{1,0:T(8,128)(2,1)S(1)}, u32[]{:S(2)}, u32[]{:S(2)}) collective-permute-start(bf16[16,4096]{1,0:T(8,128)(2,1)S(1)} %pad_maximum_fusion.1.refs_0_), channel_id=1, source_target_pairs={{0,2},{1,3},{2,0},{3,1},{4,6},{5,7},{6,4},{7,5},{8,10},{9,11},{10,... | collective-permute-start | bytes 393224 | tf_op jit(solution)/shard_map/ppermute | solution.py:35
  18.8 1.4 %collective-permute-start.6 = (bf16[16,4096]{1,0:T(8,128)(2,1)S(1)}, bf16[16,4096]{1,0:T(8,128)(2,1)S(1)}, u32[]{:S(2)}, u32[]{:S(2)}) collective-permute-start(bf16[16,4096]{1,0:T(8,128)(2,1)S(1)} %pad_maximum_fusion.1.refs_0_), channel_id=1, source_target_pairs={{0,1},{1,0},{2,3},{3,2},{4,5},{5,4},{6,7},{7,6},{8,9},{9,8},{10,11... | collective-permute-start | bytes 393224 | tf_op jit(solution)/shard_map/ppermute | solution.py:35
  19.5 1.5 %collective-permute-start.8 = (bf16[16,4096]{1,0:T(8,128)(2,1)S(1)}, bf16[16,4096]{1,0:T(8,128)(2,1)S(1)}, u32[]{:S(2)}, u32[]{:S(2)}) collective-permute-start(bf16[16,4096]{1,0:T(8,128)(2,1)S(1)} %collective-permute-done.4.refs_2_), channel_id=1, source_target_pairs={{0,1},{1,0},{2,3},{3,2},{4,5},{5,4},{6,7},{7,6},{8,9},{9,8},{10,11... | collective-permute-start | bytes 393224 | tf_op jit(solution)/shard_map/ppermute | solution.py:35
  25.1 4.1 %collective-permute-start.17 = (bf16[64,4096]{1,0:T(8,128)(2,1)S(1)}, bf16[64,4096]{1,0:T(8,128)(2,1)S(1)}, u32[]{:S(2)}, u32[]{:S(2)}) collective-permute-start(bf16[64,4096]{1,0:T(8,128)(2,1)S(1)} %get-tuple-element.60), channel_id=1, source_target_pairs={{0,1},{1,0},{2,3},{3,2},{4,5},{5,4},{6,7},{7,6},{8,9},{9,8},{10,11... | collective-permute-start | bytes 1572872 | tf_op jit(solution)/shard_map/ppermute | solution.py:35
  28.8 4.1 %collective-permute-start.10 = (bf16[64,4096]{1,0:T(8,128)(2,1)S(1)}, bf16[64,4096]{1,0:T(8,128)(2,1)S(1)}, u32[]{:S(2)}, u32[]{:S(2)}) collective-permute-start(bf16[64,4096]{1,0:T(8,128)(2,1)S(1)} %get-tuple-element.58), channel_id=1, source_target_pairs={{0,1},{1,0},{2,3},{3,2},{4,5},{5,4},{6,7},{7,6},{8,9},{9,8},{10,11... | collective-permute-start | bytes 1572872 | tf_op jit(solution)/shard_map/ppermute | solution.py:35
  29.4 6.9 %collective-permute-start.18 = (bf16[16,4096]{1,0:T(8,128)(2,1)S(1)}, bf16[16,4096]{1,0:T(8,128)(2,1)S(1)}, u32[]{:S(2)}, u32[]{:S(2)}) collective-permute-start(bf16[16,4096]{1,0:T(8,128)(2,1)S(1)} %get-tuple-element.93), channel_id=1, source_target_pairs={{0,6},{1,7},{2,4},{3,5},{4,2},{5,3},{6,0},{7,1},{8,14},{9,15},{10,... | collective-permute-start | bytes 393224 | tf_op jit(solution)/shard_map/ppermute | solution.py:35
  31.7 7.9 %collective-permute-start.19 = (bf16[16,4096]{1,0:T(8,128)(2,1)S(1)}, bf16[16,4096]{1,0:T(8,128)(2,1)S(1)}, u32[]{:S(2)}, u32[]{:S(2)}) collective-permute-start(bf16[16,4096]{1,0:T(8,128)(2,1)S(1)} %get-tuple-element.95), channel_id=1, source_target_pairs={{0,4},{1,5},{2,6},{3,7},{4,0},{5,1},{6,2},{7,3},{8,12},{9,13},{10,... | collective-permute-start | bytes 393224 | tf_op jit(solution)/shard_map/ppermute | solution.py:35
  32.4 7.2 %collective-permute-start.20 = (bf16[16,4096]{1,0:T(8,128)(2,1)S(1)}, bf16[16,4096]{1,0:T(8,128)(2,1)S(1)}, u32[]{:S(2)}, u32[]{:S(2)}) collective-permute-start(bf16[16,4096]{1,0:T(8,128)(2,1)S(1)} %get-tuple-element.94), channel_id=1, source_target_pairs={{0,2},{1,3},{2,0},{3,1},{4,6},{5,7},{6,4},{7,5},{8,10},{9,11},{10,... | collective-permute-start | bytes 393224 | tf_op jit(solution)/shard_map/ppermute | solution.py:35
  33.1 10.3 %collective-permute-start.11 = (bf16[16,4096]{1,0:T(8,128)(2,1)S(1)}, bf16[16,4096]{1,0:T(8,128)(2,1)S(1)}, u32[]{:S(2)}, u32[]{:S(2)}) collective-permute-start(bf16[16,4096]{1,0:T(8,128)(2,1)S(1)} %get-tuple-element.90), channel_id=1, source_target_pairs={{0,6},{1,7},{2,4},{3,5},{4,2},{5,3},{6,0},{7,1},{8,14},{9,15},{10,... | collective-permute-start | bytes 393224 | tf_op jit(solution)/shard_map/ppermute | solution.py:35
  35.5 8.9 %collective-permute-start.12 = (bf16[16,4096]{1,0:T(8,128)(2,1)S(1)}, bf16[16,4096]{1,0:T(8,128)(2,1)S(1)}, u32[]{:S(2)}, u32[]{:S(2)}) collective-permute-start(bf16[16,4096]{1,0:T(8,128)(2,1)S(1)} %get-tuple-element.92), channel_id=1, source_target_pairs={{0,4},{1,5},{2,6},{3,7},{4,0},{5,1},{6,2},{7,3},{8,12},{9,13},{10,... | collective-permute-start | bytes 393224 | tf_op jit(solution)/shard_map/ppermute | solution.py:35
  36.3 8.2 %collective-permute-start.13 = (bf16[16,4096]{1,0:T(8,128)(2,1)S(1)}, bf16[16,4096]{1,0:T(8,128)(2,1)S(1)}, u32[]{:S(2)}, u32[]{:S(2)}) collective-permute-start(bf16[16,4096]{1,0:T(8,128)(2,1)S(1)} %get-tuple-element.91), channel_id=1, source_target_pairs={{0,2},{1,3},{2,0},{3,1},{4,6},{5,7},{6,4},{7,5},{8,10},{9,11},{10,... | collective-permute-start | bytes 393224 | tf_op jit(solution)/shard_map/ppermute | solution.py:35
  39.8 8.5 %collective-permute-start.21 = (bf16[4,4096]{1,0:T(4,128)(2,1)S(1)}, bf16[4,4096]{1,0:T(4,128)(2,1)S(1)}, u32[]{:S(2)}, u32[]{:S(2)}) collective-permute-start(bf16[4,4096]{1,0:T(4,128)(2,1)S(1)} %get-tuple-element.99), channel_id=1, source_target_pairs={{0,24},{1,25},{2,26},{3,27},{4,28},{5,29},{6,30},{7,31},{8,16},{9,... | collective-permute-start | bytes 98312 | tf_op jit(solution)/shard_map/ppermute | solution.py:35
  43.5 5.6 %collective-permute-start.22 = (bf16[4,4096]{1,0:T(4,128)(2,1)S(1)}, bf16[4,4096]{1,0:T(4,128)(2,1)S(1)}, u32[]{:S(2)}, u32[]{:S(2)}) collective-permute-start(bf16[4,4096]{1,0:T(4,128)(2,1)S(1)} %get-tuple-element.101), channel_id=1, source_target_pairs={{0,16},{1,17},{2,18},{3,19},{4,20},{5,21},{6,22},{7,23},{8,24},{9,... | collective-permute-start | bytes 98312 | tf_op jit(solution)/shard_map/ppermute | solution.py:35
  43.5 5.6 %collective-permute-start.23 = (bf16[4,4096]{1,0:T(4,128)(2,1)S(1)}, bf16[4,4096]{1,0:T(4,128)(2,1)S(1)}, u32[]{:S(2)}, u32[]{:S(2)}) collective-permute-start(bf16[4,4096]{1,0:T(4,128)(2,1)S(1)} %get-tuple-element.100), channel_id=1, source_target_pairs={{0,8},{1,9},{2,10},{3,11},{4,12},{5,13},{6,14},{7,15},{8,0},{9,1},... | collective-permute-start | bytes 98312 | tf_op jit(solution)/shard_map/ppermute | solution.py:35
  44.6 6.1 %collective-permute-start.14 = (bf16[4,4096]{1,0:T(4,128)(2,1)S(1)}, bf16[4,4096]{1,0:T(4,128)(2,1)S(1)}, u32[]{:S(2)}, u32[]{:S(2)}) collective-permute-start(bf16[4,4096]{1,0:T(4,128)(2,1)S(1)} %get-tuple-element.96), channel_id=1, source_target_pairs={{0,24},{1,25},{2,26},{3,27},{4,28},{5,29},{6,30},{7,31},{8,16},{9,... | collective-permute-start | bytes 98312 | tf_op jit(solution)/shard_map/ppermute | solution.py:35
  48.3 4.8 %collective-permute-start.15 = (bf16[4,4096]{1,0:T(4,128)(2,1)S(1)}, bf16[4,4096]{1,0:T(4,128)(2,1)S(1)}, u32[]{:S(2)}, u32[]{:S(2)}) collective-permute-start(bf16[4,4096]{1,0:T(4,128)(2,1)S(1)} %get-tuple-element.98), channel_id=1, source_target_pairs={{0,16},{1,17},{2,18},{3,19},{4,20},{5,21},{6,22},{7,23},{8,24},{9,... | collective-permute-start | bytes 98312 | tf_op jit(solution)/shard_map/ppermute | solution.py:35
  48.3 4.8 %collective-permute-start.16 = (bf16[4,4096]{1,0:T(4,128)(2,1)S(1)}, bf16[4,4096]{1,0:T(4,128)(2,1)S(1)}, u32[]{:S(2)}, u32[]{:S(2)}) collective-permute-start(bf16[4,4096]{1,0:T(4,128)(2,1)S(1)} %get-tuple-element.97), channel_id=1, source_target_pairs={{0,8},{1,9},{2,10},{3,11},{4,12},{5,13},{6,14},{7,15},{8,0},{9,1},... | collective-permute-start | bytes 98312 | tf_op jit(solution)/shard_map/ppermute | solution.py:35
  54.0 5.8 %collective-permute-start.24 = (bf16[4,4224]{1,0:T(4,128)(2,1)S(1)}, bf16[4,4224]{1,0:T(4,128)(2,1)S(1)}, u32[]{:S(2)}, u32[]{:S(2)}) collective-permute-start(bf16[4,4224]{1,0:T(4,128)(2,1)S(1)} %pad_maximum_fusion.2), channel_id=1, source_target_pairs={{0,24},{1,25},{2,26},{3,27},{4,28},{5,29},{6,30},{7,31},{8,16},{9,... | collective-permute-start | bytes 101384 | tf_op jit(solution)/shard_map/ppermute | solution.py:35
  55.5 4.9 %collective-permute-start.25 = (bf16[4,4224]{1,0:T(4,128)(2,1)S(1)}, bf16[4,4224]{1,0:T(4,128)(2,1)S(1)}, u32[]{:S(2)}, u32[]{:S(2)}) collective-permute-start(bf16[4,4224]{1,0:T(4,128)(2,1)S(1)} %pad_maximum_fusion.2), channel_id=1, source_target_pairs={{0,16},{1,17},{2,18},{3,19},{4,20},{5,21},{6,22},{7,23},{8,24},{9,... | collective-permute-start | bytes 101384 | tf_op jit(solution)/shard_map/ppermute | solution.py:35
  56.1 4.5 %collective-permute-start.26 = (bf16[4,4224]{1,0:T(4,128)(2,1)S(1)}, bf16[4,4224]{1,0:T(4,128)(2,1)S(1)}, u32[]{:S(2)}, u32[]{:S(2)}) collective-permute-start(bf16[4,4224]{1,0:T(4,128)(2,1)S(1)} %pad_maximum_fusion.2), channel_id=1, source_target_pairs={{0,8},{1,9},{2,10},{3,11},{4,12},{5,13},{6,14},{7,15},{8,0},{9,1},... | collective-permute-start | bytes 101384 | tf_op jit(solution)/shard_map/ppermute | solution.py:35
  60.8 6.0 %collective-permute-start.27 = (bf16[16,4224]{1,0:T(8,128)(2,1)S(1)}, bf16[16,4224]{1,0:T(8,128)(2,1)S(1)}, u32[]{:S(2)}, u32[]{:S(2)}) collective-permute-start(bf16[16,4224]{1,0:T(8,128)(2,1)S(1)} %pad_maximum_fusion.refs_0_), channel_id=1, source_target_pairs={{0,6},{1,7},{2,4},{3,5},{4,2},{5,3},{6,0},{7,1},{8,14},{9,15},{10,... | collective-permute-start | bytes 405512 | tf_op jit(solution)/shard_map/ppermute | solution.py:35
  62.9 5.3 %collective-permute-start.28 = (bf16[16,4224]{1,0:T(8,128)(2,1)S(1)}, bf16[16,4224]{1,0:T(8,128)(2,1)S(1)}, u32[]{:S(2)}, u32[]{:S(2)}) collective-permute-start(bf16[16,4224]{1,0:T(8,128)(2,1)S(1)} %pad_maximum_fusion.refs_0_), channel_id=1, source_target_pairs={{0,4},{1,5},{2,6},{3,7},{4,0},{5,1},{6,2},{7,3},{8,12},{9,13},{10,... | collective-permute-start | bytes 405512 | tf_op jit(solution)/shard_map/ppermute | solution.py:35
  63.8 5.0 %collective-permute-start.29 = (bf16[16,4224]{1,0:T(8,128)(2,1)S(1)}, bf16[16,4224]{1,0:T(8,128)(2,1)S(1)}, u32[]{:S(2)}, u32[]{:S(2)}) collective-permute-start(bf16[16,4224]{1,0:T(8,128)(2,1)S(1)} %pad_maximum_fusion.refs_0_), channel_id=1, source_target_pairs={{0,2},{1,3},{2,0},{3,1},{4,6},{5,7},{6,4},{7,5},{8,10},{9,11},{10,... | collective-permute-start | bytes 405512 | tf_op jit(solution)/shard_map/ppermute | solution.py:35
  66.5 2.9 %collective-permute-start.30 = (bf16[16,4224]{1,0:T(8,128)(2,1)S(1)}, bf16[16,4224]{1,0:T(8,128)(2,1)S(1)}, u32[]{:S(2)}, u32[]{:S(2)}) collective-permute-start(bf16[16,4224]{1,0:T(8,128)(2,1)S(1)} %pad_maximum_fusion.refs_0_), channel_id=1, source_target_pairs={{0,1},{1,0},{2,3},{3,2},{4,5},{5,4},{6,7},{7,6},{8,9},{9,8},{10,11... | collective-permute-start | bytes 405512 | tf_op jit(solution)/shard_map/ppermute | solution.py:35
  68.8 1.4 %collective-permute-start.31 = (bf16[16,4224]{1,0:T(8,128)(2,1)S(1)}, bf16[16,4224]{1,0:T(8,128)(2,1)S(1)}, u32[]{:S(2)}, u32[]{:S(2)}) collective-permute-start(bf16[16,4224]{1,0:T(8,128)(2,1)S(1)} %collective-permute-done.27.refs_1_), channel_id=1, source_target_pairs={{0,1},{1,0},{2,3},{3,2},{4,5},{5,4},{6,7},{7,6},{8,9},{9,8},{10,11... | collective-permute-start | bytes 405512 | tf_op jit(solution)/shard_map/ppermute | solution.py:35
  68.9 1.5 %collective-permute-start.32 = (bf16[16,4224]{1,0:T(8,128)(2,1)S(1)}, bf16[16,4224]{1,0:T(8,128)(2,1)S(1)}, u32[]{:S(2)}, u32[]{:S(2)}) collective-permute-start(bf16[16,4224]{1,0:T(8,128)(2,1)S(1)} %collective-permute-done.28.refs_2_), channel_id=1, source_target_pairs={{0,1},{1,0},{2,3},{3,2},{4,5},{5,4},{6,7},{7,6},{8,9},{9,8},{10,11... | collective-permute-start | bytes 405512 | tf_op jit(solution)/shard_map/ppermute | solution.py:35
  69.4 1.4 %collective-permute-start.33 = (bf16[16,4224]{1,0:T(8,128)(2,1)S(1)}, bf16[16,4224]{1,0:T(8,128)(2,1)S(1)}, u32[]{:S(2)}, u32[]{:S(2)}) collective-permute-start(bf16[16,4224]{1,0:T(8,128)(2,1)S(1)} %collective-permute-done.29.refs_3_), channel_id=1, source_target_pairs={{0,1},{1,0},{2,3},{3,2},{4,5},{5,4},{6,7},{7,6},{8,9},{9,8},{10,11... | collective-permute-start | bytes 405512 | tf_op jit(solution)/shard_map/ppermute | solution.py:35
  (9 other events, 77.6 us)

commit v4 on v3

--- a/solution.py
+++ b/solution.py
@@ -50,19 +50,23 @@
     if len(levels) > 1:
         blocks = blocks + [swap(rows, mask) for mask in levels[1]]
     if beside[1] is not None:
-        blocks[1:], beside[1] = tie(blocks[1:], beside[1])
+        blocks[1], beside[1] = tie(blocks[1], beside[1])
     return blocks + [swap(block, mask) for mask in levels[0] for block in blocks], beside
 
 
 def scatter_rows(sums, levels):
+    received = []
     for level in levels:
+        for part in received:
+            sums = sums + part.astype(jnp.float32)
         count = sums.shape[0] // (len(level) + 1)
-        own = sums[:count]
-        for place, mask in enumerate(level):
-            block = sums[(place + 1) * count : (place + 2) * count]
-            own = own + swap(block.astype(jnp.bfloat16), mask).astype(jnp.float32)
-        sums = own
-    return sums
+        blocks = sums[count:].astype(jnp.bfloat16)
+        received = [
+            swap(blocks[place * count : (place + 1) * count], mask)
+            for place, mask in enumerate(level)
+        ]
+        sums = sums[:count]
+    return [sums] + received
 
 
 def row_masks(levels):
@@ -72,13 +76,47 @@
     return masks
 
 
-def split_float(value):
-    pieces = []
-    for _ in range(PIECES):
-        piece = lax.reduce_precision(value, 8, 7)
-        pieces.append(piece)
-        value = value - piece
-    return pieces
+def slope_kernel(parts, *refs):
+    pol_parts, ref_parts = refs[:parts], refs[parts : 2 * parts]
+    states_ref, ids, payload = refs[2 * parts :]
+    count, width = states_ref.shape
+    states = states_ref[...].astype(jnp.float32)
+    chosen = lax.broadcasted_iota(jnp.int32, (count, width), 1) == ids[...]
+
+    def token_logprob(terms):
+        logits = states
+        for term in terms:
+            logits = logits + term[...].astype(jnp.float32)
+        row_peak = jnp.max(logits, axis=1, keepdims=True)
+        total = jnp.sum(jnp.exp(logits - row_peak), axis=1, keepdims=True)
+        log_total = row_peak + jnp.log(total)
+        picked = jnp.sum(jnp.where(chosen, logits, 0.0), axis=1, keepdims=True)
+        return logits, log_total, picked - log_total
+
+    logits, log_total, pol_lp = token_logprob(pol_parts)
+    _, _, ref_lp = token_logprob(ref_parts)
+    slopes = jnp.exp(logits - log_total) - jnp.where(chosen, 1.0, 0.0)
+    payload[:, :width] = slopes.astype(jnp.bfloat16)
+    lane = lax.broadcasted_iota(jnp.int32, (count, LANES), 1)
+    rest = pol_lp - ref_lp
+    extra = jnp.zeros((count, LANES), jnp.float32)
+    for place in range(PIECES):
+        piece = rest.astype(jnp.bfloat16).astype(jnp.float32)
+        extra = jnp.where(lane == place, piece, extra)
+        rest = rest - piece
+    payload[:, width:] = extra.astype(jnp.bfloat16)
+
+
+def slope_rows(pol_parts, ref_parts, states, ids):
+    count, width = states.shape
+    vmem = pl.BlockSpec(memory_space=pltpu.VMEM)
+    return pl.pallas_call(
+        functools.partial(slope_kernel, len(pol_parts)),
+        out_shape=jax.ShapeDtypeStruct((count, width + LANES), jnp.bfloat16),
+        in_specs=[vmem] * (2 * len(pol_parts) + 2),
+        out_specs=vmem,
+        compiler_params=pltpu.CompilerParams(vmem_limit_bytes=FETCH_VMEM),
+    )(*pol_parts, *ref_parts, states, ids)
 
 
 NT = (((1,), (1,)), ((), ()))
@@ -386,26 +424,9 @@
     def reduce_rows(sent, kept):
         return scatter_rows(kept + swap(sent, levels[0][0]).astype(jnp.float32), levels[1:])
 
-    ref_sums = reduce_rows(ref_sent, ref_kept)
-    pol_sums = reduce_rows(pol_sent, pol_kept)
-
-    states = hidden_states.astype(jnp.float32)
-    columns = jnp.arange(width, dtype=jnp.int32)
-    chosen = columns[None, :] == token_ids[:, None]
-
-    def token_logprob(logits):
-        row_peak = jnp.max(logits, axis=1)
-        log_total = row_peak + jnp.log(jnp.sum(jnp.exp(logits - row_peak[:, None]), axis=1))
-        return jnp.sum(jnp.where(chosen, logits, 0.0), axis=1) - log_total, log_total
-
-    logits = states + pol_sums
-    pol_lp, log_total = token_logprob(logits)
-    ref_lp, _ = token_logprob(states + ref_sums)
-    slopes = jnp.exp(logits - log_total[:, None]) - chosen.astype(jnp.float32)
-    extra = jnp.stack(split_float(pol_lp - ref_lp), axis=1)
-    extra = jnp.pad(extra, ((0, 0), (0, LANES - PIECES)))
-    payload = jnp.concatenate([slopes, extra], axis=1).astype(jnp.bfloat16)
-
+    ref_parts = reduce_rows(ref_sent, ref_kept)
+    pol_parts = reduce_rows(pol_sent, pol_kept)
+    payload = slope_rows(pol_parts, ref_parts, hidden_states, token_ids[:, None])
     slope_blocks, (_, down_again) = gather_blocks(payload, levels, (None, fetch([pol_down_w])))
     grad_gate, grad_up, grad_down, advantage = backward(
         slope_blocks,

time: 80.3 us -> 79.2 us (0.986)
  waiting for transfers between devices: 13.7 us -> 12.5 us
    ppermute x34, waiting for transfers between devices: 13.7 us -> 12.5 us  [swap(): return lax.ppermute(values, 'fsdp', [(i, i ^ mask) for i in range(members)])]
  transfers between devices with their start and end apart: 34 -> 34, of which waited for: 21 -> 16; matrix products, arithmetic and copies ran while one was open for 1% -> 1% of each run, Pallas kernels for 18% -> 18%
where the time goes in v4:
time: 79.2 us; the launch traced here: 79 us
  starting transfers between devices  37.1 us (47%)
  Pallas kernels  27.7 us (35%)
  waiting for transfers between devices  12.5 us (16%)
  between operations  0.9 us (1%)
    ppermute x34, starting transfers between devices, swap(): return lax.ppermute(values, 'fsdp', [(i, i ^ mask) for i in range(members)])  37.1 us
    ppermute x34, waiting for transfers between devices, swap(): return lax.ppermute(values, 'fsdp', [(i, i ^ mask) for i in range(members)])  12.5 us
    pallas_call x3, Pallas kernels, fetch(): pl.pallas_call(fetch_kernel, out_shape=[jax.ShapeDtypeStruct(w.shape, w.d...  10.8 us
    pallas_call x1, Pallas kernels, backward(): pl.pallas_call(functools.partial(backward_kernel, len(blocks), chunk, tok...  9.45 us
    pallas_call x2, Pallas kernels, forward_call(): pl.pallas_call(kernel, out_shape=shapes, in_specs=[vmem] * (len(operands)...  7.26 us
  transfers between devices with their start and end apart: 34, of which 16 were waited for; matrix products, arithmetic and copies ran while one was open for 1% of the time, Pallas kernels for 18%

profile of v4, /device:TPU:0, one launch (start us, length us, event | category | flops | bytes accessed | tf_op | source)
XLA Modules:
  0.0 79.0 jit_solution(14807519624762528985)
XLA Ops:
  0.6 5.1 %collective-permute-start = (bf16[4,4096]{1,0:T(4,128)(2,1)}, bf16[4,4096]{1,0:T(4,128)(2,1)S(1)}, u32[]{:S(2)}, u32[]{:S(2)}) collective-permute-start(bf16[4,4096]{1,0:T(4,128)(2,1)} %refs_8_.1), channel_id=1, source_target_pairs={{0,24},{1,25},{2,26},{3,27},{4,28},{5,29},{6,30},{7,31},{8,16},{9,... | collective-permute-start | bytes 98312 | tf_op jit(solution)/shard_map/ppermute | solution.py:35
  5.8 0.6 collective-permute-start.2
  6.4 4.3 %shard_map.156 = (bf16[462,4096]{1,0:T(8,128)(2,1)S(1)}, bf16[462,4096]{1,0:T(8,128)(2,1)S(1)}, bf16[462,4096]{1,0:T(8,128)(2,1)S(1)}) custom-call(bf16[462,4096]{1,0:T(8,128)(2,1)} %bitcast.9, bf16[462,4096]{1,0:T(8,128)(2,1)} %bitcast.10, bf16[462,4096]{1,0:T(8,128)(2,1)} %refs_2_.2), custom_call_target="tpu_custom_call" | custom-call | bytes 11354112 | tf_op jit(solution)/shard_map/pallas_call | solution.py:154
  10.9 2.7 %collective-permute-start.3 = (bf16[16,4096]{1,0:T(8,128)(2,1)S(1)}, bf16[16,4096]{1,0:T(8,128)(2,1)S(1)}, u32[]{:S(2)}, u32[]{:S(2)}) collective-permute-start(bf16[16,4096]{1,0:T(8,128)(2,1)S(1)} %pad_maximum_fusion.1.refs_0_), channel_id=1, source_target_pairs={{0,6},{1,7},{2,4},{3,5},{4,2},{5,3},{6,0},{7,1},{8,14},{9,15},{10,... | collective-permute-start | bytes 393224 | tf_op jit(solution)/shard_map/ppermute | solution.py:35
  14.5 4.3 %shard_map.157 = (bf16[462,4096]{1,0:T(8,128)(2,1)S(1)}, bf16[462,4096]{1,0:T(8,128)(2,1)S(1)}, bf16[462,4096]{1,0:T(8,128)(2,1)S(1)}) custom-call(bf16[462,4096]{1,0:T(8,128)(2,1)} %bitcast.11, bf16[462,4096]{1,0:T(8,128)(2,1)} %bitcast.12, bf16[462,4096]{1,0:T(8,128)(2,1)} %refs_0_.1), custom_call_target="tpu_custom_call" | custom-call | bytes 11354112 | tf_op jit(solution)/shard_map/pallas_call | solution.py:154
  20.9 3.8 %shard_map.158 = (bf16[128,4096]{1,0:T(8,128)(2,1)S(1)}, bf16[64,4096]{1,0:T(8,128)(2,1)S(1)}, f32[64,4096]{1,0:T(8,128)S(1)}) custom-call(bf16[16,4096]{1,0:T(8,128)(2,1)S(1)} %pad_maximum_fusion.1.refs_0_, bf16[16,4096]{1,0:T(8,128)(2,1)S(1)} %collective-permute-done.3.refs_1_, bf16[16,4096]{1,0:T(8,128)(2,1)S(1)} %collective-permute-done.4.refs_2_, ...), custom_call_target="tpu_custom_call" | custom-call | flops 1453326336 | bytes 11354112 | tf_op jit(solution)/shard_map/pallas_call | solution.py:216
  25.1 3.5 %shard_map.159 = (f32[462,128]{1,0:T(8,128)S(1)}, f32[462,128]{1,0:T(8,128)S(1)}, bf16[462,128]{1,0:T(8,128)(2,1)S(1)}, bf16[64,4096]{1,0:T(8,128)(2,1)S(1)}, f32[64,4096]{1,0:T(8,128)S(1)}) custom-call(bf16[128,4096]{1,0:T(8,128)(2,1)S(1)} %get-tuple-element.47.normed.refs_8_, bf16[462,4096]{1,0:T(8,128)(2,1)S(1)} %get-tuple-element.48.refs_0_, ...), custom_call_target="tpu_custom_call" | custom-call | flops 1453326336 | bytes 11354112 | tf_op jit(solution)/shard_map/pallas_call | solution.py:216
  29.0 2.6 %collective-permute-start.18 = (bf16[16,4096]{1,0:T(8,128)(2,1)S(1)}, bf16[16,4096]{1,0:T(8,128)(2,1)S(1)}, u32[]{:S(2)}, u32[]{:S(2)}) collective-permute-start(bf16[16,4096]{1,0:T(8,128)(2,1)S(1)} %get-tuple-element.72), channel_id=1, source_target_pairs={{0,6},{1,7},{2,4},{3,5},{4,2},{5,3},{6,0},{7,1},{8,14},{9,15},{10,... | collective-permute-start | bytes 393224 | tf_op jit(solution)/shard_map/ppermute | solution.py:35
  31.7 0.5 collective-permute-start.19
  32.8 2.6 %collective-permute-start.11 = (bf16[16,4096]{1,0:T(8,128)(2,1)S(1)}, bf16[16,4096]{1,0:T(8,128)(2,1)S(1)}, u32[]{:S(2)}, u32[]{:S(2)}) collective-permute-start(bf16[16,4096]{1,0:T(8,128)(2,1)S(1)} %get-tuple-element.75), channel_id=1, source_target_pairs={{0,6},{1,7},{2,4},{3,5},{4,2},{5,3},{6,0},{7,1},{8,14},{9,15},{10,... | collective-permute-start | bytes 393224 | tf_op jit(solution)/shard_map/ppermute | solution.py:35
  36.0 2.1 %collective-permute-start.13 = (bf16[16,4096]{1,0:T(8,128)(2,1)S(1)}, bf16[16,4096]{1,0:T(8,128)(2,1)S(1)}, u32[]{:S(2)}, u32[]{:S(2)}) collective-permute-start(bf16[16,4096]{1,0:T(8,128)(2,1)S(1)} %get-tuple-element.76), channel_id=1, source_target_pairs={{0,2},{1,3},{2,0},{3,1},{4,6},{5,7},{6,4},{7,5},{8,10},{9,11},{10,... | collective-permute-start | bytes 393224 | tf_op jit(solution)/shard_map/ppermute | solution.py:35
  38.0 1.6 %collective-permute-done.19 = bf16[16,4096]{1,0:T(8,128)(2,1)S(1)} collective-permute-done((bf16[16,4096]{1,0:T(8,128)(2,1)S(1)}, bf16[16,4096]{1,0:T(8,128)(2,1)S(1)}, u32[]{:S(2)}, u32[]{:S(2)}) %collective-permute-start.19) | collective-permute-done | bytes 131104 | tf_op jit(solution)/shard_map/ppermute | solution.py:35
  39.7 3.7 %collective-permute-start.21 = (bf16[4,4096]{1,0:T(4,128)(2,1)S(1)}, bf16[4,4096]{1,0:T(4,128)(2,1)S(1)}, u32[]{:S(2)}, u32[]{:S(2)}) collective-permute-start(bf16[4,4096]{1,0:T(4,128)(2,1)S(1)} %get-tuple-element.80), channel_id=1, source_target_pairs={{0,24},{1,25},{2,26},{3,27},{4,28},{5,29},{6,30},{7,31},{8,16},{9,... | collective-permute-start | bytes 98312 | tf_op jit(solution)/shard_map/ppermute | solution.py:35
  43.4 0.8 collective-permute-start.23
  44.6 3.7 %collective-permute-start.14 = (bf16[4,4096]{1,0:T(4,128)(2,1)S(1)}, bf16[4,4096]{1,0:T(4,128)(2,1)S(1)}, u32[]{:S(2)}, u32[]{:S(2)}) collective-permute-start(bf16[4,4096]{1,0:T(4,128)(2,1)S(1)} %get-tuple-element.83), channel_id=1, source_target_pairs={{0,24},{1,25},{2,26},{3,27},{4,28},{5,29},{6,30},{7,31},{8,16},{9,... | collective-permute-start | bytes 98312 | tf_op jit(solution)/shard_map/ppermute | solution.py:35
  48.2 0.8 collective-permute-start.16
  49.2 1.5 %collective-permute-done.14.refs_1_ = bf16[4,4096]{1,0:T(4,128)(2,1)S(1)} collective-permute-done((bf16[4,4096]{1,0:T(4,128)(2,1)S(1)}, bf16[4,4096]{1,0:T(4,128)(2,1)S(1)}, u32[]{:S(2)}, u32[]{:S(2)}) %collective-permute-start.14) | collective-permute-done | bytes 32800 | tf_op jit(solution)/shard_map/ppermute | solution.py:35
  50.7 2.4 %collective-permute-done.15.refs_2_ = bf16[4,4096]{1,0:T(4,128)(2,1)S(1)} collective-permute-done((bf16[4,4096]{1,0:T(4,128)(2,1)S(1)}, bf16[4,4096]{1,0:T(4,128)(2,1)S(1)}, u32[]{:S(2)}, u32[]{:S(2)}) %collective-permute-start.15) | collective-permute-done | bytes 32800 | tf_op jit(solution)/shard_map/ppermute | solution.py:35
  53.3 1.5 %collective-permute-start.24 = (bf16[4,4224]{1,0:T(4,128)(2,1)S(1)}, bf16[4,4224]{1,0:T(4,128)(2,1)S(1)}, u32[]{:S(2)}, u32[]{:S(2)}) collective-permute-start(bf16[4,4224]{1,0:T(4,128)(2,1)S(1)} %shard_map.160), channel_id=1, source_target_pairs={{0,24},{1,25},{2,26},{3,27},{4,28},{5,29},{6,30},{7,31},{8,16},{9,... | collective-permute-start | bytes 101384 | tf_op jit(solution)/shard_map/ppermute | solution.py:35
  54.9 0.6 collective-permute-start.25
  55.5 2.3 %collective-permute-start.26 = (bf16[4,4224]{1,0:T(4,128)(2,1)S(1)}, bf16[4,4224]{1,0:T(4,128)(2,1)S(1)}, u32[]{:S(2)}, u32[]{:S(2)}) collective-permute-start(bf16[4,4224]{1,0:T(4,128)(2,1)S(1)} %shard_map.160), channel_id=1, source_target_pairs={{0,8},{1,9},{2,10},{3,11},{4,12},{5,13},{6,14},{7,15},{8,0},{9,1},... | collective-permute-start | bytes 101384 | tf_op jit(solution)/shard_map/ppermute | solution.py:35
  57.8 1.3 %collective-permute-done.24 = bf16[4,4224]{1,0:T(4,128)(2,1)S(1)} collective-permute-done((bf16[4,4224]{1,0:T(4,128)(2,1)S(1)}, bf16[4,4224]{1,0:T(4,128)(2,1)S(1)}, u32[]{:S(2)}, u32[]{:S(2)}) %collective-permute-start.24) | collective-permute-done | bytes 33824 | tf_op jit(solution)/shard_map/ppermute | solution.py:35
  59.1 0.6 collective-permute-done.25
  60.2 2.1 %collective-permute-start.27 = (bf16[16,4224]{1,0:T(8,128)(2,1)S(1)}, bf16[16,4224]{1,0:T(8,128)(2,1)S(1)}, u32[]{:S(2)}, u32[]{:S(2)}) collective-permute-start(bf16[16,4224]{1,0:T(8,128)(2,1)S(1)} %pad_maximum_fusion.refs_0_), channel_id=1, source_target_pairs={{0,6},{1,7},{2,4},{3,5},{4,2},{5,3},{6,0},{7,1},{8,14},{9,15},{10,... | collective-permute-start | bytes 405512 | tf_op jit(solution)/shard_map/ppermute | solution.py:35
  62.3 0.9 %collective-permute-start.28 = (bf16[16,4224]{1,0:T(8,128)(2,1)S(1)}, bf16[16,4224]{1,0:T(8,128)(2,1)S(1)}, u32[]{:S(2)}, u32[]{:S(2)}) collective-permute-start(bf16[16,4224]{1,0:T(8,128)(2,1)S(1)} %pad_maximum_fusion.refs_0_), channel_id=1, source_target_pairs={{0,4},{1,5},{2,6},{3,7},{4,0},{5,1},{6,2},{7,3},{8,12},{9,13},{10,... | collective-permute-start | bytes 405512 | tf_op jit(solution)/shard_map/ppermute | solution.py:35
  63.2 0.5 collective-permute-start.29
  63.7 2.1 %shard_map.161.refs_16_ = bf16[462,4096]{1,0:T(8,128)(2,1)S(1)} custom-call(bf16[462,4096]{1,0:T(8,128)(2,1)} %refs_0_.1), custom_call_target="tpu_custom_call" | custom-call | bytes 3784704 | tf_op jit(solution)/shard_map/pallas_call | solution.py:154
  66.4 1.2 %collective-permute-done.28.refs_2_ = bf16[16,4224]{1,0:T(8,128)(2,1)S(1)} collective-permute-done((bf16[16,4224]{1,0:T(8,128)(2,1)S(1)}, bf16[16,4224]{1,0:T(8,128)(2,1)S(1)}, u32[]{:S(2)}, u32[]{:S(2)}) %collective-permute-start.28) | collective-permute-done | bytes 135200 | tf_op jit(solution)/shard_map/ppermute | solution.py:35
  67.6 0.6 collective-permute-done.29.refs_3_
  68.2 0.7 collective-permute-done.32.refs_6_
  69.0 0.6 collective-permute-done.33.refs_7_
  69.6 9.4 %shard_map.162 = (f32[462,4096]{1,0:T(8,128)}, f32[462,4096]{1,0:T(8,128)}, f32[462,4096]{1,0:T(8,128)}, f32[1,32]{1,0:T(1,128)}) custom-call(bf16[16,4224]{1,0:T(8,128)(2,1)S(1)} %pad_maximum_fusion.refs_0_, bf16[16,4224]{1,0:T(8,128)(2,1)S(1)} %collective-permute-done.27.refs_1_, bf16[16,4224]{1,0:T(8,128)(2,1)S(1)} %collective-permute-done.28.refs_2_, ...), custom_call_target="tpu_custom_call" | custom-call | flops 1937768448 | bytes 26492928 | tf_op jit(solution)/shard_map/pallas_call | solution.py:363
  (70 shorter events, 6.9 us)
Async XLA Ops:
  0.6 10.1 %collective-permute-start = (bf16[4,4096]{1,0:T(4,128)(2,1)}, bf16[4,4096]{1,0:T(4,128)(2,1)S(1)}, u32[]{:S(2)}, u32[]{:S(2)}) collective-permute-start(bf16[4,4096]{1,0:T(4,128)(2,1)} %refs_8_.1), channel_id=1, source_target_pairs={{0,24},{1,25},{2,26},{3,27},{4,28},{5,29},{6,30},{7,31},{8,16},{9,... | collective-permute-start | bytes 98312 | tf_op jit(solution)/shard_map/ppermute | solution.py:35
  5.8 5.0 %collective-permute-start.1 = (bf16[4,4096]{1,0:T(4,128)(2,1)}, bf16[4,4096]{1,0:T(4,128)(2,1)S(1)}, u32[]{:S(2)}, u32[]{:S(2)}) collective-permute-start(bf16[4,4096]{1,0:T(4,128)(2,1)} %refs_8_.1), channel_id=1, source_target_pairs={{0,16},{1,17},{2,18},{3,19},{4,20},{5,21},{6,22},{7,23},{8,24},{9,... | collective-permute-start | bytes 98312 | tf_op jit(solution)/shard_map/ppermute | solution.py:35
  5.8 5.0 %collective-permute-start.2 = (bf16[4,4096]{1,0:T(4,128)(2,1)}, bf16[4,4096]{1,0:T(4,128)(2,1)S(1)}, u32[]{:S(2)}, u32[]{:S(2)}) collective-permute-start(bf16[4,4096]{1,0:T(4,128)(2,1)} %refs_8_.1), channel_id=1, source_target_pairs={{0,8},{1,9},{2,10},{3,11},{4,12},{5,13},{6,14},{7,15},{8,0},{9,1},... | collective-permute-start | bytes 98312 | tf_op jit(solution)/shard_map/ppermute | solution.py:35
  10.9 8.0 %collective-permute-start.3 = (bf16[16,4096]{1,0:T(8,128)(2,1)S(1)}, bf16[16,4096]{1,0:T(8,128)(2,1)S(1)}, u32[]{:S(2)}, u32[]{:S(2)}) collective-permute-start(bf16[16,4096]{1,0:T(8,128)(2,1)S(1)} %pad_maximum_fusion.1.refs_0_), channel_id=1, source_target_pairs={{0,6},{1,7},{2,4},{3,5},{4,2},{5,3},{6,0},{7,1},{8,14},{9,15},{10,... | collective-permute-start | bytes 393224 | tf_op jit(solution)/shard_map/ppermute | solution.py:35
  13.6 5.8 %collective-permute-start.4 = (bf16[16,4096]{1,0:T(8,128)(2,1)S(1)}, bf16[16,4096]{1,0:T(8,128)(2,1)S(1)}, u32[]{:S(2)}, u32[]{:S(2)}) collective-permute-start(bf16[16,4096]{1,0:T(8,128)(2,1)S(1)} %pad_maximum_fusion.1.refs_0_), channel_id=1, source_target_pairs={{0,4},{1,5},{2,6},{3,7},{4,0},{5,1},{6,2},{7,3},{8,12},{9,13},{10,... | collective-permute-start | bytes 393224 | tf_op jit(solution)/shard_map/ppermute | solution.py:35
  14.1 5.4 %collective-permute-start.5 = (bf16[16,4096]{1,0:T(8,128)(2,1)S(1)}, bf16[16,4096]{1,0:T(8,128)(2,1)S(1)}, u32[]{:S(2)}, u32[]{:S(2)}) collective-permute-start(bf16[16,4096]{1,0:T(8,128)(2,1)S(1)} %pad_maximum_fusion.1.refs_0_), channel_id=1, source_target_pairs={{0,2},{1,3},{2,0},{3,1},{4,6},{5,7},{6,4},{7,5},{8,10},{9,11},{10,... | collective-permute-start | bytes 393224 | tf_op jit(solution)/shard_map/ppermute | solution.py:35
  18.8 1.4 %collective-permute-start.6 = (bf16[16,4096]{1,0:T(8,128)(2,1)S(1)}, bf16[16,4096]{1,0:T(8,128)(2,1)S(1)}, u32[]{:S(2)}, u32[]{:S(2)}) collective-permute-start(bf16[16,4096]{1,0:T(8,128)(2,1)S(1)} %pad_maximum_fusion.1.refs_0_), channel_id=1, source_target_pairs={{0,1},{1,0},{2,3},{3,2},{4,5},{5,4},{6,7},{7,6},{8,9},{9,8},{10,11... | collective-permute-start | bytes 393224 | tf_op jit(solution)/shard_map/ppermute | solution.py:35
  18.9 1.5 %collective-permute-start.7 = (bf16[16,4096]{1,0:T(8,128)(2,1)S(1)}, bf16[16,4096]{1,0:T(8,128)(2,1)S(1)}, u32[]{:S(2)}, u32[]{:S(2)}) collective-permute-start(bf16[16,4096]{1,0:T(8,128)(2,1)S(1)} %collective-permute-done.3.refs_1_), channel_id=1, source_target_pairs={{0,1},{1,0},{2,3},{3,2},{4,5},{5,4},{6,7},{7,6},{8,9},{9,8},{10,11... | collective-permute-start | bytes 393224 | tf_op jit(solution)/shard_map/ppermute | solution.py:35
  19.5 1.4 %collective-permute-start.9 = (bf16[16,4096]{1,0:T(8,128)(2,1)S(1)}, bf16[16,4096]{1,0:T(8,128)(2,1)S(1)}, u32[]{:S(2)}, u32[]{:S(2)}) collective-permute-start(bf16[16,4096]{1,0:T(8,128)(2,1)S(1)} %collective-permute-done.5.refs_3_), channel_id=1, source_target_pairs={{0,1},{1,0},{2,3},{3,2},{4,5},{5,4},{6,7},{7,6},{8,9},{9,8},{10,11... | collective-permute-start | bytes 393224 | tf_op jit(solution)/shard_map/ppermute | solution.py:35
  24.7 4.1 %collective-permute-start.17 = (bf16[64,4096]{1,0:T(8,128)(2,1)S(1)}, bf16[64,4096]{1,0:T(8,128)(2,1)S(1)}, u32[]{:S(2)}, u32[]{:S(2)}) collective-permute-start(bf16[64,4096]{1,0:T(8,128)(2,1)S(1)} %get-tuple-element.54), channel_id=1, source_target_pairs={{0,1},{1,0},{2,3},{3,2},{4,5},{5,4},{6,7},{7,6},{8,9},{9,8},{10,11... | collective-permute-start | bytes 1572872 | tf_op jit(solution)/shard_map/ppermute | solution.py:35
  28.6 4.0 %collective-permute-start.10 = (bf16[64,4096]{1,0:T(8,128)(2,1)S(1)}, bf16[64,4096]{1,0:T(8,128)(2,1)S(1)}, u32[]{:S(2)}, u32[]{:S(2)}) collective-permute-start(bf16[64,4096]{1,0:T(8,128)(2,1)S(1)} %get-tuple-element.52), channel_id=1, source_target_pairs={{0,1},{1,0},{2,3},{3,2},{4,5},{5,4},{6,7},{7,6},{8,9},{9,8},{10,11... | collective-permute-start | bytes 1572872 | tf_op jit(solution)/shard_map/ppermute | solution.py:35
  29.0 6.9 %collective-permute-start.18 = (bf16[16,4096]{1,0:T(8,128)(2,1)S(1)}, bf16[16,4096]{1,0:T(8,128)(2,1)S(1)}, u32[]{:S(2)}, u32[]{:S(2)}) collective-permute-start(bf16[16,4096]{1,0:T(8,128)(2,1)S(1)} %get-tuple-element.72), channel_id=1, source_target_pairs={{0,6},{1,7},{2,4},{3,5},{4,2},{5,3},{6,0},{7,1},{8,14},{9,15},{10,... | collective-permute-start | bytes 393224 | tf_op jit(solution)/shard_map/ppermute | solution.py:35
  31.7 7.9 %collective-permute-start.19 = (bf16[16,4096]{1,0:T(8,128)(2,1)S(1)}, bf16[16,4096]{1,0:T(8,128)(2,1)S(1)}, u32[]{:S(2)}, u32[]{:S(2)}) collective-permute-start(bf16[16,4096]{1,0:T(8,128)(2,1)S(1)} %get-tuple-element.74), channel_id=1, source_target_pairs={{0,4},{1,5},{2,6},{3,7},{4,0},{5,1},{6,2},{7,3},{8,12},{9,13},{10,... | collective-permute-start | bytes 393224 | tf_op jit(solution)/shard_map/ppermute | solution.py:35
  32.2 7.4 %collective-permute-start.20 = (bf16[16,4096]{1,0:T(8,128)(2,1)S(1)}, bf16[16,4096]{1,0:T(8,128)(2,1)S(1)}, u32[]{:S(2)}, u32[]{:S(2)}) collective-permute-start(bf16[16,4096]{1,0:T(8,128)(2,1)S(1)} %get-tuple-element.73), channel_id=1, source_target_pairs={{0,2},{1,3},{2,0},{3,1},{4,6},{5,7},{6,4},{7,5},{8,10},{9,11},{10,... | collective-permute-start | bytes 393224 | tf_op jit(solution)/shard_map/ppermute | solution.py:35
  32.8 10.6 %collective-permute-start.11 = (bf16[16,4096]{1,0:T(8,128)(2,1)S(1)}, bf16[16,4096]{1,0:T(8,128)(2,1)S(1)}, u32[]{:S(2)}, u32[]{:S(2)}) collective-permute-start(bf16[16,4096]{1,0:T(8,128)(2,1)S(1)} %get-tuple-element.75), channel_id=1, source_target_pairs={{0,6},{1,7},{2,4},{3,5},{4,2},{5,3},{6,0},{7,1},{8,14},{9,15},{10,... | collective-permute-start | bytes 393224 | tf_op jit(solution)/shard_map/ppermute | solution.py:35
  35.4 8.8 %collective-permute-start.12 = (bf16[16,4096]{1,0:T(8,128)(2,1)S(1)}, bf16[16,4096]{1,0:T(8,128)(2,1)S(1)}, u32[]{:S(2)}, u32[]{:S(2)}) collective-permute-start(bf16[16,4096]{1,0:T(8,128)(2,1)S(1)} %get-tuple-element.77), channel_id=1, source_target_pairs={{0,4},{1,5},{2,6},{3,7},{4,0},{5,1},{6,2},{7,3},{8,12},{9,13},{10,... | collective-permute-start | bytes 393224 | tf_op jit(solution)/shard_map/ppermute | solution.py:35
  36.0 8.5 %collective-permute-start.13 = (bf16[16,4096]{1,0:T(8,128)(2,1)S(1)}, bf16[16,4096]{1,0:T(8,128)(2,1)S(1)}, u32[]{:S(2)}, u32[]{:S(2)}) collective-permute-start(bf16[16,4096]{1,0:T(8,128)(2,1)S(1)} %get-tuple-element.76), channel_id=1, source_target_pairs={{0,2},{1,3},{2,0},{3,1},{4,6},{5,7},{6,4},{7,5},{8,10},{9,11},{10,... | collective-permute-start | bytes 393224 | tf_op jit(solution)/shard_map/ppermute | solution.py:35
  39.7 8.5 %collective-permute-start.21 = (bf16[4,4096]{1,0:T(4,128)(2,1)S(1)}, bf16[4,4096]{1,0:T(4,128)(2,1)S(1)}, u32[]{:S(2)}, u32[]{:S(2)}) collective-permute-start(bf16[4,4096]{1,0:T(4,128)(2,1)S(1)} %get-tuple-element.80), channel_id=1, source_target_pairs={{0,24},{1,25},{2,26},{3,27},{4,28},{5,29},{6,30},{7,31},{8,16},{9,... | collective-permute-start | bytes 98312 | tf_op jit(solution)/shard_map/ppermute | solution.py:35
  43.4 5.7 %collective-permute-start.22 = (bf16[4,4096]{1,0:T(4,128)(2,1)S(1)}, bf16[4,4096]{1,0:T(4,128)(2,1)S(1)}, u32[]{:S(2)}, u32[]{:S(2)}) collective-permute-start(bf16[4,4096]{1,0:T(4,128)(2,1)S(1)} %get-tuple-element.79), channel_id=1, source_target_pairs={{0,16},{1,17},{2,18},{3,19},{4,20},{5,21},{6,22},{7,23},{8,24},{9,... | collective-permute-start | bytes 98312 | tf_op jit(solution)/shard_map/ppermute | solution.py:35
  43.4 5.7 %collective-permute-start.23 = (bf16[4,4096]{1,0:T(4,128)(2,1)S(1)}, bf16[4,4096]{1,0:T(4,128)(2,1)S(1)}, u32[]{:S(2)}, u32[]{:S(2)}) collective-permute-start(bf16[4,4096]{1,0:T(4,128)(2,1)S(1)} %get-tuple-element.78), channel_id=1, source_target_pairs={{0,8},{1,9},{2,10},{3,11},{4,12},{5,13},{6,14},{7,15},{8,0},{9,1},... | collective-permute-start | bytes 98312 | tf_op jit(solution)/shard_map/ppermute | solution.py:35
  44.6 6.1 %collective-permute-start.14 = (bf16[4,4096]{1,0:T(4,128)(2,1)S(1)}, bf16[4,4096]{1,0:T(4,128)(2,1)S(1)}, u32[]{:S(2)}, u32[]{:S(2)}) collective-permute-start(bf16[4,4096]{1,0:T(4,128)(2,1)S(1)} %get-tuple-element.83), channel_id=1, source_target_pairs={{0,24},{1,25},{2,26},{3,27},{4,28},{5,29},{6,30},{7,31},{8,16},{9,... | collective-permute-start | bytes 98312 | tf_op jit(solution)/shard_map/ppermute | solution.py:35
  48.2 4.8 %collective-permute-start.15 = (bf16[4,4096]{1,0:T(4,128)(2,1)S(1)}, bf16[4,4096]{1,0:T(4,128)(2,1)S(1)}, u32[]{:S(2)}, u32[]{:S(2)}) collective-permute-start(bf16[4,4096]{1,0:T(4,128)(2,1)S(1)} %get-tuple-element.82), channel_id=1, source_target_pairs={{0,16},{1,17},{2,18},{3,19},{4,20},{5,21},{6,22},{7,23},{8,24},{9,... | collective-permute-start | bytes 98312 | tf_op jit(solution)/shard_map/ppermute | solution.py:35
  48.2 4.8 %collective-permute-start.16 = (bf16[4,4096]{1,0:T(4,128)(2,1)S(1)}, bf16[4,4096]{1,0:T(4,128)(2,1)S(1)}, u32[]{:S(2)}, u32[]{:S(2)}) collective-permute-start(bf16[4,4096]{1,0:T(4,128)(2,1)S(1)} %get-tuple-element.81), channel_id=1, source_target_pairs={{0,8},{1,9},{2,10},{3,11},{4,12},{5,13},{6,14},{7,15},{8,0},{9,1},... | collective-permute-start | bytes 98312 | tf_op jit(solution)/shard_map/ppermute | solution.py:35
  53.3 5.8 %collective-permute-start.24 = (bf16[4,4224]{1,0:T(4,128)(2,1)S(1)}, bf16[4,4224]{1,0:T(4,128)(2,1)S(1)}, u32[]{:S(2)}, u32[]{:S(2)}) collective-permute-start(bf16[4,4224]{1,0:T(4,128)(2,1)S(1)} %shard_map.160), channel_id=1, source_target_pairs={{0,24},{1,25},{2,26},{3,27},{4,28},{5,29},{6,30},{7,31},{8,16},{9,... | collective-permute-start | bytes 101384 | tf_op jit(solution)/shard_map/ppermute | solution.py:35
  54.9 4.9 %collective-permute-start.25 = (bf16[4,4224]{1,0:T(4,128)(2,1)S(1)}, bf16[4,4224]{1,0:T(4,128)(2,1)S(1)}, u32[]{:S(2)}, u32[]{:S(2)}) collective-permute-start(bf16[4,4224]{1,0:T(4,128)(2,1)S(1)} %shard_map.160), channel_id=1, source_target_pairs={{0,16},{1,17},{2,18},{3,19},{4,20},{5,21},{6,22},{7,23},{8,24},{9,... | collective-permute-start | bytes 101384 | tf_op jit(solution)/shard_map/ppermute | solution.py:35
  55.5 4.5 %collective-permute-start.26 = (bf16[4,4224]{1,0:T(4,128)(2,1)S(1)}, bf16[4,4224]{1,0:T(4,128)(2,1)S(1)}, u32[]{:S(2)}, u32[]{:S(2)}) collective-permute-start(bf16[4,4224]{1,0:T(4,128)(2,1)S(1)} %shard_map.160), channel_id=1, source_target_pairs={{0,8},{1,9},{2,10},{3,11},{4,12},{5,13},{6,14},{7,15},{8,0},{9,1},... | collective-permute-start | bytes 101384 | tf_op jit(solution)/shard_map/ppermute | solution.py:35
  60.2 6.0 %collective-permute-start.27 = (bf16[16,4224]{1,0:T(8,128)(2,1)S(1)}, bf16[16,4224]{1,0:T(8,128)(2,1)S(1)}, u32[]{:S(2)}, u32[]{:S(2)}) collective-permute-start(bf16[16,4224]{1,0:T(8,128)(2,1)S(1)} %pad_maximum_fusion.refs_0_), channel_id=1, source_target_pairs={{0,6},{1,7},{2,4},{3,5},{4,2},{5,3},{6,0},{7,1},{8,14},{9,15},{10,... | collective-permute-start | bytes 405512 | tf_op jit(solution)/shard_map/ppermute | solution.py:35
  62.3 5.3 %collective-permute-start.28 = (bf16[16,4224]{1,0:T(8,128)(2,1)S(1)}, bf16[16,4224]{1,0:T(8,128)(2,1)S(1)}, u32[]{:S(2)}, u32[]{:S(2)}) collective-permute-start(bf16[16,4224]{1,0:T(8,128)(2,1)S(1)} %pad_maximum_fusion.refs_0_), channel_id=1, source_target_pairs={{0,4},{1,5},{2,6},{3,7},{4,0},{5,1},{6,2},{7,3},{8,12},{9,13},{10,... | collective-permute-start | bytes 405512 | tf_op jit(solution)/shard_map/ppermute | solution.py:35
  63.2 5.0 %collective-permute-start.29 = (bf16[16,4224]{1,0:T(8,128)(2,1)S(1)}, bf16[16,4224]{1,0:T(8,128)(2,1)S(1)}, u32[]{:S(2)}, u32[]{:S(2)}) collective-permute-start(bf16[16,4224]{1,0:T(8,128)(2,1)S(1)} %pad_maximum_fusion.refs_0_), channel_id=1, source_target_pairs={{0,2},{1,3},{2,0},{3,1},{4,6},{5,7},{6,4},{7,5},{8,10},{9,11},{10,... | collective-permute-start | bytes 405512 | tf_op jit(solution)/shard_map/ppermute | solution.py:35
  65.8 2.4 %collective-permute-start.30 = (bf16[16,4224]{1,0:T(8,128)(2,1)S(1)}, bf16[16,4224]{1,0:T(8,128)(2,1)S(1)}, u32[]{:S(2)}, u32[]{:S(2)}) collective-permute-start(bf16[16,4224]{1,0:T(8,128)(2,1)S(1)} %pad_maximum_fusion.refs_0_), channel_id=1, source_target_pairs={{0,1},{1,0},{2,3},{3,2},{4,5},{5,4},{6,7},{7,6},{8,9},{9,8},{10,11... | collective-permute-start | bytes 405512 | tf_op jit(solution)/shard_map/ppermute | solution.py:35
  66.2 2.0 %collective-permute-start.31 = (bf16[16,4224]{1,0:T(8,128)(2,1)S(1)}, bf16[16,4224]{1,0:T(8,128)(2,1)S(1)}, u32[]{:S(2)}, u32[]{:S(2)}) collective-permute-start(bf16[16,4224]{1,0:T(8,128)(2,1)S(1)} %collective-permute-done.27.refs_1_), channel_id=1, source_target_pairs={{0,1},{1,0},{2,3},{3,2},{4,5},{5,4},{6,7},{7,6},{8,9},{9,8},{10,11... | collective-permute-start | bytes 405512 | tf_op jit(solution)/shard_map/ppermute | solution.py:35
  67.6 1.4 %collective-permute-start.32 = (bf16[16,4224]{1,0:T(8,128)(2,1)S(1)}, bf16[16,4224]{1,0:T(8,128)(2,1)S(1)}, u32[]{:S(2)}, u32[]{:S(2)}) collective-permute-start(bf16[16,4224]{1,0:T(8,128)(2,1)S(1)} %collective-permute-done.28.refs_2_), channel_id=1, source_target_pairs={{0,1},{1,0},{2,3},{3,2},{4,5},{5,4},{6,7},{7,6},{8,9},{9,8},{10,11... | collective-permute-start | bytes 405512 | tf_op jit(solution)/shard_map/ppermute | solution.py:35
  (9 other events, 71.3 us)

commit v5 on v4

--- a/solution.py
+++ b/solution.py
@@ -123,7 +123,7 @@
 NN = (((1,), (0,)), ((), ()))
 
 
-def column_chunk(width, wanted=1024):
+def column_chunk(width, wanted):
     return wanted if width % wanted == 0 else width
 
 
@@ -164,7 +164,7 @@
     )(*[keep_in_hbm(w) for w in weights])
 
 
-def forward_model(weights, normed, hidden_rows, sent, kept, chunk):
+def forward_model(weights, normed, hidden_rows, sent, kept):
     gate_w, up_w, down_w = weights
     half = kept.shape[0]
     gate = dot(gate_w[...], normed[...], NT)
@@ -172,18 +172,13 @@
     hidden = gate * (1.0 / (1.0 + jnp.exp(-gate))) * up
     hidden_rows[...] = hidden.T.astype(jnp.bfloat16)
 
-    def outer(step, _):
-        columns = pl.ds(pl.multiple_of(step * chunk, chunk), chunk)
-        part = dot(hidden_rows[...], down_w[:, columns], NN)
-        kept[:, columns] = part[:half]
-        sent[:, columns] = part[half:].astype(jnp.bfloat16)
-        return 0
-
-    lax.fori_loop(0, normed.shape[1] // chunk, outer, 0)
+    part = dot(hidden_rows[...], down_w[...], NN)
+    kept[...] = part[:half]
+    sent[...] = part[half:].astype(jnp.bfloat16)
     return gate, up, hidden
 
 
-def reference_kernel(block_count, chunk, *refs):
+def reference_kernel(block_count, *refs):
     blocks = refs[:block_count]
     gain, *weights = refs[block_count : block_count + 4]
     normed, sent, kept, hidden_rows = refs[block_count + 4 :]
@@ -194,13 +189,13 @@
         normed[place * height : (place + 1) * height, :] = (values * factor * gain[...]).astype(
             jnp.bfloat16
         )
-    forward_model(weights, normed, hidden_rows, sent, kept, chunk)
-
-
-def policy_kernel(chunk, normed, *refs):
+    forward_model(weights, normed, hidden_rows, sent, kept)
+
+
+def policy_kernel(normed, *refs):
     weights = refs[:3]
     gate_out, up_out, hidden_out, sent, kept, hidden_rows = refs[3:]
-    gate, up, hidden = forward_model(weights, normed, hidden_rows, sent, kept, chunk)
+    gate, up, hidden = forward_model(weights, normed, hidden_rows, sent, kept)
     gate_out[...] = gate
     up_out[...] = up
     hidden_out[...] = hidden.astype(jnp.bfloat16)
@@ -232,7 +227,7 @@
     width = blocks[0].shape[1]
     tokens = sum(block.shape[0] for block in blocks)
     return forward_call(
-        functools.partial(reference_kernel, len(blocks), column_chunk(width)),
+        functools.partial(reference_kernel, len(blocks)),
         blocks + [gain],
         [jax.ShapeDtypeStruct((tokens, width), jnp.bfloat16)],
         weights,
@@ -244,7 +239,7 @@
     tokens, width = normed.shape
     units = weights[0].shape[0]
     return forward_call(
-        functools.partial(policy_kernel, column_chunk(width)),
+        policy_kernel,
         [normed],
         [jax.ShapeDtypeStruct((units, tokens), jnp.float32)] * 2
         + [jax.ShapeDtypeStruct((units, tokens), jnp.bfloat16)],

time: 79.2 us -> 78 us (0.985)
  Pallas kernels: 27.7 us -> 26.5 us
    pallas_call x2, Pallas kernels: 7.26 us -> 6.06 us  [forward_call(): pl.pallas_call(kernel, out_shape=shapes, in_specs=[vmem] * (len(operands)...]
where the time goes in v5:
time: 78 us; the launch traced here: 77.8 us
  starting transfers between devices  37 us (47%)
  Pallas kernels  26.5 us (34%)
  waiting for transfers between devices  12.5 us (16%)
  between operations  0.9 us (1%)
    ppermute x34, starting transfers between devices, swap(): return lax.ppermute(values, 'fsdp', [(i, i ^ mask) for i in range(members)])  37 us
    ppermute x34, waiting for transfers between devices, swap(): return lax.ppermute(values, 'fsdp', [(i, i ^ mask) for i in range(members)])  12.5 us
    pallas_call x3, Pallas kernels, fetch(): pl.pallas_call(fetch_kernel, out_shape=[jax.ShapeDtypeStruct(w.shape, w.d...  10.8 us
    pallas_call x1, Pallas kernels, backward(): pl.pallas_call(functools.partial(backward_kernel, len(blocks), chunk, tok...  9.44 us
    pallas_call x2, Pallas kernels, forward_call(): pl.pallas_call(kernel, out_shape=shapes, in_specs=[vmem] * (len(operands)...  6.06 us
  transfers between devices with their start and end apart: 34, of which 16 were waited for; matrix products, arithmetic and copies ran while one was open for 1% of the time, Pallas kernels for 18%

profile of v5, /device:TPU:0, one launch (start us, length us, event | category | flops | bytes accessed | tf_op | source)
XLA Modules:
  0.0 77.8 jit_solution(773054521006230808)
XLA Ops:
  0.6 5.1 %collective-permute-start = (bf16[4,4096]{1,0:T(4,128)(2,1)}, bf16[4,4096]{1,0:T(4,128)(2,1)S(1)}, u32[]{:S(2)}, u32[]{:S(2)}) collective-permute-start(bf16[4,4096]{1,0:T(4,128)(2,1)} %refs_8_.1), channel_id=1, source_target_pairs={{0,24},{1,25},{2,26},{3,27},{4,28},{5,29},{6,30},{7,31},{8,16},{9,... | collective-permute-start | bytes 98312 | tf_op jit(solution)/shard_map/ppermute | solution.py:35
  5.8 0.6 collective-permute-start.2
  6.4 4.3 %shard_map.156 = (bf16[462,4096]{1,0:T(8,128)(2,1)S(1)}, bf16[462,4096]{1,0:T(8,128)(2,1)S(1)}, bf16[462,4096]{1,0:T(8,128)(2,1)S(1)}) custom-call(bf16[462,4096]{1,0:T(8,128)(2,1)} %bitcast.9, bf16[462,4096]{1,0:T(8,128)(2,1)} %bitcast.10, bf16[462,4096]{1,0:T(8,128)(2,1)} %refs_2_.2), custom_call_target="tpu_custom_call" | custom-call | bytes 11354112 | tf_op jit(solution)/shard_map/pallas_call | solution.py:154
  10.9 2.7 %collective-permute-start.3 = (bf16[16,4096]{1,0:T(8,128)(2,1)S(1)}, bf16[16,4096]{1,0:T(8,128)(2,1)S(1)}, u32[]{:S(2)}, u32[]{:S(2)}) collective-permute-start(bf16[16,4096]{1,0:T(8,128)(2,1)S(1)} %pad_maximum_fusion.1.refs_0_), channel_id=1, source_target_pairs={{0,6},{1,7},{2,4},{3,5},{4,2},{5,3},{6,0},{7,1},{8,14},{9,15},{10,... | collective-permute-start | bytes 393224 | tf_op jit(solution)/shard_map/ppermute | solution.py:35
  14.5 4.3 %shard_map.157 = (bf16[462,4096]{1,0:T(8,128)(2,1)S(1)}, bf16[462,4096]{1,0:T(8,128)(2,1)S(1)}, bf16[462,4096]{1,0:T(8,128)(2,1)S(1)}) custom-call(bf16[462,4096]{1,0:T(8,128)(2,1)} %bitcast.11, bf16[462,4096]{1,0:T(8,128)(2,1)} %bitcast.12, bf16[462,4096]{1,0:T(8,128)(2,1)} %refs_0_.1), custom_call_target="tpu_custom_call" | custom-call | bytes 11354112 | tf_op jit(solution)/shard_map/pallas_call | solution.py:154
  20.9 3.2 %shard_map.158 = (bf16[128,4096]{1,0:T(8,128)(2,1)S(1)}, bf16[64,4096]{1,0:T(8,128)(2,1)S(1)}, f32[64,4096]{1,0:T(8,128)S(1)}) custom-call(bf16[16,4096]{1,0:T(8,128)(2,1)S(1)} %pad_maximum_fusion.1.refs_0_, bf16[16,4096]{1,0:T(8,128)(2,1)S(1)} %collective-permute-done.3.refs_1_, bf16[16,4096]{1,0:T(8,128)(2,1)S(1)} %collective-permute-done.4.refs_2_, ...), custom_call_target="tpu_custom_call" | custom-call | flops 1453326336 | bytes 11354112 | tf_op jit(solution)/shard_map/pallas_call | solution.py:211
  24.5 2.9 %shard_map.159 = (f32[462,128]{1,0:T(8,128)S(1)}, f32[462,128]{1,0:T(8,128)S(1)}, bf16[462,128]{1,0:T(8,128)(2,1)S(1)}, bf16[64,4096]{1,0:T(8,128)(2,1)S(1)}, f32[64,4096]{1,0:T(8,128)S(1)}) custom-call(bf16[128,4096]{1,0:T(8,128)(2,1)S(1)} %get-tuple-element.47.normed.refs_8_, bf16[462,4096]{1,0:T(8,128)(2,1)S(1)} %get-tuple-element.48.refs_0_, ...), custom_call_target="tpu_custom_call" | custom-call | flops 1453326336 | bytes 11354112 | tf_op jit(solution)/shard_map/pallas_call | solution.py:211
  27.8 2.6 %collective-permute-start.18 = (bf16[16,4096]{1,0:T(8,128)(2,1)S(1)}, bf16[16,4096]{1,0:T(8,128)(2,1)S(1)}, u32[]{:S(2)}, u32[]{:S(2)}) collective-permute-start(bf16[16,4096]{1,0:T(8,128)(2,1)S(1)} %get-tuple-element.72), channel_id=1, source_target_pairs={{0,6},{1,7},{2,4},{3,5},{4,2},{5,3},{6,0},{7,1},{8,14},{9,15},{10,... | collective-permute-start | bytes 393224 | tf_op jit(solution)/shard_map/ppermute | solution.py:35
  30.5 0.5 collective-permute-start.19
  31.6 2.6 %collective-permute-start.11 = (bf16[16,4096]{1,0:T(8,128)(2,1)S(1)}, bf16[16,4096]{1,0:T(8,128)(2,1)S(1)}, u32[]{:S(2)}, u32[]{:S(2)}) collective-permute-start(bf16[16,4096]{1,0:T(8,128)(2,1)S(1)} %get-tuple-element.75), channel_id=1, source_target_pairs={{0,6},{1,7},{2,4},{3,5},{4,2},{5,3},{6,0},{7,1},{8,14},{9,15},{10,... | collective-permute-start | bytes 393224 | tf_op jit(solution)/shard_map/ppermute | solution.py:35
  34.8 2.1 %collective-permute-start.13 = (bf16[16,4096]{1,0:T(8,128)(2,1)S(1)}, bf16[16,4096]{1,0:T(8,128)(2,1)S(1)}, u32[]{:S(2)}, u32[]{:S(2)}) collective-permute-start(bf16[16,4096]{1,0:T(8,128)(2,1)S(1)} %get-tuple-element.76), channel_id=1, source_target_pairs={{0,2},{1,3},{2,0},{3,1},{4,6},{5,7},{6,4},{7,5},{8,10},{9,11},{10,... | collective-permute-start | bytes 393224 | tf_op jit(solution)/shard_map/ppermute | solution.py:35
  36.8 1.6 %collective-permute-done.19 = bf16[16,4096]{1,0:T(8,128)(2,1)S(1)} collective-permute-done((bf16[16,4096]{1,0:T(8,128)(2,1)S(1)}, bf16[16,4096]{1,0:T(8,128)(2,1)S(1)}, u32[]{:S(2)}, u32[]{:S(2)}) %collective-permute-start.19) | collective-permute-done | bytes 131104 | tf_op jit(solution)/shard_map/ppermute | solution.py:35
  38.5 3.7 %collective-permute-start.21 = (bf16[4,4096]{1,0:T(4,128)(2,1)S(1)}, bf16[4,4096]{1,0:T(4,128)(2,1)S(1)}, u32[]{:S(2)}, u32[]{:S(2)}) collective-permute-start(bf16[4,4096]{1,0:T(4,128)(2,1)S(1)} %get-tuple-element.80), channel_id=1, source_target_pairs={{0,24},{1,25},{2,26},{3,27},{4,28},{5,29},{6,30},{7,31},{8,16},{9,... | collective-permute-start | bytes 98312 | tf_op jit(solution)/shard_map/ppermute | solution.py:35
  42.2 0.8 collective-permute-start.23
  43.3 3.7 %collective-permute-start.14 = (bf16[4,4096]{1,0:T(4,128)(2,1)S(1)}, bf16[4,4096]{1,0:T(4,128)(2,1)S(1)}, u32[]{:S(2)}, u32[]{:S(2)}) collective-permute-start(bf16[4,4096]{1,0:T(4,128)(2,1)S(1)} %get-tuple-element.83), channel_id=1, source_target_pairs={{0,24},{1,25},{2,26},{3,27},{4,28},{5,29},{6,30},{7,31},{8,16},{9,... | collective-permute-start | bytes 98312 | tf_op jit(solution)/shard_map/ppermute | solution.py:35
  47.0 0.8 collective-permute-start.16
  48.0 1.5 %collective-permute-done.14.refs_1_ = bf16[4,4096]{1,0:T(4,128)(2,1)S(1)} collective-permute-done((bf16[4,4096]{1,0:T(4,128)(2,1)S(1)}, bf16[4,4096]{1,0:T(4,128)(2,1)S(1)}, u32[]{:S(2)}, u32[]{:S(2)}) %collective-permute-start.14) | collective-permute-done | bytes 32800 | tf_op jit(solution)/shard_map/ppermute | solution.py:35
  49.5 2.4 %collective-permute-done.15.refs_2_ = bf16[4,4096]{1,0:T(4,128)(2,1)S(1)} collective-permute-done((bf16[4,4096]{1,0:T(4,128)(2,1)S(1)}, bf16[4,4096]{1,0:T(4,128)(2,1)S(1)}, u32[]{:S(2)}, u32[]{:S(2)}) %collective-permute-start.15) | collective-permute-done | bytes 32800 | tf_op jit(solution)/shard_map/ppermute | solution.py:35
  52.1 1.5 %collective-permute-start.24 = (bf16[4,4224]{1,0:T(4,128)(2,1)S(1)}, bf16[4,4224]{1,0:T(4,128)(2,1)S(1)}, u32[]{:S(2)}, u32[]{:S(2)}) collective-permute-start(bf16[4,4224]{1,0:T(4,128)(2,1)S(1)} %shard_map.160), channel_id=1, source_target_pairs={{0,24},{1,25},{2,26},{3,27},{4,28},{5,29},{6,30},{7,31},{8,16},{9,... | collective-permute-start | bytes 101384 | tf_op jit(solution)/shard_map/ppermute | solution.py:35
  53.6 0.6 collective-permute-start.25
  54.3 2.3 %collective-permute-start.26 = (bf16[4,4224]{1,0:T(4,128)(2,1)S(1)}, bf16[4,4224]{1,0:T(4,128)(2,1)S(1)}, u32[]{:S(2)}, u32[]{:S(2)}) collective-permute-start(bf16[4,4224]{1,0:T(4,128)(2,1)S(1)} %shard_map.160), channel_id=1, source_target_pairs={{0,8},{1,9},{2,10},{3,11},{4,12},{5,13},{6,14},{7,15},{8,0},{9,1},... | collective-permute-start | bytes 101384 | tf_op jit(solution)/shard_map/ppermute | solution.py:35
  56.6 1.3 %collective-permute-done.24 = bf16[4,4224]{1,0:T(4,128)(2,1)S(1)} collective-permute-done((bf16[4,4224]{1,0:T(4,128)(2,1)S(1)}, bf16[4,4224]{1,0:T(4,128)(2,1)S(1)}, u32[]{:S(2)}, u32[]{:S(2)}) %collective-permute-start.24) | collective-permute-done | bytes 33824 | tf_op jit(solution)/shard_map/ppermute | solution.py:35
  57.9 0.6 collective-permute-done.25
  59.0 2.1 %collective-permute-start.27 = (bf16[16,4224]{1,0:T(8,128)(2,1)S(1)}, bf16[16,4224]{1,0:T(8,128)(2,1)S(1)}, u32[]{:S(2)}, u32[]{:S(2)}) collective-permute-start(bf16[16,4224]{1,0:T(8,128)(2,1)S(1)} %pad_maximum_fusion.refs_0_), channel_id=1, source_target_pairs={{0,6},{1,7},{2,4},{3,5},{4,2},{5,3},{6,0},{7,1},{8,14},{9,15},{10,... | collective-permute-start | bytes 405512 | tf_op jit(solution)/shard_map/ppermute | solution.py:35
  61.1 0.9 %collective-permute-start.28 = (bf16[16,4224]{1,0:T(8,128)(2,1)S(1)}, bf16[16,4224]{1,0:T(8,128)(2,1)S(1)}, u32[]{:S(2)}, u32[]{:S(2)}) collective-permute-start(bf16[16,4224]{1,0:T(8,128)(2,1)S(1)} %pad_maximum_fusion.refs_0_), channel_id=1, source_target_pairs={{0,4},{1,5},{2,6},{3,7},{4,0},{5,1},{6,2},{7,3},{8,12},{9,13},{10,... | collective-permute-start | bytes 405512 | tf_op jit(solution)/shard_map/ppermute | solution.py:35
  62.0 0.5 collective-permute-start.29
  62.5 2.1 %shard_map.161.refs_16_ = bf16[462,4096]{1,0:T(8,128)(2,1)S(1)} custom-call(bf16[462,4096]{1,0:T(8,128)(2,1)} %refs_0_.1), custom_call_target="tpu_custom_call" | custom-call | bytes 3784704 | tf_op jit(solution)/shard_map/pallas_call | solution.py:154
  65.2 1.2 %collective-permute-done.28.refs_2_ = bf16[16,4224]{1,0:T(8,128)(2,1)S(1)} collective-permute-done((bf16[16,4224]{1,0:T(8,128)(2,1)S(1)}, bf16[16,4224]{1,0:T(8,128)(2,1)S(1)}, u32[]{:S(2)}, u32[]{:S(2)}) %collective-permute-start.28) | collective-permute-done | bytes 135200 | tf_op jit(solution)/shard_map/ppermute | solution.py:35
  66.4 0.6 collective-permute-done.29.refs_3_
  67.0 0.7 collective-permute-done.32.refs_6_
  67.7 0.6 collective-permute-done.33.refs_7_
  68.4 9.4 %shard_map.162 = (f32[462,4096]{1,0:T(8,128)}, f32[462,4096]{1,0:T(8,128)}, f32[462,4096]{1,0:T(8,128)}, f32[1,32]{1,0:T(1,128)}) custom-call(bf16[16,4224]{1,0:T(8,128)(2,1)S(1)} %pad_maximum_fusion.refs_0_, bf16[16,4224]{1,0:T(8,128)(2,1)S(1)} %collective-permute-done.27.refs_1_, bf16[16,4224]{1,0:T(8,128)(2,1)S(1)} %collective-permute-done.28.refs_2_, ...), custom_call_target="tpu_custom_call" | custom-call | flops 1937768448 | bytes 26492928 | tf_op jit(solution)/shard_map/pallas_call | solution.py:358
  (70 shorter events, 6.9 us)
Async XLA Ops:
  0.6 10.1 %collective-permute-start = (bf16[4,4096]{1,0:T(4,128)(2,1)}, bf16[4,4096]{1,0:T(4,128)(2,1)S(1)}, u32[]{:S(2)}, u32[]{:S(2)}) collective-permute-start(bf16[4,4096]{1,0:T(4,128)(2,1)} %refs_8_.1), channel_id=1, source_target_pairs={{0,24},{1,25},{2,26},{3,27},{4,28},{5,29},{6,30},{7,31},{8,16},{9,... | collective-permute-start | bytes 98312 | tf_op jit(solution)/shard_map/ppermute | solution.py:35
  5.8 5.0 %collective-permute-start.1 = (bf16[4,4096]{1,0:T(4,128)(2,1)}, bf16[4,4096]{1,0:T(4,128)(2,1)S(1)}, u32[]{:S(2)}, u32[]{:S(2)}) collective-permute-start(bf16[4,4096]{1,0:T(4,128)(2,1)} %refs_8_.1), channel_id=1, source_target_pairs={{0,16},{1,17},{2,18},{3,19},{4,20},{5,21},{6,22},{7,23},{8,24},{9,... | collective-permute-start | bytes 98312 | tf_op jit(solution)/shard_map/ppermute | solution.py:35
  5.8 5.0 %collective-permute-start.2 = (bf16[4,4096]{1,0:T(4,128)(2,1)}, bf16[4,4096]{1,0:T(4,128)(2,1)S(1)}, u32[]{:S(2)}, u32[]{:S(2)}) collective-permute-start(bf16[4,4096]{1,0:T(4,128)(2,1)} %refs_8_.1), channel_id=1, source_target_pairs={{0,8},{1,9},{2,10},{3,11},{4,12},{5,13},{6,14},{7,15},{8,0},{9,1},... | collective-permute-start | bytes 98312 | tf_op jit(solution)/shard_map/ppermute | solution.py:35
  10.9 8.0 %collective-permute-start.3 = (bf16[16,4096]{1,0:T(8,128)(2,1)S(1)}, bf16[16,4096]{1,0:T(8,128)(2,1)S(1)}, u32[]{:S(2)}, u32[]{:S(2)}) collective-permute-start(bf16[16,4096]{1,0:T(8,128)(2,1)S(1)} %pad_maximum_fusion.1.refs_0_), channel_id=1, source_target_pairs={{0,6},{1,7},{2,4},{3,5},{4,2},{5,3},{6,0},{7,1},{8,14},{9,15},{10,... | collective-permute-start | bytes 393224 | tf_op jit(solution)/shard_map/ppermute | solution.py:35
  13.6 5.8 %collective-permute-start.4 = (bf16[16,4096]{1,0:T(8,128)(2,1)S(1)}, bf16[16,4096]{1,0:T(8,128)(2,1)S(1)}, u32[]{:S(2)}, u32[]{:S(2)}) collective-permute-start(bf16[16,4096]{1,0:T(8,128)(2,1)S(1)} %pad_maximum_fusion.1.refs_0_), channel_id=1, source_target_pairs={{0,4},{1,5},{2,6},{3,7},{4,0},{5,1},{6,2},{7,3},{8,12},{9,13},{10,... | collective-permute-start | bytes 393224 | tf_op jit(solution)/shard_map/ppermute | solution.py:35
  14.1 5.4 %collective-permute-start.5 = (bf16[16,4096]{1,0:T(8,128)(2,1)S(1)}, bf16[16,4096]{1,0:T(8,128)(2,1)S(1)}, u32[]{:S(2)}, u32[]{:S(2)}) collective-permute-start(bf16[16,4096]{1,0:T(8,128)(2,1)S(1)} %pad_maximum_fusion.1.refs_0_), channel_id=1, source_target_pairs={{0,2},{1,3},{2,0},{3,1},{4,6},{5,7},{6,4},{7,5},{8,10},{9,11},{10,... | collective-permute-start | bytes 393224 | tf_op jit(solution)/shard_map/ppermute | solution.py:35
  18.8 1.4 %collective-permute-start.6 = (bf16[16,4096]{1,0:T(8,128)(2,1)S(1)}, bf16[16,4096]{1,0:T(8,128)(2,1)S(1)}, u32[]{:S(2)}, u32[]{:S(2)}) collective-permute-start(bf16[16,4096]{1,0:T(8,128)(2,1)S(1)} %pad_maximum_fusion.1.refs_0_), channel_id=1, source_target_pairs={{0,1},{1,0},{2,3},{3,2},{4,5},{5,4},{6,7},{7,6},{8,9},{9,8},{10,11... | collective-permute-start | bytes 393224 | tf_op jit(solution)/shard_map/ppermute | solution.py:35
  18.9 1.5 %collective-permute-start.7 = (bf16[16,4096]{1,0:T(8,128)(2,1)S(1)}, bf16[16,4096]{1,0:T(8,128)(2,1)S(1)}, u32[]{:S(2)}, u32[]{:S(2)}) collective-permute-start(bf16[16,4096]{1,0:T(8,128)(2,1)S(1)} %collective-permute-done.3.refs_1_), channel_id=1, source_target_pairs={{0,1},{1,0},{2,3},{3,2},{4,5},{5,4},{6,7},{7,6},{8,9},{9,8},{10,11... | collective-permute-start | bytes 393224 | tf_op jit(solution)/shard_map/ppermute | solution.py:35
  19.5 1.4 %collective-permute-start.9 = (bf16[16,4096]{1,0:T(8,128)(2,1)S(1)}, bf16[16,4096]{1,0:T(8,128)(2,1)S(1)}, u32[]{:S(2)}, u32[]{:S(2)}) collective-permute-start(bf16[16,4096]{1,0:T(8,128)(2,1)S(1)} %collective-permute-done.5.refs_3_), channel_id=1, source_target_pairs={{0,1},{1,0},{2,3},{3,2},{4,5},{5,4},{6,7},{7,6},{8,9},{9,8},{10,11... | collective-permute-start | bytes 393224 | tf_op jit(solution)/shard_map/ppermute | solution.py:35
  24.1 3.5 %collective-permute-start.17 = (bf16[64,4096]{1,0:T(8,128)(2,1)S(1)}, bf16[64,4096]{1,0:T(8,128)(2,1)S(1)}, u32[]{:S(2)}, u32[]{:S(2)}) collective-permute-start(bf16[64,4096]{1,0:T(8,128)(2,1)S(1)} %get-tuple-element.54), channel_id=1, source_target_pairs={{0,1},{1,0},{2,3},{3,2},{4,5},{5,4},{6,7},{7,6},{8,9},{9,8},{10,11... | collective-permute-start | bytes 1572872 | tf_op jit(solution)/shard_map/ppermute | solution.py:35
  27.4 4.0 %collective-permute-start.10 = (bf16[64,4096]{1,0:T(8,128)(2,1)S(1)}, bf16[64,4096]{1,0:T(8,128)(2,1)S(1)}, u32[]{:S(2)}, u32[]{:S(2)}) collective-permute-start(bf16[64,4096]{1,0:T(8,128)(2,1)S(1)} %get-tuple-element.52), channel_id=1, source_target_pairs={{0,1},{1,0},{2,3},{3,2},{4,5},{5,4},{6,7},{7,6},{8,9},{9,8},{10,11... | collective-permute-start | bytes 1572872 | tf_op jit(solution)/shard_map/ppermute | solution.py:35
  27.8 6.9 %collective-permute-start.18 = (bf16[16,4096]{1,0:T(8,128)(2,1)S(1)}, bf16[16,4096]{1,0:T(8,128)(2,1)S(1)}, u32[]{:S(2)}, u32[]{:S(2)}) collective-permute-start(bf16[16,4096]{1,0:T(8,128)(2,1)S(1)} %get-tuple-element.72), channel_id=1, source_target_pairs={{0,6},{1,7},{2,4},{3,5},{4,2},{5,3},{6,0},{7,1},{8,14},{9,15},{10,... | collective-permute-start | bytes 393224 | tf_op jit(solution)/shard_map/ppermute | solution.py:35
  30.5 7.9 %collective-permute-start.19 = (bf16[16,4096]{1,0:T(8,128)(2,1)S(1)}, bf16[16,4096]{1,0:T(8,128)(2,1)S(1)}, u32[]{:S(2)}, u32[]{:S(2)}) collective-permute-start(bf16[16,4096]{1,0:T(8,128)(2,1)S(1)} %get-tuple-element.74), channel_id=1, source_target_pairs={{0,4},{1,5},{2,6},{3,7},{4,0},{5,1},{6,2},{7,3},{8,12},{9,13},{10,... | collective-permute-start | bytes 393224 | tf_op jit(solution)/shard_map/ppermute | solution.py:35
  31.0 7.4 %collective-permute-start.20 = (bf16[16,4096]{1,0:T(8,128)(2,1)S(1)}, bf16[16,4096]{1,0:T(8,128)(2,1)S(1)}, u32[]{:S(2)}, u32[]{:S(2)}) collective-permute-start(bf16[16,4096]{1,0:T(8,128)(2,1)S(1)} %get-tuple-element.73), channel_id=1, source_target_pairs={{0,2},{1,3},{2,0},{3,1},{4,6},{5,7},{6,4},{7,5},{8,10},{9,11},{10,... | collective-permute-start | bytes 393224 | tf_op jit(solution)/shard_map/ppermute | solution.py:35
  31.6 10.7 %collective-permute-start.11 = (bf16[16,4096]{1,0:T(8,128)(2,1)S(1)}, bf16[16,4096]{1,0:T(8,128)(2,1)S(1)}, u32[]{:S(2)}, u32[]{:S(2)}) collective-permute-start(bf16[16,4096]{1,0:T(8,128)(2,1)S(1)} %get-tuple-element.75), channel_id=1, source_target_pairs={{0,6},{1,7},{2,4},{3,5},{4,2},{5,3},{6,0},{7,1},{8,14},{9,15},{10,... | collective-permute-start | bytes 393224 | tf_op jit(solution)/shard_map/ppermute | solution.py:35
  34.2 8.8 %collective-permute-start.12 = (bf16[16,4096]{1,0:T(8,128)(2,1)S(1)}, bf16[16,4096]{1,0:T(8,128)(2,1)S(1)}, u32[]{:S(2)}, u32[]{:S(2)}) collective-permute-start(bf16[16,4096]{1,0:T(8,128)(2,1)S(1)} %get-tuple-element.77), channel_id=1, source_target_pairs={{0,4},{1,5},{2,6},{3,7},{4,0},{5,1},{6,2},{7,3},{8,12},{9,13},{10,... | collective-permute-start | bytes 393224 | tf_op jit(solution)/shard_map/ppermute | solution.py:35
  34.8 8.5 %collective-permute-start.13 = (bf16[16,4096]{1,0:T(8,128)(2,1)S(1)}, bf16[16,4096]{1,0:T(8,128)(2,1)S(1)}, u32[]{:S(2)}, u32[]{:S(2)}) collective-permute-start(bf16[16,4096]{1,0:T(8,128)(2,1)S(1)} %get-tuple-element.76), channel_id=1, source_target_pairs={{0,2},{1,3},{2,0},{3,1},{4,6},{5,7},{6,4},{7,5},{8,10},{9,11},{10,... | collective-permute-start | bytes 393224 | tf_op jit(solution)/shard_map/ppermute | solution.py:35
  38.5 8.5 %collective-permute-start.21 = (bf16[4,4096]{1,0:T(4,128)(2,1)S(1)}, bf16[4,4096]{1,0:T(4,128)(2,1)S(1)}, u32[]{:S(2)}, u32[]{:S(2)}) collective-permute-start(bf16[4,4096]{1,0:T(4,128)(2,1)S(1)} %get-tuple-element.80), channel_id=1, source_target_pairs={{0,24},{1,25},{2,26},{3,27},{4,28},{5,29},{6,30},{7,31},{8,16},{9,... | collective-permute-start | bytes 98312 | tf_op jit(solution)/shard_map/ppermute | solution.py:35
  42.2 5.7 %collective-permute-start.22 = (bf16[4,4096]{1,0:T(4,128)(2,1)S(1)}, bf16[4,4096]{1,0:T(4,128)(2,1)S(1)}, u32[]{:S(2)}, u32[]{:S(2)}) collective-permute-start(bf16[4,4096]{1,0:T(4,128)(2,1)S(1)} %get-tuple-element.79), channel_id=1, source_target_pairs={{0,16},{1,17},{2,18},{3,19},{4,20},{5,21},{6,22},{7,23},{8,24},{9,... | collective-permute-start | bytes 98312 | tf_op jit(solution)/shard_map/ppermute | solution.py:35
  42.2 5.7 %collective-permute-start.23 = (bf16[4,4096]{1,0:T(4,128)(2,1)S(1)}, bf16[4,4096]{1,0:T(4,128)(2,1)S(1)}, u32[]{:S(2)}, u32[]{:S(2)}) collective-permute-start(bf16[4,4096]{1,0:T(4,128)(2,1)S(1)} %get-tuple-element.78), channel_id=1, source_target_pairs={{0,8},{1,9},{2,10},{3,11},{4,12},{5,13},{6,14},{7,15},{8,0},{9,1},... | collective-permute-start | bytes 98312 | tf_op jit(solution)/shard_map/ppermute | solution.py:35
  43.3 6.1 %collective-permute-start.14 = (bf16[4,4096]{1,0:T(4,128)(2,1)S(1)}, bf16[4,4096]{1,0:T(4,128)(2,1)S(1)}, u32[]{:S(2)}, u32[]{:S(2)}) collective-permute-start(bf16[4,4096]{1,0:T(4,128)(2,1)S(1)} %get-tuple-element.83), channel_id=1, source_target_pairs={{0,24},{1,25},{2,26},{3,27},{4,28},{5,29},{6,30},{7,31},{8,16},{9,... | collective-permute-start | bytes 98312 | tf_op jit(solution)/shard_map/ppermute | solution.py:35
  47.0 4.8 %collective-permute-start.15 = (bf16[4,4096]{1,0:T(4,128)(2,1)S(1)}, bf16[4,4096]{1,0:T(4,128)(2,1)S(1)}, u32[]{:S(2)}, u32[]{:S(2)}) collective-permute-start(bf16[4,4096]{1,0:T(4,128)(2,1)S(1)} %get-tuple-element.82), channel_id=1, source_target_pairs={{0,16},{1,17},{2,18},{3,19},{4,20},{5,21},{6,22},{7,23},{8,24},{9,... | collective-permute-start | bytes 98312 | tf_op jit(solution)/shard_map/ppermute | solution.py:35
  47.0 4.8 %collective-permute-start.16 = (bf16[4,4096]{1,0:T(4,128)(2,1)S(1)}, bf16[4,4096]{1,0:T(4,128)(2,1)S(1)}, u32[]{:S(2)}, u32[]{:S(2)}) collective-permute-start(bf16[4,4096]{1,0:T(4,128)(2,1)S(1)} %get-tuple-element.81), channel_id=1, source_target_pairs={{0,8},{1,9},{2,10},{3,11},{4,12},{5,13},{6,14},{7,15},{8,0},{9,1},... | collective-permute-start | bytes 98312 | tf_op jit(solution)/shard_map/ppermute | solution.py:35
  52.1 5.8 %collective-permute-start.24 = (bf16[4,4224]{1,0:T(4,128)(2,1)S(1)}, bf16[4,4224]{1,0:T(4,128)(2,1)S(1)}, u32[]{:S(2)}, u32[]{:S(2)}) collective-permute-start(bf16[4,4224]{1,0:T(4,128)(2,1)S(1)} %shard_map.160), channel_id=1, source_target_pairs={{0,24},{1,25},{2,26},{3,27},{4,28},{5,29},{6,30},{7,31},{8,16},{9,... | collective-permute-start | bytes 101384 | tf_op jit(solution)/shard_map/ppermute | solution.py:35
  53.6 4.9 %collective-permute-start.25 = (bf16[4,4224]{1,0:T(4,128)(2,1)S(1)}, bf16[4,4224]{1,0:T(4,128)(2,1)S(1)}, u32[]{:S(2)}, u32[]{:S(2)}) collective-permute-start(bf16[4,4224]{1,0:T(4,128)(2,1)S(1)} %shard_map.160), channel_id=1, source_target_pairs={{0,16},{1,17},{2,18},{3,19},{4,20},{5,21},{6,22},{7,23},{8,24},{9,... | collective-permute-start | bytes 101384 | tf_op jit(solution)/shard_map/ppermute | solution.py:35
  54.3 4.5 %collective-permute-start.26 = (bf16[4,4224]{1,0:T(4,128)(2,1)S(1)}, bf16[4,4224]{1,0:T(4,128)(2,1)S(1)}, u32[]{:S(2)}, u32[]{:S(2)}) collective-permute-start(bf16[4,4224]{1,0:T(4,128)(2,1)S(1)} %shard_map.160), channel_id=1, source_target_pairs={{0,8},{1,9},{2,10},{3,11},{4,12},{5,13},{6,14},{7,15},{8,0},{9,1},... | collective-permute-start | bytes 101384 | tf_op jit(solution)/shard_map/ppermute | solution.py:35
  59.0 6.0 %collective-permute-start.27 = (bf16[16,4224]{1,0:T(8,128)(2,1)S(1)}, bf16[16,4224]{1,0:T(8,128)(2,1)S(1)}, u32[]{:S(2)}, u32[]{:S(2)}) collective-permute-start(bf16[16,4224]{1,0:T(8,128)(2,1)S(1)} %pad_maximum_fusion.refs_0_), channel_id=1, source_target_pairs={{0,6},{1,7},{2,4},{3,5},{4,2},{5,3},{6,0},{7,1},{8,14},{9,15},{10,... | collective-permute-start | bytes 405512 | tf_op jit(solution)/shard_map/ppermute | solution.py:35
  61.1 5.3 %collective-permute-start.28 = (bf16[16,4224]{1,0:T(8,128)(2,1)S(1)}, bf16[16,4224]{1,0:T(8,128)(2,1)S(1)}, u32[]{:S(2)}, u32[]{:S(2)}) collective-permute-start(bf16[16,4224]{1,0:T(8,128)(2,1)S(1)} %pad_maximum_fusion.refs_0_), channel_id=1, source_target_pairs={{0,4},{1,5},{2,6},{3,7},{4,0},{5,1},{6,2},{7,3},{8,12},{9,13},{10,... | collective-permute-start | bytes 405512 | tf_op jit(solution)/shard_map/ppermute | solution.py:35
  62.0 5.0 %collective-permute-start.29 = (bf16[16,4224]{1,0:T(8,128)(2,1)S(1)}, bf16[16,4224]{1,0:T(8,128)(2,1)S(1)}, u32[]{:S(2)}, u32[]{:S(2)}) collective-permute-start(bf16[16,4224]{1,0:T(8,128)(2,1)S(1)} %pad_maximum_fusion.refs_0_), channel_id=1, source_target_pairs={{0,2},{1,3},{2,0},{3,1},{4,6},{5,7},{6,4},{7,5},{8,10},{9,11},{10,... | collective-permute-start | bytes 405512 | tf_op jit(solution)/shard_map/ppermute | solution.py:35
  64.6 2.4 %collective-permute-start.30 = (bf16[16,4224]{1,0:T(8,128)(2,1)S(1)}, bf16[16,4224]{1,0:T(8,128)(2,1)S(1)}, u32[]{:S(2)}, u32[]{:S(2)}) collective-permute-start(bf16[16,4224]{1,0:T(8,128)(2,1)S(1)} %pad_maximum_fusion.refs_0_), channel_id=1, source_target_pairs={{0,1},{1,0},{2,3},{3,2},{4,5},{5,4},{6,7},{7,6},{8,9},{9,8},{10,11... | collective-permute-start | bytes 405512 | tf_op jit(solution)/shard_map/ppermute | solution.py:35
  65.0 2.0 %collective-permute-start.31 = (bf16[16,4224]{1,0:T(8,128)(2,1)S(1)}, bf16[16,4224]{1,0:T(8,128)(2,1)S(1)}, u32[]{:S(2)}, u32[]{:S(2)}) collective-permute-start(bf16[16,4224]{1,0:T(8,128)(2,1)S(1)} %collective-permute-done.27.refs_1_), channel_id=1, source_target_pairs={{0,1},{1,0},{2,3},{3,2},{4,5},{5,4},{6,7},{7,6},{8,9},{9,8},{10,11... | collective-permute-start | bytes 405512 | tf_op jit(solution)/shard_map/ppermute | solution.py:35
  66.4 1.4 %collective-permute-start.32 = (bf16[16,4224]{1,0:T(8,128)(2,1)S(1)}, bf16[16,4224]{1,0:T(8,128)(2,1)S(1)}, u32[]{:S(2)}, u32[]{:S(2)}) collective-permute-start(bf16[16,4224]{1,0:T(8,128)(2,1)S(1)} %collective-permute-done.28.refs_2_), channel_id=1, source_target_pairs={{0,1},{1,0},{2,3},{3,2},{4,5},{5,4},{6,7},{7,6},{8,9},{9,8},{10,11... | collective-permute-start | bytes 405512 | tf_op jit(solution)/shard_map/ppermute | solution.py:35
  (9 other events, 71.3 us)

commit v6 on v5

--- a/solution.py
+++ b/solution.py
@@ -26,7 +26,9 @@
     levels, rest = [bits[:1]], bits[1:]
     while rest:
         low, rest = rest[:2], rest[2:]
-        levels.append([low[0] | low[1], low[1], low[0]] if len(low) == 2 else low)
+        both = low[0] | low[-1]
+        group = [both, low[-1], low[0]] if len(levels) == 1 else [low[-1], both, low[0]]
+        levels.append(group if len(low) == 2 else low)
     return [level for level in levels if level]
 
 
@@ -322,11 +324,9 @@
 
         return body
 
-    early = steps - steps // 4
     down_step = product(2, down_left, slopes, down_buf)
-    lax.fori_loop(0, early, down_step, 0)
+    lax.fori_loop(0, steps, down_step, 0)
     grad_hidden = dot(down[...], slopes[...], NT) * weight
-    lax.fori_loop(early, steps, down_step, 0)
     gate = gate_ref[...]
     sigmoid = 1.0 / (1.0 + jnp.exp(-gate))
     gate_left[...] = (

time: 78 us -> 77.8 us (level)
  starting transfers between devices: 37 us -> 35.4 us
  waiting for transfers between devices: 12.5 us -> 14 us
    ppermute x34, starting transfers between devices: 37 us -> 35.4 us  [swap(): return lax.ppermute(values, 'fsdp', [(i, i ^ mask) for i in range(members)])]
    ppermute x34, waiting for transfers between devices: 12.5 us -> 14 us  [swap(): return lax.ppermute(values, 'fsdp', [(i, i ^ mask) for i in range(members)])]
  transfers between devices with their start and end apart: 34 -> 34, of which waited for: 16 -> 17; matrix products, arithmetic and copies ran while one was open for 1% -> 1% of each run, Pallas kernels for 18% -> 18%
where the time goes in v6:
time: 77.8 us; the launch traced here: 77.7 us
  starting transfers between devices  35.4 us (46%)
  Pallas kernels  26.5 us (34%)
  waiting for transfers between devices  14 us (18%)
  between operations  0.91 us (1%)
    ppermute x34, starting transfers between devices, swap(): return lax.ppermute(values, 'fsdp', [(i, i ^ mask) for i in range(members)])  35.4 us
    ppermute x34, waiting for transfers between devices, swap(): return lax.ppermute(values, 'fsdp', [(i, i ^ mask) for i in range(members)])  14 us
    pallas_call x3, Pallas kernels, fetch(): pl.pallas_call(fetch_kernel, out_shape=[jax.ShapeDtypeStruct(w.shape, w.d...  10.8 us
    pallas_call x1, Pallas kernels, backward(): pl.pallas_call(functools.partial(backward_kernel, len(blocks), chunk, tok...  9.43 us
    pallas_call x2, Pallas kernels, forward_call(): pl.pallas_call(kernel, out_shape=shapes, in_specs=[vmem] * (len(operands)...  6.06 us
  transfers between devices with their start and end apart: 34, of which 17 were waited for; matrix products, arithmetic and copies ran while one was open for 1% of the time, Pallas kernels for 18%

profile of v6, /device:TPU:0, one launch (start us, length us, event | category | flops | bytes accessed | tf_op | source)
XLA Modules:
  0.0 77.7 jit_solution(16938278035963616110)
XLA Ops:
  0.6 4.1 %collective-permute-start = (bf16[4,4096]{1,0:T(4,128)(2,1)}, bf16[4,4096]{1,0:T(4,128)(2,1)S(1)}, u32[]{:S(2)}, u32[]{:S(2)}) collective-permute-start(bf16[4,4096]{1,0:T(4,128)(2,1)} %refs_8_.1), channel_id=1, source_target_pairs={{0,16},{1,17},{2,18},{3,19},{4,20},{5,21},{6,22},{7,23},{8,24},{9,... | collective-permute-start | bytes 98312 | tf_op jit(solution)/shard_map/ppermute | solution.py:37
  4.8 1.3 %collective-permute-start.1 = (bf16[4,4096]{1,0:T(4,128)(2,1)}, bf16[4,4096]{1,0:T(4,128)(2,1)S(1)}, u32[]{:S(2)}, u32[]{:S(2)}) collective-permute-start(bf16[4,4096]{1,0:T(4,128)(2,1)} %refs_8_.1), channel_id=1, source_target_pairs={{0,24},{1,25},{2,26},{3,27},{4,28},{5,29},{6,30},{7,31},{8,16},{9,... | collective-permute-start | bytes 98312 | tf_op jit(solution)/shard_map/ppermute | solution.py:37
  6.3 4.3 %shard_map.156 = (bf16[462,4096]{1,0:T(8,128)(2,1)S(1)}, bf16[462,4096]{1,0:T(8,128)(2,1)S(1)}, bf16[462,4096]{1,0:T(8,128)(2,1)S(1)}) custom-call(bf16[462,4096]{1,0:T(8,128)(2,1)} %bitcast.9, bf16[462,4096]{1,0:T(8,128)(2,1)} %bitcast.10, bf16[462,4096]{1,0:T(8,128)(2,1)} %refs_2_.2), custom_call_target="tpu_custom_call" | custom-call | bytes 11354112 | tf_op jit(solution)/shard_map/pallas_call | solution.py:156
  10.8 2.5 %collective-permute-start.3 = (bf16[16,4096]{1,0:T(8,128)(2,1)S(1)}, bf16[16,4096]{1,0:T(8,128)(2,1)S(1)}, u32[]{:S(2)}, u32[]{:S(2)}) collective-permute-start(bf16[16,4096]{1,0:T(8,128)(2,1)S(1)} %pad_maximum_fusion.1.refs_0_), channel_id=1, source_target_pairs={{0,6},{1,7},{2,4},{3,5},{4,2},{5,3},{6,0},{7,1},{8,14},{9,15},{10,... | collective-permute-start | bytes 393224 | tf_op jit(solution)/shard_map/ppermute | solution.py:37
  14.4 4.3 %shard_map.157 = (bf16[462,4096]{1,0:T(8,128)(2,1)S(1)}, bf16[462,4096]{1,0:T(8,128)(2,1)S(1)}, bf16[462,4096]{1,0:T(8,128)(2,1)S(1)}) custom-call(bf16[462,4096]{1,0:T(8,128)(2,1)} %bitcast.11, bf16[462,4096]{1,0:T(8,128)(2,1)} %bitcast.12, bf16[462,4096]{1,0:T(8,128)(2,1)} %refs_0_.1), custom_call_target="tpu_custom_call" | custom-call | bytes 11354112 | tf_op jit(solution)/shard_map/pallas_call | solution.py:156
  20.9 3.2 %shard_map.158 = (bf16[128,4096]{1,0:T(8,128)(2,1)S(1)}, bf16[64,4096]{1,0:T(8,128)(2,1)S(1)}, f32[64,4096]{1,0:T(8,128)S(1)}) custom-call(bf16[16,4096]{1,0:T(8,128)(2,1)S(1)} %pad_maximum_fusion.1.refs_0_, bf16[16,4096]{1,0:T(8,128)(2,1)S(1)} %collective-permute-done.3.refs_1_, bf16[16,4096]{1,0:T(8,128)(2,1)S(1)} %collective-permute-done.4.refs_2_, ...), custom_call_target="tpu_custom_call" | custom-call | flops 1453326336 | bytes 11354112 | tf_op jit(solution)/shard_map/pallas_call | solution.py:213
  24.4 2.9 %shard_map.159 = (f32[462,128]{1,0:T(8,128)S(1)}, f32[462,128]{1,0:T(8,128)S(1)}, bf16[462,128]{1,0:T(8,128)(2,1)S(1)}, bf16[64,4096]{1,0:T(8,128)(2,1)S(1)}, f32[64,4096]{1,0:T(8,128)S(1)}) custom-call(bf16[128,4096]{1,0:T(8,128)(2,1)S(1)} %get-tuple-element.47.normed.refs_8_, bf16[462,4096]{1,0:T(8,128)(2,1)S(1)} %get-tuple-element.48.refs_0_, ...), custom_call_target="tpu_custom_call" | custom-call | flops 1453326336 | bytes 11354112 | tf_op jit(solution)/shard_map/pallas_call | solution.py:213
  27.8 2.5 %collective-permute-start.18 = (bf16[16,4096]{1,0:T(8,128)(2,1)S(1)}, bf16[16,4096]{1,0:T(8,128)(2,1)S(1)}, u32[]{:S(2)}, u32[]{:S(2)}) collective-permute-start(bf16[16,4096]{1,0:T(8,128)(2,1)S(1)} %get-tuple-element.72), channel_id=1, source_target_pairs={{0,6},{1,7},{2,4},{3,5},{4,2},{5,3},{6,0},{7,1},{8,14},{9,15},{10,... | collective-permute-start | bytes 393224 | tf_op jit(solution)/shard_map/ppermute | solution.py:37
  30.8 0.5 collective-permute-start.20
  31.5 2.5 %collective-permute-start.11 = (bf16[16,4096]{1,0:T(8,128)(2,1)S(1)}, bf16[16,4096]{1,0:T(8,128)(2,1)S(1)}, u32[]{:S(2)}, u32[]{:S(2)}) collective-permute-start(bf16[16,4096]{1,0:T(8,128)(2,1)S(1)} %get-tuple-element.75), channel_id=1, source_target_pairs={{0,6},{1,7},{2,4},{3,5},{4,2},{5,3},{6,0},{7,1},{8,14},{9,15},{10,... | collective-permute-start | bytes 393224 | tf_op jit(solution)/shard_map/ppermute | solution.py:37
  34.8 1.8 %collective-permute-start.13 = (bf16[16,4096]{1,0:T(8,128)(2,1)S(1)}, bf16[16,4096]{1,0:T(8,128)(2,1)S(1)}, u32[]{:S(2)}, u32[]{:S(2)}) collective-permute-start(bf16[16,4096]{1,0:T(8,128)(2,1)S(1)} %get-tuple-element.76), channel_id=1, source_target_pairs={{0,2},{1,3},{2,0},{3,1},{4,6},{5,7},{6,4},{7,5},{8,10},{9,11},{10,... | collective-permute-start | bytes 393224 | tf_op jit(solution)/shard_map/ppermute | solution.py:37
  36.6 1.6 %collective-permute-done.19 = bf16[16,4096]{1,0:T(8,128)(2,1)S(1)} collective-permute-done((bf16[16,4096]{1,0:T(8,128)(2,1)S(1)}, bf16[16,4096]{1,0:T(8,128)(2,1)S(1)}, u32[]{:S(2)}, u32[]{:S(2)}) %collective-permute-start.19) | collective-permute-done | bytes 131104 | tf_op jit(solution)/shard_map/ppermute | solution.py:37
  38.3 2.9 %collective-permute-start.21 = (bf16[4,4096]{1,0:T(4,128)(2,1)S(1)}, bf16[4,4096]{1,0:T(4,128)(2,1)S(1)}, u32[]{:S(2)}, u32[]{:S(2)}) collective-permute-start(bf16[4,4096]{1,0:T(4,128)(2,1)S(1)} %get-tuple-element.80), channel_id=1, source_target_pairs={{0,16},{1,17},{2,18},{3,19},{4,20},{5,21},{6,22},{7,23},{8,24},{9,... | collective-permute-start | bytes 98312 | tf_op jit(solution)/shard_map/ppermute | solution.py:37
  41.2 1.3 %collective-permute-start.22 = (bf16[4,4096]{1,0:T(4,128)(2,1)S(1)}, bf16[4,4096]{1,0:T(4,128)(2,1)S(1)}, u32[]{:S(2)}, u32[]{:S(2)}) collective-permute-start(bf16[4,4096]{1,0:T(4,128)(2,1)S(1)} %get-tuple-element.79), channel_id=1, source_target_pairs={{0,24},{1,25},{2,26},{3,27},{4,28},{5,29},{6,30},{7,31},{8,16},{9,... | collective-permute-start | bytes 98312 | tf_op jit(solution)/shard_map/ppermute | solution.py:37
  43.1 2.9 %collective-permute-start.14 = (bf16[4,4096]{1,0:T(4,128)(2,1)S(1)}, bf16[4,4096]{1,0:T(4,128)(2,1)S(1)}, u32[]{:S(2)}, u32[]{:S(2)}) collective-permute-start(bf16[4,4096]{1,0:T(4,128)(2,1)S(1)} %get-tuple-element.83), channel_id=1, source_target_pairs={{0,16},{1,17},{2,18},{3,19},{4,20},{5,21},{6,22},{7,23},{8,24},{9,... | collective-permute-start | bytes 98312 | tf_op jit(solution)/shard_map/ppermute | solution.py:37
  46.0 1.3 %collective-permute-start.15 = (bf16[4,4096]{1,0:T(4,128)(2,1)S(1)}, bf16[4,4096]{1,0:T(4,128)(2,1)S(1)}, u32[]{:S(2)}, u32[]{:S(2)}) collective-permute-start(bf16[4,4096]{1,0:T(4,128)(2,1)S(1)} %get-tuple-element.82), channel_id=1, source_target_pairs={{0,24},{1,25},{2,26},{3,27},{4,28},{5,29},{6,30},{7,31},{8,16},{9,... | collective-permute-start | bytes 98312 | tf_op jit(solution)/shard_map/ppermute | solution.py:37
  47.5 0.9 %collective-permute-done.14.refs_1_ = bf16[4,4096]{1,0:T(4,128)(2,1)S(1)} collective-permute-done((bf16[4,4096]{1,0:T(4,128)(2,1)S(1)}, bf16[4,4096]{1,0:T(4,128)(2,1)S(1)}, u32[]{:S(2)}, u32[]{:S(2)}) %collective-permute-start.14) | collective-permute-done | bytes 32800 | tf_op jit(solution)/shard_map/ppermute | solution.py:37
  48.4 3.3 %collective-permute-done.15.refs_2_ = bf16[4,4096]{1,0:T(4,128)(2,1)S(1)} collective-permute-done((bf16[4,4096]{1,0:T(4,128)(2,1)S(1)}, bf16[4,4096]{1,0:T(4,128)(2,1)S(1)}, u32[]{:S(2)}, u32[]{:S(2)}) %collective-permute-start.15) | collective-permute-done | bytes 32800 | tf_op jit(solution)/shard_map/ppermute | solution.py:37
  52.0 1.0 %collective-permute-start.24 = (bf16[4,4224]{1,0:T(4,128)(2,1)S(1)}, bf16[4,4224]{1,0:T(4,128)(2,1)S(1)}, u32[]{:S(2)}, u32[]{:S(2)}) collective-permute-start(bf16[4,4224]{1,0:T(4,128)(2,1)S(1)} %shard_map.160), channel_id=1, source_target_pairs={{0,16},{1,17},{2,18},{3,19},{4,20},{5,21},{6,22},{7,23},{8,24},{9,... | collective-permute-start | bytes 101384 | tf_op jit(solution)/shard_map/ppermute | solution.py:37
  53.0 1.3 %collective-permute-start.25 = (bf16[4,4224]{1,0:T(4,128)(2,1)S(1)}, bf16[4,4224]{1,0:T(4,128)(2,1)S(1)}, u32[]{:S(2)}, u32[]{:S(2)}) collective-permute-start(bf16[4,4224]{1,0:T(4,128)(2,1)S(1)} %shard_map.160), channel_id=1, source_target_pairs={{0,24},{1,25},{2,26},{3,27},{4,28},{5,29},{6,30},{7,31},{8,16},{9,... | collective-permute-start | bytes 101384 | tf_op jit(solution)/shard_map/ppermute | solution.py:37
  54.3 1.2 %collective-permute-start.26 = (bf16[4,4224]{1,0:T(4,128)(2,1)S(1)}, bf16[4,4224]{1,0:T(4,128)(2,1)S(1)}, u32[]{:S(2)}, u32[]{:S(2)}) collective-permute-start(bf16[4,4224]{1,0:T(4,128)(2,1)S(1)} %shard_map.160), channel_id=1, source_target_pairs={{0,8},{1,9},{2,10},{3,11},{4,12},{5,13},{6,14},{7,15},{8,0},{9,1},... | collective-permute-start | bytes 101384 | tf_op jit(solution)/shard_map/ppermute | solution.py:37
  55.6 1.4 %collective-permute-done.24 = bf16[4,4224]{1,0:T(4,128)(2,1)S(1)} collective-permute-done((bf16[4,4224]{1,0:T(4,128)(2,1)S(1)}, bf16[4,4224]{1,0:T(4,128)(2,1)S(1)}, u32[]{:S(2)}, u32[]{:S(2)}) %collective-permute-start.24) | collective-permute-done | bytes 33824 | tf_op jit(solution)/shard_map/ppermute | solution.py:37
  56.9 1.8 %collective-permute-done.25 = bf16[4,4224]{1,0:T(4,128)(2,1)S(1)} collective-permute-done((bf16[4,4224]{1,0:T(4,128)(2,1)S(1)}, bf16[4,4224]{1,0:T(4,128)(2,1)S(1)}, u32[]{:S(2)}, u32[]{:S(2)}) %collective-permute-start.25) | collective-permute-done | bytes 33824 | tf_op jit(solution)/shard_map/ppermute | solution.py:37
  58.8 2.1 %collective-permute-start.27 = (bf16[16,4224]{1,0:T(8,128)(2,1)S(1)}, bf16[16,4224]{1,0:T(8,128)(2,1)S(1)}, u32[]{:S(2)}, u32[]{:S(2)}) collective-permute-start(bf16[16,4224]{1,0:T(8,128)(2,1)S(1)} %pad_maximum_fusion.refs_0_), channel_id=1, source_target_pairs={{0,6},{1,7},{2,4},{3,5},{4,2},{5,3},{6,0},{7,1},{8,14},{9,15},{10,... | collective-permute-start | bytes 405512 | tf_op jit(solution)/shard_map/ppermute | solution.py:37
  60.9 0.9 %collective-permute-start.28 = (bf16[16,4224]{1,0:T(8,128)(2,1)S(1)}, bf16[16,4224]{1,0:T(8,128)(2,1)S(1)}, u32[]{:S(2)}, u32[]{:S(2)}) collective-permute-start(bf16[16,4224]{1,0:T(8,128)(2,1)S(1)} %pad_maximum_fusion.refs_0_), channel_id=1, source_target_pairs={{0,4},{1,5},{2,6},{3,7},{4,0},{5,1},{6,2},{7,3},{8,12},{9,13},{10,... | collective-permute-start | bytes 405512 | tf_op jit(solution)/shard_map/ppermute | solution.py:37
  61.8 0.5 collective-permute-start.29
  62.4 2.1 %shard_map.161.refs_16_ = bf16[462,4096]{1,0:T(8,128)(2,1)S(1)} custom-call(bf16[462,4096]{1,0:T(8,128)(2,1)} %refs_0_.1), custom_call_target="tpu_custom_call" | custom-call | bytes 3784704 | tf_op jit(solution)/shard_map/pallas_call | solution.py:156
  65.1 1.2 %collective-permute-done.28.refs_2_ = bf16[16,4224]{1,0:T(8,128)(2,1)S(1)} collective-permute-done((bf16[16,4224]{1,0:T(8,128)(2,1)S(1)}, bf16[16,4224]{1,0:T(8,128)(2,1)S(1)}, u32[]{:S(2)}, u32[]{:S(2)}) %collective-permute-start.28) | collective-permute-done | bytes 135200 | tf_op jit(solution)/shard_map/ppermute | solution.py:37
  66.3 0.6 collective-permute-done.29.refs_3_
  66.9 0.7 collective-permute-done.32.refs_6_
  67.6 0.6 collective-permute-done.33.refs_7_
  68.2 9.4 %shard_map.162 = (f32[462,4096]{1,0:T(8,128)}, f32[462,4096]{1,0:T(8,128)}, f32[462,4096]{1,0:T(8,128)}, f32[1,32]{1,0:T(1,128)}) custom-call(bf16[16,4224]{1,0:T(8,128)(2,1)S(1)} %pad_maximum_fusion.refs_0_, bf16[16,4224]{1,0:T(8,128)(2,1)S(1)} %collective-permute-done.27.refs_1_, bf16[16,4224]{1,0:T(8,128)(2,1)S(1)} %collective-permute-done.28.refs_2_, ...), custom_call_target="tpu_custom_call" | custom-call | flops 1937768448 | bytes 26492928 | tf_op jit(solution)/shard_map/pallas_call | solution.py:358
  (70 shorter events, 7.5 us)
Async XLA Ops:
  0.6 10.1 %collective-permute-start = (bf16[4,4096]{1,0:T(4,128)(2,1)}, bf16[4,4096]{1,0:T(4,128)(2,1)S(1)}, u32[]{:S(2)}, u32[]{:S(2)}) collective-permute-start(bf16[4,4096]{1,0:T(4,128)(2,1)} %refs_8_.1), channel_id=1, source_target_pairs={{0,16},{1,17},{2,18},{3,19},{4,20},{5,21},{6,22},{7,23},{8,24},{9,... | collective-permute-start | bytes 98312 | tf_op jit(solution)/shard_map/ppermute | solution.py:37
  4.8 6.0 %collective-permute-start.1 = (bf16[4,4096]{1,0:T(4,128)(2,1)}, bf16[4,4096]{1,0:T(4,128)(2,1)S(1)}, u32[]{:S(2)}, u32[]{:S(2)}) collective-permute-start(bf16[4,4096]{1,0:T(4,128)(2,1)} %refs_8_.1), channel_id=1, source_target_pairs={{0,24},{1,25},{2,26},{3,27},{4,28},{5,29},{6,30},{7,31},{8,16},{9,... | collective-permute-start | bytes 98312 | tf_op jit(solution)/shard_map/ppermute | solution.py:37
  6.1 4.6 %collective-permute-start.2 = (bf16[4,4096]{1,0:T(4,128)(2,1)}, bf16[4,4096]{1,0:T(4,128)(2,1)S(1)}, u32[]{:S(2)}, u32[]{:S(2)}) collective-permute-start(bf16[4,4096]{1,0:T(4,128)(2,1)} %refs_8_.1), channel_id=1, source_target_pairs={{0,8},{1,9},{2,10},{3,11},{4,12},{5,13},{6,14},{7,15},{8,0},{9,1},... | collective-permute-start | bytes 98312 | tf_op jit(solution)/shard_map/ppermute | solution.py:37
  10.8 8.0 %collective-permute-start.3 = (bf16[16,4096]{1,0:T(8,128)(2,1)S(1)}, bf16[16,4096]{1,0:T(8,128)(2,1)S(1)}, u32[]{:S(2)}, u32[]{:S(2)}) collective-permute-start(bf16[16,4096]{1,0:T(8,128)(2,1)S(1)} %pad_maximum_fusion.1.refs_0_), channel_id=1, source_target_pairs={{0,6},{1,7},{2,4},{3,5},{4,2},{5,3},{6,0},{7,1},{8,14},{9,15},{10,... | collective-permute-start | bytes 393224 | tf_op jit(solution)/shard_map/ppermute | solution.py:37
  13.3 6.0 %collective-permute-start.4 = (bf16[16,4096]{1,0:T(8,128)(2,1)S(1)}, bf16[16,4096]{1,0:T(8,128)(2,1)S(1)}, u32[]{:S(2)}, u32[]{:S(2)}) collective-permute-start(bf16[16,4096]{1,0:T(8,128)(2,1)S(1)} %pad_maximum_fusion.1.refs_0_), channel_id=1, source_target_pairs={{0,4},{1,5},{2,6},{3,7},{4,0},{5,1},{6,2},{7,3},{8,12},{9,13},{10,... | collective-permute-start | bytes 393224 | tf_op jit(solution)/shard_map/ppermute | solution.py:37
  13.8 5.6 %collective-permute-start.5 = (bf16[16,4096]{1,0:T(8,128)(2,1)S(1)}, bf16[16,4096]{1,0:T(8,128)(2,1)S(1)}, u32[]{:S(2)}, u32[]{:S(2)}) collective-permute-start(bf16[16,4096]{1,0:T(8,128)(2,1)S(1)} %pad_maximum_fusion.1.refs_0_), channel_id=1, source_target_pairs={{0,2},{1,3},{2,0},{3,1},{4,6},{5,7},{6,4},{7,5},{8,10},{9,11},{10,... | collective-permute-start | bytes 393224 | tf_op jit(solution)/shard_map/ppermute | solution.py:37
  18.7 1.4 %collective-permute-start.6 = (bf16[16,4096]{1,0:T(8,128)(2,1)S(1)}, bf16[16,4096]{1,0:T(8,128)(2,1)S(1)}, u32[]{:S(2)}, u32[]{:S(2)}) collective-permute-start(bf16[16,4096]{1,0:T(8,128)(2,1)S(1)} %pad_maximum_fusion.1.refs_0_), channel_id=1, source_target_pairs={{0,1},{1,0},{2,3},{3,2},{4,5},{5,4},{6,7},{7,6},{8,9},{9,8},{10,11... | collective-permute-start | bytes 393224 | tf_op jit(solution)/shard_map/ppermute | solution.py:37
  18.8 1.5 %collective-permute-start.7 = (bf16[16,4096]{1,0:T(8,128)(2,1)S(1)}, bf16[16,4096]{1,0:T(8,128)(2,1)S(1)}, u32[]{:S(2)}, u32[]{:S(2)}) collective-permute-start(bf16[16,4096]{1,0:T(8,128)(2,1)S(1)} %collective-permute-done.3.refs_1_), channel_id=1, source_target_pairs={{0,1},{1,0},{2,3},{3,2},{4,5},{5,4},{6,7},{7,6},{8,9},{9,8},{10,11... | collective-permute-start | bytes 393224 | tf_op jit(solution)/shard_map/ppermute | solution.py:37
  19.4 1.4 %collective-permute-start.9 = (bf16[16,4096]{1,0:T(8,128)(2,1)S(1)}, bf16[16,4096]{1,0:T(8,128)(2,1)S(1)}, u32[]{:S(2)}, u32[]{:S(2)}) collective-permute-start(bf16[16,4096]{1,0:T(8,128)(2,1)S(1)} %collective-permute-done.5.refs_3_), channel_id=1, source_target_pairs={{0,1},{1,0},{2,3},{3,2},{4,5},{5,4},{6,7},{7,6},{8,9},{9,8},{10,11... | collective-permute-start | bytes 393224 | tf_op jit(solution)/shard_map/ppermute | solution.py:37
  24.1 3.5 %collective-permute-start.17 = (bf16[64,4096]{1,0:T(8,128)(2,1)S(1)}, bf16[64,4096]{1,0:T(8,128)(2,1)S(1)}, u32[]{:S(2)}, u32[]{:S(2)}) collective-permute-start(bf16[64,4096]{1,0:T(8,128)(2,1)S(1)} %get-tuple-element.54), channel_id=1, source_target_pairs={{0,1},{1,0},{2,3},{3,2},{4,5},{5,4},{6,7},{7,6},{8,9},{9,8},{10,11... | collective-permute-start | bytes 1572872 | tf_op jit(solution)/shard_map/ppermute | solution.py:37
  27.3 4.0 %collective-permute-start.10 = (bf16[64,4096]{1,0:T(8,128)(2,1)S(1)}, bf16[64,4096]{1,0:T(8,128)(2,1)S(1)}, u32[]{:S(2)}, u32[]{:S(2)}) collective-permute-start(bf16[64,4096]{1,0:T(8,128)(2,1)S(1)} %get-tuple-element.52), channel_id=1, source_target_pairs={{0,1},{1,0},{2,3},{3,2},{4,5},{5,4},{6,7},{7,6},{8,9},{9,8},{10,11... | collective-permute-start | bytes 1572872 | tf_op jit(solution)/shard_map/ppermute | solution.py:37
  27.8 7.0 %collective-permute-start.18 = (bf16[16,4096]{1,0:T(8,128)(2,1)S(1)}, bf16[16,4096]{1,0:T(8,128)(2,1)S(1)}, u32[]{:S(2)}, u32[]{:S(2)}) collective-permute-start(bf16[16,4096]{1,0:T(8,128)(2,1)S(1)} %get-tuple-element.72), channel_id=1, source_target_pairs={{0,6},{1,7},{2,4},{3,5},{4,2},{5,3},{6,0},{7,1},{8,14},{9,15},{10,... | collective-permute-start | bytes 393224 | tf_op jit(solution)/shard_map/ppermute | solution.py:37
  30.3 7.9 %collective-permute-start.19 = (bf16[16,4096]{1,0:T(8,128)(2,1)S(1)}, bf16[16,4096]{1,0:T(8,128)(2,1)S(1)}, u32[]{:S(2)}, u32[]{:S(2)}) collective-permute-start(bf16[16,4096]{1,0:T(8,128)(2,1)S(1)} %get-tuple-element.74), channel_id=1, source_target_pairs={{0,4},{1,5},{2,6},{3,7},{4,0},{5,1},{6,2},{7,3},{8,12},{9,13},{10,... | collective-permute-start | bytes 393224 | tf_op jit(solution)/shard_map/ppermute | solution.py:37
  30.8 7.4 %collective-permute-start.20 = (bf16[16,4096]{1,0:T(8,128)(2,1)S(1)}, bf16[16,4096]{1,0:T(8,128)(2,1)S(1)}, u32[]{:S(2)}, u32[]{:S(2)}) collective-permute-start(bf16[16,4096]{1,0:T(8,128)(2,1)S(1)} %get-tuple-element.73), channel_id=1, source_target_pairs={{0,2},{1,3},{2,0},{3,1},{4,6},{5,7},{6,4},{7,5},{8,10},{9,11},{10,... | collective-permute-start | bytes 393224 | tf_op jit(solution)/shard_map/ppermute | solution.py:37
  31.5 11.1 %collective-permute-start.11 = (bf16[16,4096]{1,0:T(8,128)(2,1)S(1)}, bf16[16,4096]{1,0:T(8,128)(2,1)S(1)}, u32[]{:S(2)}, u32[]{:S(2)}) collective-permute-start(bf16[16,4096]{1,0:T(8,128)(2,1)S(1)} %get-tuple-element.75), channel_id=1, source_target_pairs={{0,6},{1,7},{2,4},{3,5},{4,2},{5,3},{6,0},{7,1},{8,14},{9,15},{10,... | collective-permute-start | bytes 393224 | tf_op jit(solution)/shard_map/ppermute | solution.py:37
  34.0 8.9 %collective-permute-start.12 = (bf16[16,4096]{1,0:T(8,128)(2,1)S(1)}, bf16[16,4096]{1,0:T(8,128)(2,1)S(1)}, u32[]{:S(2)}, u32[]{:S(2)}) collective-permute-start(bf16[16,4096]{1,0:T(8,128)(2,1)S(1)} %get-tuple-element.77), channel_id=1, source_target_pairs={{0,4},{1,5},{2,6},{3,7},{4,0},{5,1},{6,2},{7,3},{8,12},{9,13},{10,... | collective-permute-start | bytes 393224 | tf_op jit(solution)/shard_map/ppermute | solution.py:37
  34.8 8.2 %collective-permute-start.13 = (bf16[16,4096]{1,0:T(8,128)(2,1)S(1)}, bf16[16,4096]{1,0:T(8,128)(2,1)S(1)}, u32[]{:S(2)}, u32[]{:S(2)}) collective-permute-start(bf16[16,4096]{1,0:T(8,128)(2,1)S(1)} %get-tuple-element.76), channel_id=1, source_target_pairs={{0,2},{1,3},{2,0},{3,1},{4,6},{5,7},{6,4},{7,5},{8,10},{9,11},{10,... | collective-permute-start | bytes 393224 | tf_op jit(solution)/shard_map/ppermute | solution.py:37
  38.3 9.0 %collective-permute-start.21 = (bf16[4,4096]{1,0:T(4,128)(2,1)S(1)}, bf16[4,4096]{1,0:T(4,128)(2,1)S(1)}, u32[]{:S(2)}, u32[]{:S(2)}) collective-permute-start(bf16[4,4096]{1,0:T(4,128)(2,1)S(1)} %get-tuple-element.80), channel_id=1, source_target_pairs={{0,16},{1,17},{2,18},{3,19},{4,20},{5,21},{6,22},{7,23},{8,24},{9,... | collective-permute-start | bytes 98312 | tf_op jit(solution)/shard_map/ppermute | solution.py:37
  41.2 6.3 %collective-permute-start.22 = (bf16[4,4096]{1,0:T(4,128)(2,1)S(1)}, bf16[4,4096]{1,0:T(4,128)(2,1)S(1)}, u32[]{:S(2)}, u32[]{:S(2)}) collective-permute-start(bf16[4,4096]{1,0:T(4,128)(2,1)S(1)} %get-tuple-element.79), channel_id=1, source_target_pairs={{0,24},{1,25},{2,26},{3,27},{4,28},{5,29},{6,30},{7,31},{8,16},{9,... | collective-permute-start | bytes 98312 | tf_op jit(solution)/shard_map/ppermute | solution.py:37
  42.5 5.0 %collective-permute-start.23 = (bf16[4,4096]{1,0:T(4,128)(2,1)S(1)}, bf16[4,4096]{1,0:T(4,128)(2,1)S(1)}, u32[]{:S(2)}, u32[]{:S(2)}) collective-permute-start(bf16[4,4096]{1,0:T(4,128)(2,1)S(1)} %get-tuple-element.78), channel_id=1, source_target_pairs={{0,8},{1,9},{2,10},{3,11},{4,12},{5,13},{6,14},{7,15},{8,0},{9,1},... | collective-permute-start | bytes 98312 | tf_op jit(solution)/shard_map/ppermute | solution.py:37
  43.1 5.3 %collective-permute-start.14 = (bf16[4,4096]{1,0:T(4,128)(2,1)S(1)}, bf16[4,4096]{1,0:T(4,128)(2,1)S(1)}, u32[]{:S(2)}, u32[]{:S(2)}) collective-permute-start(bf16[4,4096]{1,0:T(4,128)(2,1)S(1)} %get-tuple-element.83), channel_id=1, source_target_pairs={{0,16},{1,17},{2,18},{3,19},{4,20},{5,21},{6,22},{7,23},{8,24},{9,... | collective-permute-start | bytes 98312 | tf_op jit(solution)/shard_map/ppermute | solution.py:37
  46.0 5.7 %collective-permute-start.15 = (bf16[4,4096]{1,0:T(4,128)(2,1)S(1)}, bf16[4,4096]{1,0:T(4,128)(2,1)S(1)}, u32[]{:S(2)}, u32[]{:S(2)}) collective-permute-start(bf16[4,4096]{1,0:T(4,128)(2,1)S(1)} %get-tuple-element.82), channel_id=1, source_target_pairs={{0,24},{1,25},{2,26},{3,27},{4,28},{5,29},{6,30},{7,31},{8,16},{9,... | collective-permute-start | bytes 98312 | tf_op jit(solution)/shard_map/ppermute | solution.py:37
  47.4 4.4 %collective-permute-start.16 = (bf16[4,4096]{1,0:T(4,128)(2,1)S(1)}, bf16[4,4096]{1,0:T(4,128)(2,1)S(1)}, u32[]{:S(2)}, u32[]{:S(2)}) collective-permute-start(bf16[4,4096]{1,0:T(4,128)(2,1)S(1)} %get-tuple-element.81), channel_id=1, source_target_pairs={{0,8},{1,9},{2,10},{3,11},{4,12},{5,13},{6,14},{7,15},{8,0},{9,1},... | collective-permute-start | bytes 98312 | tf_op jit(solution)/shard_map/ppermute | solution.py:37
  52.0 4.9 %collective-permute-start.24 = (bf16[4,4224]{1,0:T(4,128)(2,1)S(1)}, bf16[4,4224]{1,0:T(4,128)(2,1)S(1)}, u32[]{:S(2)}, u32[]{:S(2)}) collective-permute-start(bf16[4,4224]{1,0:T(4,128)(2,1)S(1)} %shard_map.160), channel_id=1, source_target_pairs={{0,16},{1,17},{2,18},{3,19},{4,20},{5,21},{6,22},{7,23},{8,24},{9,... | collective-permute-start | bytes 101384 | tf_op jit(solution)/shard_map/ppermute | solution.py:37
  53.0 5.7 %collective-permute-start.25 = (bf16[4,4224]{1,0:T(4,128)(2,1)S(1)}, bf16[4,4224]{1,0:T(4,128)(2,1)S(1)}, u32[]{:S(2)}, u32[]{:S(2)}) collective-permute-start(bf16[4,4224]{1,0:T(4,128)(2,1)S(1)} %shard_map.160), channel_id=1, source_target_pairs={{0,24},{1,25},{2,26},{3,27},{4,28},{5,29},{6,30},{7,31},{8,16},{9,... | collective-permute-start | bytes 101384 | tf_op jit(solution)/shard_map/ppermute | solution.py:37
  54.3 4.4 %collective-permute-start.26 = (bf16[4,4224]{1,0:T(4,128)(2,1)S(1)}, bf16[4,4224]{1,0:T(4,128)(2,1)S(1)}, u32[]{:S(2)}, u32[]{:S(2)}) collective-permute-start(bf16[4,4224]{1,0:T(4,128)(2,1)S(1)} %shard_map.160), channel_id=1, source_target_pairs={{0,8},{1,9},{2,10},{3,11},{4,12},{5,13},{6,14},{7,15},{8,0},{9,1},... | collective-permute-start | bytes 101384 | tf_op jit(solution)/shard_map/ppermute | solution.py:37
  58.8 6.0 %collective-permute-start.27 = (bf16[16,4224]{1,0:T(8,128)(2,1)S(1)}, bf16[16,4224]{1,0:T(8,128)(2,1)S(1)}, u32[]{:S(2)}, u32[]{:S(2)}) collective-permute-start(bf16[16,4224]{1,0:T(8,128)(2,1)S(1)} %pad_maximum_fusion.refs_0_), channel_id=1, source_target_pairs={{0,6},{1,7},{2,4},{3,5},{4,2},{5,3},{6,0},{7,1},{8,14},{9,15},{10,... | collective-permute-start | bytes 405512 | tf_op jit(solution)/shard_map/ppermute | solution.py:37
  60.9 5.3 %collective-permute-start.28 = (bf16[16,4224]{1,0:T(8,128)(2,1)S(1)}, bf16[16,4224]{1,0:T(8,128)(2,1)S(1)}, u32[]{:S(2)}, u32[]{:S(2)}) collective-permute-start(bf16[16,4224]{1,0:T(8,128)(2,1)S(1)} %pad_maximum_fusion.refs_0_), channel_id=1, source_target_pairs={{0,4},{1,5},{2,6},{3,7},{4,0},{5,1},{6,2},{7,3},{8,12},{9,13},{10,... | collective-permute-start | bytes 405512 | tf_op jit(solution)/shard_map/ppermute | solution.py:37
  61.8 5.0 %collective-permute-start.29 = (bf16[16,4224]{1,0:T(8,128)(2,1)S(1)}, bf16[16,4224]{1,0:T(8,128)(2,1)S(1)}, u32[]{:S(2)}, u32[]{:S(2)}) collective-permute-start(bf16[16,4224]{1,0:T(8,128)(2,1)S(1)} %pad_maximum_fusion.refs_0_), channel_id=1, source_target_pairs={{0,2},{1,3},{2,0},{3,1},{4,6},{5,7},{6,4},{7,5},{8,10},{9,11},{10,... | collective-permute-start | bytes 405512 | tf_op jit(solution)/shard_map/ppermute | solution.py:37
  64.5 2.4 %collective-permute-start.30 = (bf16[16,4224]{1,0:T(8,128)(2,1)S(1)}, bf16[16,4224]{1,0:T(8,128)(2,1)S(1)}, u32[]{:S(2)}, u32[]{:S(2)}) collective-permute-start(bf16[16,4224]{1,0:T(8,128)(2,1)S(1)} %pad_maximum_fusion.refs_0_), channel_id=1, source_target_pairs={{0,1},{1,0},{2,3},{3,2},{4,5},{5,4},{6,7},{7,6},{8,9},{9,8},{10,11... | collective-permute-start | bytes 405512 | tf_op jit(solution)/shard_map/ppermute | solution.py:37
  64.8 2.0 %collective-permute-start.31 = (bf16[16,4224]{1,0:T(8,128)(2,1)S(1)}, bf16[16,4224]{1,0:T(8,128)(2,1)S(1)}, u32[]{:S(2)}, u32[]{:S(2)}) collective-permute-start(bf16[16,4224]{1,0:T(8,128)(2,1)S(1)} %collective-permute-done.27.refs_1_), channel_id=1, source_target_pairs={{0,1},{1,0},{2,3},{3,2},{4,5},{5,4},{6,7},{7,6},{8,9},{9,8},{10,11... | collective-permute-start | bytes 405512 | tf_op jit(solution)/shard_map/ppermute | solution.py:37
  66.3 1.4 %collective-permute-start.32 = (bf16[16,4224]{1,0:T(8,128)(2,1)S(1)}, bf16[16,4224]{1,0:T(8,128)(2,1)S(1)}, u32[]{:S(2)}, u32[]{:S(2)}) collective-permute-start(bf16[16,4224]{1,0:T(8,128)(2,1)S(1)} %collective-permute-done.28.refs_2_), channel_id=1, source_target_pairs={{0,1},{1,0},{2,3},{3,2},{4,5},{5,4},{6,7},{7,6},{8,9},{9,8},{10,11... | collective-permute-start | bytes 405512 | tf_op jit(solution)/shard_map/ppermute | solution.py:37
  (9 other events, 70.9 us)
